TPU v7x, 32 devices: a whole 2x2x4 slice. The times are simulated.
32 devices in a mesh: dp: 16 (over z, x, core), tensor: 2 (over y).
Axes of the slice: x: 2, y: 2, z: 4, core: 2. Of those that a mesh axis runs over, the one named last changes fastest.
Arguments:
- tokens: bfloat16 [32, 512, 1024], P('dp', 'tensor')
- clip_count: int32 [16], P('dp'), may hold values from 1 to 2, as said below
- first_norm_gain: bfloat16 [1024], replicated, may hold values from 0.5 to 1.5
- first_norm_shift: bfloat16 [1024], replicated, may hold values from -1.5 to 1.5
- first_up_weight: bfloat16 [1024, 4096], P(None, 'tensor'), may hold values from -0.1875 to 0.1875
- first_up_bias: bfloat16 [4096], P('tensor'), may hold values from -1.5 to 1.5
- first_down_weight: bfloat16 [4096, 1024], P('tensor'), may hold values from -0.1875 to 0.1875
- first_down_bias: bfloat16 [1024], replicated, may hold values from -1.5 to 1.5
- attend_norm_gain: bfloat16 [1024], replicated, may hold values from 0.5 to 1.5
- attend_norm_shift: bfloat16 [1024], replicated, may hold values from -1.5 to 1.5
- query_weight: bfloat16 [1024, 1024], P(None, 'tensor'), may hold values from -0.1875 to 0.1875
- query_bias: bfloat16 [1024], P('tensor'), may hold values from -1.5 to 1.5
- key_weight: bfloat16 [1024, 1024], P(None, 'tensor'), may hold values from -0.1875 to 0.1875
- value_weight: bfloat16 [1024, 1024], P(None, 'tensor'), may hold values from -0.1875 to 0.1875
- value_bias: bfloat16 [1024], P('tensor'), may hold values from -1.5 to 1.5
- output_weight: bfloat16 [1024, 1024], P('tensor'), may hold values from -1.5 to 1.5
- output_bias: bfloat16 [1024], replicated, may hold values from -1.5 to 1.5
- relative_table: bfloat16 [73, 64], replicated, may hold values from -5 to 5
- convolve_norm_gain: bfloat16 [1024], replicated, may hold values from 0.5 to 1.5
- convolve_norm_shift: bfloat16 [1024], replicated, may hold values from -1.5 to 1.5
- pointwise_in: bfloat16 [2, 1024, 1024], P(None, None, 'tensor'), may hold values from -0.1875 to 0.1875
- depthwise_weight: bfloat16 [31, 1024], P(None, 'tensor')
- depth_norm_gain: bfloat16 [1024], P('tensor'), may hold values from 0.5 to 1.5
- depth_norm_shift: bfloat16 [1024], P('tensor'), may hold values from -1.5 to 1.5
- pointwise_out: bfloat16 [1024, 1024], P('tensor'), may hold values from -0.25 to 0.25
- second_norm_gain: bfloat16 [1024], replicated, may hold values from 0.5 to 1.5
- second_norm_shift: bfloat16 [1024], replicated, may hold values from -1.5 to 1.5
- second_up_weight: bfloat16 [1024, 4096], P(None, 'tensor'), may hold values from -0.1875 to 0.1875
- second_up_bias: bfloat16 [4096], P('tensor'), may hold values from -1.5 to 1.5
- second_down_weight: bfloat16 [4096, 1024], P('tensor'), may hold values from -0.1875 to 0.1875
- second_down_bias: bfloat16 [1024], replicated, may hold values from -1.5 to 1.5
- final_norm_gain: bfloat16 [1024], replicated, may hold values from 0.5 to 1.5
- final_norm_shift: bfloat16 [1024], replicated, may hold values from -1.5 to 1.5
- cotangent: bfloat16 [32, 512, 1024], P('dp', 'tensor'), may hold values from -6 to 6
Outputs:
- output: bfloat16 [32, 512, 1024], P('dp', 'tensor')
- input_grad: float32 [32, 512, 1024], P('dp', 'tensor')
- grad_first_norm_gain: float32 [1024], replicated
- grad_first_norm_shift: float32 [1024], replicated
- grad_first_up_weight: float32 [1024, 4096], P(None, 'tensor')
- grad_first_up_bias: float32 [4096], P('tensor')
- grad_first_down_weight: float32 [4096, 1024], P('tensor')
- grad_first_down_bias: float32 [1024], replicated
- grad_attend_norm_gain: float32 [1024], replicated
- grad_attend_norm_shift: float32 [1024], replicated
- grad_query_weight: float32 [1024, 1024], P(None, 'tensor')
- grad_query_bias: float32 [1024], P('tensor')
- grad_key_weight: float32 [1024, 1024], P(None, 'tensor')
- grad_value_weight: float32 [1024, 1024], P(None, 'tensor')
- grad_value_bias: float32 [1024], P('tensor')
- grad_output_weight: float32 [1024, 1024], P('tensor')
- grad_output_bias: float32 [1024], replicated
- grad_relative_table: float32 [73, 64], replicated
- grad_convolve_norm_gain: float32 [1024], replicated
- grad_convolve_norm_shift: float32 [1024], replicated
- grad_pointwise_in: float32 [2, 1024, 1024], P(None, None, 'tensor')
- grad_depthwise_weight: float32 [31, 1024], P(None, 'tensor')
- grad_depth_norm_gain: float32 [1024], P('tensor')
- grad_depth_norm_shift: float32 [1024], P('tensor')
- grad_pointwise_out: float32 [1024, 1024], P('tensor')
- grad_second_norm_gain: float32 [1024], replicated
- grad_second_norm_shift: float32 [1024], replicated
- grad_second_up_weight: float32 [1024, 4096], P(None, 'tensor')
- grad_second_up_bias: float32 [4096], P('tensor')
- grad_second_down_weight: float32 [4096, 1024], P('tensor')
- grad_second_down_bias: float32 [1024], replicated
- grad_final_norm_gain: float32 [1024], replicated
- grad_final_norm_shift: float32 [1024], replicated
Inputs may be any that keep to these rules, and one draw needn't show every extreme that they name: `clip_count`: for each index of dp, the number of its 2 slots that hold live clips: slots 0 to count - 1 of that index are live and its other slots are ignored; some index holds 2.
All inputs are finite; a program needn't handle non-finite values.
Results may differ from a plain program's by a relative error of at most 0.03.
Values may be sent and summed in bfloat16 or wider, within the bound.
No kernel may reach another device: no remote copies, remote signals or barrier semaphores. Data moves between devices by JAX's collectives and lax.ppermute only.
A program may use at most 384 MiB of HBM per device.

v0:
```python
import math

import jax
import jax.numpy as jnp
from jax import lax
from jax.sharding import PartitionSpec as P

D = 1024
HEAD_DIM = 64
CONV_K = 31
BACK = 64
AHEAD = 8
QBLK = 512


epsilon = 1e-05


def product(left, right):
    return jnp.dot(left, right, preferred_element_type=jnp.float32)


def product_left(left, right):
    return lax.dot_general(
        left, right, (((0,), (0,)), ((), ())), preferred_element_type=jnp.float32
    )


def product_right(left, right):
    return lax.dot_general(
        left, right, (((1,), (1,)), ((), ())), preferred_element_type=jnp.float32
    )


def widen(value):
    return value.astype(jnp.float32)


def accumulate(total, extra):
    if total is None:
        return extra
    return tuple((left + right for left, right in zip(total, extra)))


def layer_norm(values, gain, shift):
    center = jnp.mean(values, axis=-1, keepdims=True)
    offset = values - center
    inverse = lax.rsqrt(jnp.mean(offset * offset, axis=-1, keepdims=True) + epsilon)
    normal = offset * inverse
    return (normal * gain + shift, normal, inverse)


def norm_back(incoming, normal, inverse, gain):
    scaled = incoming * gain
    first_mean = jnp.mean(scaled, axis=-1, keepdims=True)
    second_mean = jnp.mean(scaled * normal, axis=-1, keepdims=True)
    result = inverse * (scaled - first_mean - normal * second_mean)
    return (result, jnp.sum(incoming * normal, axis=0), jnp.sum(incoming, axis=0))


def gather_rows(values):
    return lax.all_gather(values, "tensor", axis=0, tiled=True)


def spread_normed(values):
    return gather_rows(values)


def spread_grads(values):
    return lax.all_gather(values, "tensor", axis=0, tiled=True)


def sum_rows(term, count):
    summed = lax.psum_scatter(
        term(jnp.int32(0), count * lax.axis_size("tensor")).astype(jnp.bfloat16),
        "tensor",
        scatter_dimension=0,
        tiled=True,
    ).astype(jnp.float32)
    return summed


def sum_grads(term, count):
    summed = lax.psum_scatter(
        term(jnp.int32(0), count * lax.axis_size("tensor")).astype(jnp.bfloat16),
        "tensor",
        scatter_dimension=0,
        tiled=True,
    ).astype(jnp.float32)
    return summed


def distance(rows, length, begin):
    return (
        lax.broadcasted_iota(jnp.int32, (rows, length), 1)
        - lax.broadcasted_iota(jnp.int32, (rows, length), 0)
        - begin
    )


def place_columns(matrix, first_column, total):
    matrix = matrix[:, :, -first_column:]
    first_column = 0
    matrix = matrix[:, :, : total - first_column]
    return matrix


def take_columns(matrix, first_column, width):
    total = matrix.shape[-1]
    before = max(0, -first_column)
    after = max(0, first_column + width - total)
    padded = jnp.pad(matrix, ((0, 0), (0, 0), (before, after)))
    return padded


def spread_band(relative, begin, length):
    heads, rows, width = relative.shape
    padded = jnp.pad(relative, ((0, 0), (0, 0), (0, rows)))
    flat = padded.reshape(heads, rows * (width + rows))[:, : rows * (width + rows - 1)]
    band = flat.reshape(heads, rows, width + rows - 1)
    placed = place_columns(band, begin - BACK, length)
    offset = distance(rows, length, begin)
    inner = jnp.where(offset > AHEAD, relative[:, :, width - 1 :], placed)
    return jnp.where(offset < -BACK, relative[:, :, :1], inner)


def gather_band(incoming, begin, width):
    heads, rows, length = incoming.shape
    offset = distance(rows, length, begin)
    back_total = jnp.sum(jnp.where(offset < -BACK, incoming, 0.0), axis=-1, keepdims=True)
    ahead_total = jnp.sum(jnp.where(offset > AHEAD, incoming, 0.0), axis=-1, keepdims=True)
    band = take_columns(incoming, begin - BACK, width + rows - 1)
    flat = jnp.pad(band.reshape(heads, rows * (width + rows - 1)), ((0, 0), (0, rows)))
    inner = flat.reshape(heads, rows, width + rows)[:, :, :width]
    return jnp.concatenate(
        [
            inner[:, :, :1] + back_total,
            inner[:, :, 1 : width - 1],
            inner[:, :, width - 1 :] + ahead_total,
        ],
        axis=-1,
    )


def block_scores(query_block, keys, relative_table, begin, length):
    content = jnp.einsum("qhe,khe->hqk", query_block, keys, preferred_element_type=jnp.float32)
    relative = jnp.einsum(
        "qhe,re->hqr", query_block, relative_table, preferred_element_type=jnp.float32
    )
    return (content + spread_band(relative, begin, length)) * (1.0 / math.sqrt(HEAD_DIM))


def feed_forward(residual, gain, shift, up_weight, up_bias, down_weight, down_bias):
    normed, normal, inverse = layer_norm(residual, gain, shift)
    gathered = spread_normed(normed.astype(jnp.bfloat16))
    before = product(gathered, up_weight) + up_bias
    sigma = jax.nn.sigmoid(before)
    hidden = (before * sigma).astype(jnp.bfloat16)

    def term(start, count):
        return product(hidden, down_weight)

    branch = sum_rows(term, residual.shape[0]) + down_bias
    return (residual + 0.5 * branch, (normal, inverse, gathered, before, sigma, hidden))


def feed_back(incoming, kept, gain, up_weight, down_weight):
    normal, inverse, gathered, before, sigma, hidden = kept
    branch_grad = 0.5 * incoming
    spread = spread_grads(branch_grad.astype(jnp.bfloat16))
    down_grad = product_left(hidden, spread)
    before_grad = product_right(spread, down_weight) * sigma * (1.0 + before * (1.0 - sigma))
    before_low = before_grad.astype(jnp.bfloat16)
    up_grad = product_left(gathered, before_low)

    def term(start, count):
        return product_right(before_low, up_weight)

    normed_grad = sum_grads(term, incoming.shape[0])
    residual_grad, gain_grad, shift_grad = norm_back(normed_grad, normal, inverse, gain)
    return (
        incoming + residual_grad,
        (
            gain_grad,
            shift_grad,
            up_grad,
            jnp.sum(before_grad, axis=0),
            down_grad,
            jnp.sum(branch_grad, axis=0),
        ),
    )


def attend(
    residual,
    gain,
    shift,
    query_weight,
    query_bias,
    key_weight,
    value_weight,
    value_bias,
    output_weight,
    output_bias,
    relative_table,
):
    normed, normal, inverse = layer_norm(residual, gain, shift)
    gathered = spread_normed(normed.astype(jnp.bfloat16))
    length = gathered.shape[0]
    shape = (length, query_weight.shape[1] // HEAD_DIM, HEAD_DIM)
    query = (product(gathered, query_weight) + query_bias).astype(jnp.bfloat16).reshape(shape)
    keys = product(gathered, key_weight).astype(jnp.bfloat16).reshape(shape)
    values = (product(gathered, value_weight) + value_bias).astype(jnp.bfloat16).reshape(shape)
    scores = block_scores(query, keys, relative_table, 0, length)
    peak = jnp.max(scores, axis=-1, keepdims=True)
    weights = jnp.exp(scores - peak)
    total = jnp.sum(weights, axis=-1, keepdims=True)
    totals = [peak + jnp.log(total)]
    probs_low = (weights / total).astype(jnp.bfloat16)
    contexts = jnp.einsum("hqk,khe->qhe", probs_low, values, preferred_element_type=jnp.float32)
    context = contexts.reshape(length, -1).astype(jnp.bfloat16)

    def term(start, count):
        return product(context, output_weight)

    branch = sum_rows(term, residual.shape[0]) + output_bias
    return (residual + branch, (normal, inverse, gathered, query, keys, values, totals, context))


def attend_back(
    incoming, kept, gain, query_weight, key_weight, value_weight, output_weight, relative_table
):
    normal, inverse, gathered, query, keys, values, totals, context = kept
    length = gathered.shape[0]
    spread = spread_grads(incoming.astype(jnp.bfloat16))
    output_grad = product_left(context, spread)
    context_grad = product_right(spread, output_weight).astype(jnp.bfloat16).reshape(query.shape)
    scale = 1.0 / math.sqrt(HEAD_DIM)
    table_wide = widen(relative_table)
    key_grad = jnp.zeros(query.shape, jnp.float32)
    value_grad = jnp.zeros(query.shape, jnp.float32)
    table_grad = jnp.zeros(table_wide.shape, jnp.float32)
    query_parts = []
    for index, begin in enumerate(range(0, length, QBLK)):
        scores = block_scores(query, keys, relative_table, begin, length)
        weights = jnp.exp(scores - totals[index])
        weight_grad = jnp.einsum(
            "qhe,khe->hqk", context_grad, values, preferred_element_type=jnp.float32
        )
        value_grad = jnp.einsum(
            "hqk,qhe->khe",
            weights.astype(jnp.bfloat16),
            context_grad,
            preferred_element_type=jnp.float32,
        )
        score_grad = (
            weights * (weight_grad - jnp.sum(weights * weight_grad, axis=-1, keepdims=True))
        ).astype(jnp.bfloat16)
        key_grad = scale * jnp.einsum(
            "hqk,qhe->khe", score_grad, query, preferred_element_type=jnp.float32
        )
        relative_grad = gather_band(
            scale * score_grad.astype(jnp.float32), begin, table_wide.shape[0]
        )
        query_part = scale * jnp.einsum(
            "hqk,khe->qhe", score_grad, keys, preferred_element_type=jnp.float32
        )
        query_part = query_part + jnp.einsum(
            "hqr,re->qhe", relative_grad, table_wide, precision=lax.Precision.HIGHEST
        )
        table_grad = jnp.einsum(
            "hqr,qhe->re", relative_grad, query.astype(jnp.float32), precision=lax.Precision.HIGHEST
        )
        query_parts.append(query_part)
    query_grad = query_parts[0]
    flat_shape = (length, query.shape[1] * HEAD_DIM)
    query_low = query_grad.reshape(flat_shape).astype(jnp.bfloat16)
    key_low = key_grad.reshape(flat_shape).astype(jnp.bfloat16)
    value_low = value_grad.reshape(flat_shape).astype(jnp.bfloat16)

    def term(start, count):
        return (
            product_right(query_low, query_weight)
            + product_right(key_low, key_weight)
            + product_right(value_low, value_weight)
        )

    normed_grad = sum_grads(term, incoming.shape[0])
    residual_grad, gain_grad, shift_grad = norm_back(normed_grad, normal, inverse, gain)
    gradients = (
        gain_grad,
        shift_grad,
        product_left(gathered, query_low),
        jnp.sum(query_grad, axis=0).reshape(-1),
        product_left(gathered, key_low),
        product_left(gathered, value_low),
        jnp.sum(value_grad, axis=0).reshape(-1),
        output_grad,
        jnp.sum(incoming, axis=0),
        table_grad,
    )
    return (incoming + residual_grad, gradients)


def convolve(
    residual, gain, shift, pointwise_in, depthwise, depth_gain, depth_shift, pointwise_out
):
    normed, normal, inverse = layer_norm(residual, gain, shift)
    gathered = spread_normed(normed.astype(jnp.bfloat16))
    length = gathered.shape[0]
    linear = product(gathered, pointwise_in[0])
    sigma = jax.nn.sigmoid(product(gathered, pointwise_in[1]))
    padded = jnp.pad(linear * sigma, ((CONV_K - 1, 0), (0, 0)))
    mixed = jnp.zeros(linear.shape, jnp.float32)
    for tap in range(CONV_K):
        mixed = mixed + padded[tap : tap + length] * depthwise[tap]
    first_sum, second_sum = lax.psum(
        (jnp.sum(mixed, axis=-1), jnp.sum(mixed * mixed, axis=-1)), "tensor"
    )
    center = (first_sum / D)[:, None]
    channel_inverse = lax.rsqrt(second_sum[:, None] / D - center * center + epsilon)
    channel_normal = (mixed - center) * channel_inverse
    shaped = channel_normal * depth_gain + depth_shift
    shaped_sigma = jax.nn.sigmoid(shaped)
    active = (shaped * shaped_sigma).astype(jnp.bfloat16)

    def term(start, count):
        return product(active, pointwise_out)

    branch = sum_rows(term, residual.shape[0])
    return (
        residual + branch,
        (
            normal,
            inverse,
            gathered,
            linear,
            sigma,
            padded,
            channel_inverse,
            channel_normal,
            shaped,
            shaped_sigma,
            active,
        ),
    )


def convolve_back(incoming, kept, gain, pointwise_in, depthwise, depth_gain, pointwise_out):
    (
        normal,
        inverse,
        gathered,
        linear,
        sigma,
        padded,
        channel_inverse,
        channel_normal,
        shaped,
        shaped_sigma,
        active,
    ) = kept
    length = gathered.shape[0]
    spread = spread_grads(incoming.astype(jnp.bfloat16))
    out_grad = product_left(active, spread)
    shaped_grad = (
        product_right(spread, pointwise_out) * shaped_sigma * (1.0 + shaped * (1.0 - shaped_sigma))
    )
    scaled = shaped_grad * depth_gain
    first_sum, second_sum = lax.psum(
        (jnp.sum(scaled, axis=-1), jnp.sum(scaled * channel_normal, axis=-1)), "tensor"
    )
    mixed_grad = channel_inverse * (
        scaled - (first_sum / D)[:, None] - channel_normal * (second_sum / D)[:, None]
    )
    depth_grad = jnp.stack(
        [jnp.sum(mixed_grad * padded[tap : tap + length], axis=0) for tap in range(CONV_K)]
    )
    tail = jnp.pad(mixed_grad, ((0, CONV_K - 1), (0, 0)))
    glu_grad = jnp.zeros(mixed_grad.shape, jnp.float32)
    for tap in range(CONV_K):
        glu_grad = glu_grad + tail[CONV_K - 1 - tap : CONV_K - 1 - tap + length] * depthwise[tap]
    linear_low = (glu_grad * sigma).astype(jnp.bfloat16)
    gating_low = (glu_grad * linear * sigma * (1.0 - sigma)).astype(jnp.bfloat16)
    in_grad = jnp.stack([product_left(gathered, linear_low), product_left(gathered, gating_low)])

    def term(start, count):
        return product_right(linear_low, pointwise_in[0]) + product_right(
            gating_low, pointwise_in[1]
        )

    normed_grad = sum_grads(term, incoming.shape[0])
    residual_grad, gain_grad, shift_grad = norm_back(normed_grad, normal, inverse, gain)
    gradients = (
        gain_grad,
        shift_grad,
        in_grad,
        depth_grad,
        jnp.sum(shaped_grad * channel_normal, axis=0),
        jnp.sum(shaped_grad, axis=0),
        out_grad,
    )
    return (incoming + residual_grad, gradients)


def per_device(
    tokens,
    clip_count,
    first_norm_gain,
    first_norm_shift,
    first_up_weight,
    first_up_bias,
    first_down_weight,
    first_down_bias,
    attend_norm_gain,
    attend_norm_shift,
    query_weight,
    query_bias,
    key_weight,
    value_weight,
    value_bias,
    output_weight,
    output_bias,
    relative_table,
    convolve_norm_gain,
    convolve_norm_shift,
    pointwise_in,
    depthwise_weight,
    depth_norm_gain,
    depth_norm_shift,
    pointwise_out,
    second_norm_gain,
    second_norm_shift,
    second_up_weight,
    second_up_bias,
    second_down_weight,
    second_down_bias,
    final_norm_gain,
    final_norm_shift,
    cotangent,
):
    live_count = clip_count[0]
    slot_count = tokens.shape[0]
    first_gain = widen(first_norm_gain)
    first_shift = widen(first_norm_shift)
    first_bias_up = widen(first_up_bias)
    first_bias_down = widen(first_down_bias)
    attend_gain = widen(attend_norm_gain)
    attend_shift = widen(attend_norm_shift)
    query_wide = widen(query_bias)
    value_wide = widen(value_bias)
    output_wide = widen(output_bias)
    convolve_gain = widen(convolve_norm_gain)
    convolve_shift = widen(convolve_norm_shift)
    depth_wide = widen(depthwise_weight)
    depth_gain = widen(depth_norm_gain)
    depth_shift = widen(depth_norm_shift)
    second_gain = widen(second_norm_gain)
    second_shift = widen(second_norm_shift)
    second_bias_up = widen(second_up_bias)
    second_bias_down = widen(second_down_bias)
    final_gain = widen(final_norm_gain)
    final_shift = widen(final_norm_shift)
    first_total = None
    attend_total = None
    convolve_total = None
    second_total = None
    final_total = None
    outputs = []
    input_grads = []
    for slot in range(slot_count):
        live = (live_count > slot).astype(jnp.float32)
        start_low, grad_low = (tokens[slot], cotangent[slot])
        start_rows = widen(start_low)
        after_first, first_kept = feed_forward(
            start_rows,
            first_gain,
            first_shift,
            first_up_weight,
            first_bias_up,
            first_down_weight,
            first_bias_down,
        )
        after_attend, attend_kept = attend(
            after_first,
            attend_gain,
            attend_shift,
            query_weight,
            query_wide,
            key_weight,
            value_weight,
            value_wide,
            output_weight,
            output_wide,
            relative_table,
        )
        after_convolve, convolve_kept = convolve(
            after_attend,
            convolve_gain,
            convolve_shift,
            pointwise_in,
            depth_wide,
            depth_gain,
            depth_shift,
            pointwise_out,
        )
        after_second, second_kept = feed_forward(
            after_convolve,
            second_gain,
            second_shift,
            second_up_weight,
            second_bias_up,
            second_down_weight,
            second_bias_down,
        )
        final_rows, final_normal, final_inverse = layer_norm(after_second, final_gain, final_shift)
        outputs.append((final_rows * live).astype(jnp.bfloat16))
        grad_last, final_gain_grad, final_shift_grad = norm_back(
            widen(grad_low) * live, final_normal, final_inverse, final_gain
        )
        final_total = accumulate(final_total, (final_gain_grad, final_shift_grad))
        grad_third, second_grads = feed_back(
            grad_last, second_kept, second_gain, second_up_weight, second_down_weight
        )
        second_total = accumulate(second_total, second_grads)
        grad_second, convolve_grads = convolve_back(
            grad_third,
            convolve_kept,
            convolve_gain,
            pointwise_in,
            depth_wide,
            depth_gain,
            pointwise_out,
        )
        convolve_total = accumulate(convolve_total, convolve_grads)
        grad_first, attend_grads = attend_back(
            grad_second,
            attend_kept,
            attend_gain,
            query_weight,
            key_weight,
            value_weight,
            output_weight,
            relative_table,
        )
        attend_total = accumulate(attend_total, attend_grads)
        grad_input, first_grads = feed_back(
            grad_first, first_kept, first_gain, first_up_weight, first_down_weight
        )
        first_total = accumulate(first_total, first_grads)
        input_grads.append(grad_input)
    reduced = (
        lax.psum(first_total[2].astype(jnp.bfloat16), "dp").astype(jnp.float32),
        lax.psum(first_total[3].astype(jnp.bfloat16), "dp").astype(jnp.float32),
        lax.psum(first_total[4].astype(jnp.bfloat16), "dp").astype(jnp.float32),
        lax.psum(attend_total[2].astype(jnp.bfloat16), "dp").astype(jnp.float32),
        lax.psum(attend_total[3].astype(jnp.bfloat16), "dp").astype(jnp.float32),
        lax.psum(attend_total[4].astype(jnp.bfloat16), "dp").astype(jnp.float32),
        lax.psum(attend_total[5].astype(jnp.bfloat16), "dp").astype(jnp.float32),
        lax.psum(attend_total[6].astype(jnp.bfloat16), "dp").astype(jnp.float32),
        lax.psum(attend_total[7].astype(jnp.bfloat16), "dp").astype(jnp.float32),
        lax.psum(convolve_total[2].astype(jnp.bfloat16), "dp").astype(jnp.float32),
        lax.psum(convolve_total[3].astype(jnp.bfloat16), "dp").astype(jnp.float32),
        lax.psum(convolve_total[4].astype(jnp.bfloat16), "dp").astype(jnp.float32),
        lax.psum(convolve_total[5].astype(jnp.bfloat16), "dp").astype(jnp.float32),
        lax.psum(convolve_total[6].astype(jnp.bfloat16), "dp").astype(jnp.float32),
        lax.psum(second_total[2].astype(jnp.bfloat16), "dp").astype(jnp.float32),
        lax.psum(second_total[3].astype(jnp.bfloat16), "dp").astype(jnp.float32),
        lax.psum(second_total[4].astype(jnp.bfloat16), "dp").astype(jnp.float32),
    )
    first_total = (
        first_total[0],
        first_total[1],
        reduced[0],
        reduced[1],
        reduced[2],
        first_total[5],
    )
    attend_total = (
        attend_total[0],
        attend_total[1],
        reduced[3],
        reduced[4],
        reduced[5],
        reduced[6],
        reduced[7],
        reduced[8],
        attend_total[8],
        attend_total[9],
    )
    convolve_total = (
        convolve_total[0],
        convolve_total[1],
        reduced[9],
        reduced[10],
        reduced[11],
        reduced[12],
        reduced[13],
    )
    second_total = (
        second_total[0],
        second_total[1],
        reduced[14],
        reduced[15],
        reduced[16],
        second_total[5],
    )
    shared = lax.psum(
        (
            first_total[0],
            first_total[1],
            first_total[5],
            attend_total[0],
            attend_total[1],
            attend_total[8],
            attend_total[9],
            convolve_total[0],
            convolve_total[1],
            second_total[0],
            second_total[1],
            second_total[5],
            final_total[0],
            final_total[1],
            live_count.astype(jnp.float32),
        ),
        ("dp", "tensor"),
    )
    clips = shared[14] / lax.axis_size("tensor")
    every_grad = (
        shared[0],
        shared[1],
        first_total[2],
        first_total[3],
        first_total[4],
        shared[2],
        shared[3],
        shared[4],
        attend_total[2],
        attend_total[3],
        attend_total[4],
        attend_total[5],
        attend_total[6],
        attend_total[7],
        shared[5],
        shared[6],
        shared[7],
        shared[8],
        convolve_total[2],
        convolve_total[3],
        convolve_total[4],
        convolve_total[5],
        convolve_total[6],
        shared[9],
        shared[10],
        second_total[2],
        second_total[3],
        second_total[4],
        shared[11],
        shared[12],
        shared[13],
    )
    return (jnp.stack(outputs), jnp.stack(input_grads)) + tuple(
        (value / clips for value in every_grad)
    )


def solution(mesh):
    placed = (
        P("dp", "tensor", None),
        P("dp"),
        P(),
        P(),
        P(None, "tensor"),
        P("tensor"),
        P("tensor", None),
        P(),
        P(),
        P(),
        P(None, "tensor"),
        P("tensor"),
        P(None, "tensor"),
        P(None, "tensor"),
        P("tensor"),
        P("tensor", None),
        P(),
        P(),
        P(),
        P(),
        P(None, None, "tensor"),
        P(None, "tensor"),
        P("tensor"),
        P("tensor"),
        P("tensor", None),
        P(),
        P(),
        P(None, "tensor"),
        P("tensor"),
        P("tensor", None),
        P(),
        P(),
        P(),
        P("dp", "tensor", None),
    )
    return jax.shard_map(
        per_device,
        mesh=mesh,
        in_specs=placed,
        out_specs=(
            P("dp", "tensor", None),
            P("dp", "tensor", None),
            P(),
            P(),
            P(None, "tensor"),
            P("tensor"),
            P("tensor", None),
            P(),
            P(),
            P(),
            P(None, "tensor"),
            P("tensor"),
            P(None, "tensor"),
            P(None, "tensor"),
            P("tensor"),
            P("tensor", None),
            P(),
            P(),
            P(),
            P(),
            P(None, None, "tensor"),
            P(None, "tensor"),
            P("tensor"),
            P("tensor"),
            P("tensor", None),
            P(),
            P(),
            P(None, "tensor"),
            P("tensor"),
            P("tensor", None),
            P(),
            P(),
            P(),
        ),
        check_vma=False,
    )
```

profile of v0, /device:TPU:0, one launch (start us, length us, event | category | flops | bytes accessed | tf_op | source)
XLA Modules:
  0.0 1672.9 jit_solution(9580256326384282969)
XLA Ops:
  15.3 23.3 %all-gather.17.cloned.1.call-done = bf16[512,1024]{1,0:T(8,128)(2,1)} async-done(((bf16[256,1024]{1,0:T(8,128)(2,1)}), bf16[512,1024]{1,0:T(8,128)(2,1)}) %all-gather.17.cloned.1.call-update) | async-done | bytes 1048592 | tf_op jit(solution)/shard_map/all_gather | solution.py:62
  49.0 13.1 all-gather.25.cloned.1.call-done
  72.8 12.5 reduce-scatter.17.cloned.1.call-done
  85.3 23.1 %reduce-scatter.25.cloned.1.call-done = bf16[256,1024]{1,0:T(8,128)(2,1)} async-done(((bf16[512,1024]{1,0:T(8,128)(2,1)}), bf16[256,1024]{1,0:T(8,128)(2,1)}) %reduce-scatter.25.cloned.1.call-update) | async-done | bytes 524304 | tf_op jit(solution)/shard_map/reduce_scatter | solution.py:74
  115.4 19.8 %all-gather.19.cloned.1.call-done = bf16[512,1024]{1,0:T(8,128)(2,1)} async-done(((bf16[256,1024]{1,0:T(8,128)(2,1)}), bf16[512,1024]{1,0:T(8,128)(2,1)}) %all-gather.19.cloned.1.call-update) | async-done | bytes 1048592 | tf_op jit(solution)/shard_map/all_gather | solution.py:62
  140.7 17.8 %all-gather.27.cloned.1.call-done = bf16[512,1024]{1,0:T(8,128)(2,1)} async-done(((bf16[256,1024]{1,0:T(8,128)(2,1)}), bf16[512,1024]{1,0:T(8,128)(2,1)}) %all-gather.27.cloned.1.call-update) | async-done | bytes 1048592 | tf_op jit(solution)/shard_map/all_gather | solution.py:62
  170.3 11.5 reshape.439
  181.8 10.2 reshape.426
  209.2 13.1 reshape.427
  222.3 9.6 slice.909
  231.9 9.2 copy.108
  261.8 11.5 reshape.443
  273.3 10.3 reshape.421
  300.7 13.1 reshape.422
  313.9 9.6 slice.874
  323.5 9.2 copy.107
  348.3 20.6 %reduce-scatter.19.cloned.1.call-done = bf16[256,1024]{1,0:T(8,128)(2,1)} async-done(((bf16[512,1024]{1,0:T(8,128)(2,1)}), bf16[256,1024]{1,0:T(8,128)(2,1)}) %reduce-scatter.19.cloned.1.call-update) | async-done | bytes 524304 | tf_op jit(solution)/shard_map/reduce_scatter | solution.py:74
  374.1 20.8 %all-gather.21.cloned.1.call-done = bf16[512,1024]{1,0:T(8,128)(2,1)} async-done(((bf16[256,1024]{1,0:T(8,128)(2,1)}), bf16[512,1024]{1,0:T(8,128)(2,1)}) %all-gather.21.cloned.1.call-update) | async-done | bytes 1048592 | tf_op jit(solution)/shard_map/all_gather | solution.py:62
  405.3 12.9 all-gather.29.cloned.1.call-done
  439.4 17.1 %reduce-scatter.21.cloned.1.call-done = bf16[256,1024]{1,0:T(8,128)(2,1)} async-done(((bf16[512,1024]{1,0:T(8,128)(2,1)}), bf16[256,1024]{1,0:T(8,128)(2,1)}) %reduce-scatter.21.cloned.1.call-update) | async-done | bytes 524304 | tf_op jit(solution)/shard_map/reduce_scatter | solution.py:74
  459.0 20.6 %reduce-scatter.29.cloned.1.call-done = bf16[256,1024]{1,0:T(8,128)(2,1)} async-done(((bf16[512,1024]{1,0:T(8,128)(2,1)}), bf16[256,1024]{1,0:T(8,128)(2,1)}) %reduce-scatter.29.cloned.1.call-update) | async-done | bytes 524304 | tf_op jit(solution)/shard_map/reduce_scatter | solution.py:74
  483.5 20.6 %all-gather.31.cloned.1.call-done = bf16[512,1024]{1,0:T(8,128)(2,1)} async-done(((bf16[256,1024]{1,0:T(8,128)(2,1)}), bf16[512,1024]{1,0:T(8,128)(2,1)}) %all-gather.31.cloned.1.call-update) | async-done | bytes 1048592 | tf_op jit(solution)/shard_map/all_gather | solution.py:62
  514.6 12.9 all-gather.23.cloned.1.call-done
  538.7 11.8 reduce-scatter.31.cloned.1.call-done
  550.5 23.1 %reduce-scatter.23.cloned.1.call-done = bf16[256,1024]{1,0:T(8,128)(2,1)} async-done(((bf16[512,1024]{1,0:T(8,128)(2,1)}), bf16[256,1024]{1,0:T(8,128)(2,1)}) %reduce-scatter.23.cloned.1.call-update) | async-done | bytes 524304 | tf_op jit(solution)/shard_map/reduce_scatter | solution.py:74
  585.3 18.8 %all-gather.33.cloned.1.call-done = bf16[512,1024]{1,0:T(8,128)(2,1)} async-done(((bf16[256,1024]{1,0:T(8,128)(2,1)}), bf16[512,1024]{1,0:T(8,128)(2,1)}) %all-gather.33.cloned.1.call-update) | async-done | bytes 1048592 | tf_op jit(solution)/shard_map/all_gather | solution.py:70
  616.6 10.8 all-gather.41.cloned.1.call-done
  640.1 9.9 reduce-scatter.33.cloned.1.call-done
  652.5 20.0 %reduce-scatter.41.cloned.1.call-done = bf16[256,1024]{1,0:T(8,128)(2,1)} async-done(((bf16[512,1024]{1,0:T(8,128)(2,1)}), bf16[256,1024]{1,0:T(8,128)(2,1)}) %reduce-scatter.41.cloned.1.call-update) | async-done | bytes 524304 | tf_op jit(solution)/shard_map/reduce_scatter | solution.py:84
  687.4 9.6 add_convert_fusion
  703.8 19.4 %all-gather.35.cloned.1.call-done = bf16[512,1024]{1,0:T(8,128)(2,1)} async-done(((bf16[256,1024]{1,0:T(8,128)(2,1)}), bf16[512,1024]{1,0:T(8,128)(2,1)}) %all-gather.35.cloned.1.call-update) | async-done | bytes 1048592 | tf_op jit(solution)/shard_map/all_gather | solution.py:70
  733.6 14.1 multiply_reduce_fusion.35
  785.7 14.8 reduce-scatter.43.cloned.1.call-done
  812.9 14.0 all-gather.37.cloned.1.call-done
  841.2 9.1 copy.117
  850.3 10.1 pad.42.clone
  860.4 13.2 reshape.451
  899.1 13.0 reshape.430
  930.9 9.3 multiply_reduce_fusion
  954.6 9.5 copy.118
  964.1 10.1 pad.45.clone
  974.2 13.2 reshape.447
  1012.9 12.8 reshape.433
  1083.2 11.5 reduce-scatter.45.cloned.1.call-done
  1112.6 11.4 all-gather.47.cloned.1.call-done
  1198.9 64.4 %all-reduce.13 = (bf16[2048]{0:T(1024)(128)(2,1)S(1)}, bf16[512]{0:T(512)(128)(2,1)S(1)}, bf16[512]{0:T(512)(128)(2,1)S(1)}, bf16[31,512]{1,0:T(8,128)(2,1)S(1)}...) all-reduce(bf16[2048]{0:T(1024)(128)(2,1)S(1)} %add_convert_fusion., ...), channel_id=1, replica_groups=mesh['dp'=16,'tensor'=2] {'dp'}, use_global_device_ids=true, to_apply=%region_92.93 | all-reduce | flops 22016 | bytes 88064 | tf_op jit(solution)/shard_map/psum | solution.py:554
  1265.7 40.9 %all-reduce.19 = (f32[1024]{0:T(1024)S(1)}, f32[]{:T(128)}, f32[1024]{0:T(1024)S(1)}, f32[1024]{0:T(1024)S(1)}, f32[1024]{0:T(1024)S(1)}, /*index=5*/f32[1024]{0...) all-reduce(f32[1024]{0:T(1024)S(1)} %add.1224, ...), channel_id=1, replica_groups=mesh['dp'=16,'tensor'=2] {'dp','tensor'}, use_global_device_ids=true, to_apply=%region_84.85 | all-reduce | flops 17985 | bytes 143880 | tf_op jit(solution)/shard_map/psum | solution.py:608
  1323.4 309.6 %all-reduce.18.cloned.1.call-done = (bf16[1024,2048]{1,0:T(8,128)(2,1)}, bf16[2048,1024]{1,0:T(8,128)(2,1)}, bf16[1024,512]{1,0:T(8,128)(2,1)}, bf16[1024,512]{1...) async-done(((bf16[1024,2048]{1,0:T(8,128)(2,1)}, ...) | async-done | bytes 24117264 | tf_op jit(solution)/shard_map/psum | solution.py:553
  (865 shorter events, 606.0 us)
Async XLA Ops:
  7.2 427.0 %copy-start = (bf16[512,1024]{1,0:T(8,128)(2,1)S(1)}, bf16[512,1024]{1,0:T(8,128)(2,1)}, u32[]{:S(2)}) copy-start(bf16[512,1024]{1,0:T(8,128)(2,1)} %param.58) | copy-start | bytes 3145732
  7.2 31.4 %all-gather.17.cloned.1.call-start = ((), (), s32[]{:S(2)}) async-start(), calls=%async_computation.16 | async-start | bytes 1572864 | tf_op jit(solution)/shard_map/all_gather | solution.py:62
  14.5 47.6 %all-gather.25.cloned.1.call-start = ((), (), s32[]{:S(2)}) async-start(), calls=%async_computation.24 | async-start | bytes 1572864 | tf_op jit(solution)/shard_map/all_gather | solution.py:62
  15.2 70.0 %reduce-scatter.17.cloned.1.call-start = ((), (), s32[]{:S(2)}) async-start(), calls=%async_computation.17 | async-start | bytes 1572864 | tf_op jit(solution)/shard_map/reduce_scatter | solution.py:74
  49.0 59.4 %reduce-scatter.25.cloned.1.call-start = ((), (), s32[]{:S(2)}) async-start(), calls=%async_computation.25 | async-start | bytes 1572864 | tf_op jit(solution)/shard_map/reduce_scatter | solution.py:74
  72.6 62.6 %all-gather.19.cloned.1.call-start = ((), (), s32[]{:S(2)}) async-start(), calls=%async_computation.18 | async-start | bytes 1572864 | tf_op jit(solution)/shard_map/all_gather | solution.py:62
  72.7 296.2 %copy-start.118 = (f32[1024]{0:T(1024)}, f32[1024]{0:T(1024)S(1)}, u32[]{:S(2)}) copy-start(f32[1024]{0:T(1024)S(1)} %convert_element_type.536) | copy-start | bytes 12292
  113.7 44.8 %all-gather.27.cloned.1.call-start = ((), (), s32[]{:S(2)}) async-start(), calls=%async_computation.26 | async-start | bytes 1572864 | tf_op jit(solution)/shard_map/all_gather | solution.py:62
  114.3 234.0 %reduce-scatter.27.cloned.1.call-start = ((), (), s32[]{:S(2)}) async-start(), calls=%async_computation.27 | async-start | bytes 1572864 | tf_op jit(solution)/shard_map/reduce_scatter | solution.py:74
  255.3 113.6 %reduce-scatter.19.cloned.1.call-start = ((), (), s32[]{:S(2)}) async-start(), calls=%async_computation.19 | async-start | bytes 1572864 | tf_op jit(solution)/shard_map/reduce_scatter | solution.py:74
  348.1 46.8 %all-gather.21.cloned.1.call-start = ((), (), s32[]{:S(2)}) async-start(), calls=%async_computation.20 | async-start | bytes 1572864 | tf_op jit(solution)/shard_map/all_gather | solution.py:62
  373.5 44.8 %all-gather.29.cloned.1.call-start = ((), (), s32[]{:S(2)}) async-start(), calls=%async_computation.28 | async-start | bytes 1572864 | tf_op jit(solution)/shard_map/all_gather | solution.py:62
  373.6 383.4 %copy-start.133 = (f32[512]{0:T(512)}, f32[512]{0:T(512)S(1)}, u32[]{:S(2)}) copy-start(f32[512]{0:T(512)S(1)} %convert_element_type.556) | copy-start | bytes 6148
  373.6 349.6 %copy-start.204 = (f32[512]{0:T(512)}, f32[512]{0:T(512)S(1)}, u32[]{:S(2)}) copy-start(f32[512]{0:T(512)S(1)} %convert_element_type.557) | copy-start | bytes 6148
  374.1 82.5 %reduce-scatter.21.cloned.1.call-start = ((), (), s32[]{:S(2)}) async-start(), calls=%async_computation.21 | async-start | bytes 1572864 | tf_op jit(solution)/shard_map/reduce_scatter | solution.py:74
  434.1 299.4 %copy-start.180 = (f32[512]{0:T(512)}, f32[512]{0:T(512)S(1)}, u32[]{:S(2)}) copy-start(f32[512]{0:T(512)S(1)} %get-tuple-element.326) | copy-start | bytes 6148
  434.1 299.4 %copy-start.182 = (f32[512]{0:T(512)}, f32[512]{0:T(512)S(1)}, u32[]{:S(2)}) copy-start(f32[512]{0:T(512)S(1)} %get-tuple-element.327) | copy-start | bytes 6148
  436.1 43.6 %reduce-scatter.29.cloned.1.call-start = ((), (), s32[]{:S(2)}) async-start(), calls=%async_computation.29 | async-start | bytes 1572864 | tf_op jit(solution)/shard_map/reduce_scatter | solution.py:74
  436.1 320.9 %copy-start.184 = (f32[512]{0:T(512)}, f32[512]{0:T(512)S(1)}, u32[]{:S(2)}) copy-start(f32[512]{0:T(512)S(1)} %get-tuple-element.328) | copy-start | bytes 6148
  436.1 320.9 %copy-start.186 = (f32[512]{0:T(512)}, f32[512]{0:T(512)S(1)}, u32[]{:S(2)}) copy-start(f32[512]{0:T(512)S(1)} %get-tuple-element.329) | copy-start | bytes 6148
  439.3 64.8 %all-gather.31.cloned.1.call-start = ((), (), s32[]{:S(2)}) async-start(), calls=%async_computation.30 | async-start | bytes 1572864 | tf_op jit(solution)/shard_map/all_gather | solution.py:62
  482.7 44.8 %all-gather.23.cloned.1.call-start = ((), (), s32[]{:S(2)}) async-start(), calls=%async_computation.22 | async-start | bytes 1572864 | tf_op jit(solution)/shard_map/all_gather | solution.py:62
  483.3 67.2 %reduce-scatter.31.cloned.1.call-start = ((), (), s32[]{:S(2)}) async-start(), calls=%async_computation.31 | async-start | bytes 1572864 | tf_op jit(solution)/shard_map/reduce_scatter | solution.py:74
  514.6 59.0 %reduce-scatter.23.cloned.1.call-start = ((), (), s32[]{:S(2)}) async-start(), calls=%async_computation.23 | async-start | bytes 1572864 | tf_op jit(solution)/shard_map/reduce_scatter | solution.py:74
  537.9 66.2 %all-gather.33.cloned.1.call-start = ((), (), s32[]{:S(2)}) async-start(), calls=%async_computation.32 | async-start | bytes 1572864 | tf_op jit(solution)/shard_map/all_gather | solution.py:70
  582.6 44.8 %all-gather.41.cloned.1.call-start = ((), (), s32[]{:S(2)}) async-start(), calls=%async_computation.40 | async-start | bytes 1572864 | tf_op jit(solution)/shard_map/all_gather | solution.py:70
  584.8 65.2 %reduce-scatter.33.cloned.1.call-start = ((), (), s32[]{:S(2)}) async-start(), calls=%async_computation.33 | async-start | bytes 1572864 | tf_op jit(solution)/shard_map/reduce_scatter | solution.py:84
  616.5 56.0 %reduce-scatter.41.cloned.1.call-start = ((), (), s32[]{:S(2)}) async-start(), calls=%async_computation.41 | async-start | bytes 1572864 | tf_op jit(solution)/shard_map/reduce_scatter | solution.py:84
  639.9 60.5 %all-gather.43.cloned.1.call-start = ((), (), s32[]{:S(2)}) async-start(), calls=%async_computation.42 | async-start | bytes 1572864 | tf_op jit(solution)/shard_map/all_gather | solution.py:70
  678.9 44.3 %all-gather.35.cloned.1.call-start = ((), (), s32[]{:S(2)}) async-start(), calls=%async_computation.34 | async-start | bytes 1572864 | tf_op jit(solution)/shard_map/all_gather | solution.py:70
  687.3 96.1 %reduce-scatter.35.cloned.1.call-start = ((), (), s32[]{:S(2)}) async-start(), calls=%async_computation.35 | async-start | bytes 1572864 | tf_op jit(solution)/shard_map/reduce_scatter | solution.py:84
  756.9 43.6 %reduce-scatter.43.cloned.1.call-start = ((), (), s32[]{:S(2)}) async-start(), calls=%async_computation.43 | async-start | bytes 1572864 | tf_op jit(solution)/shard_map/reduce_scatter | solution.py:84
  769.7 57.1 %all-gather.37.cloned.1.call-start = ((), (), s32[]{:S(2)}) async-start(), calls=%async_computation.36 | async-start | bytes 1572864 | tf_op jit(solution)/shard_map/all_gather | solution.py:70
  805.4 123.5 %all-gather.45.cloned.1.call-start = ((), (), s32[]{:S(2)}) async-start(), calls=%async_computation.44 | async-start | bytes 1572864 | tf_op jit(solution)/shard_map/all_gather | solution.py:70
  812.8 270.4 %reduce-scatter.37.cloned.1.call-start = ((), (), s32[]{:S(2)}) async-start(), calls=%async_computation.37 | async-start | bytes 1572864 | tf_op jit(solution)/shard_map/reduce_scatter | solution.py:84
  917.2 117.3 %copy-start.57 = (bf16[8,64,512]{2,1,0:T(8,128)(2,1)}, bf16[8,64,512]{2,1,0:T(8,128)(2,1)S(1)}, u32[]{:S(2)}) copy-start(bf16[8,64,512]{2,1,0:T(8,128)(2,1)S(1)} %fusion.65) | copy-start | bytes 1572868
  950.0 109.3 %copy-start.55 = (bf16[8,64,512]{2,1,0:T(8,128)(2,1)}, bf16[8,64,512]{2,1,0:T(8,128)(2,1)S(1)}, u32[]{:S(2)}) copy-start(bf16[8,64,512]{2,1,0:T(8,128)(2,1)S(1)} %fusion.66) | copy-start | bytes 1572868
  1051.0 43.7 %reduce-scatter.45.cloned.1.call-start = ((), (), s32[]{:S(2)}) async-start(), calls=%async_computation.45 | async-start | bytes 1572864 | tf_op jit(solution)/shard_map/reduce_scatter | solution.py:84
  1067.6 56.4 %all-gather.47.cloned.1.call-start = ((), (), s32[]{:S(2)}) async-start(), calls=%async_computation.46 | async-start | bytes 1572864 | tf_op jit(solution)/shard_map/all_gather | solution.py:70
  1102.5 44.8 %all-gather.39.cloned.1.call-start = ((), (), s32[]{:S(2)}) async-start(), calls=%async_computation.38 | async-start | bytes 1572864 | tf_op jit(solution)/shard_map/all_gather | solution.py:70
  1112.1 151.2 %reduce-scatter.47.cloned.1.call-start = ((), (), s32[]{:S(2)}) async-start(), calls=%async_computation.47 | async-start | bytes 1572864 | tf_op jit(solution)/shard_map/reduce_scatter | solution.py:84
  1136.5 126.9 %reduce-scatter.39.cloned.1.call-start = ((), (), s32[]{:S(2)}) async-start(), calls=%async_computation.39 | async-start | bytes 1572864 | tf_op jit(solution)/shard_map/reduce_scatter | solution.py:84
  1159.8 473.1 %all-reduce.18.cloned.1.call-start = ((), (), s32[]{:S(2)}) async-start(), calls=%async_computation.48 | async-start | bytes 48234496 | tf_op jit(solution)/shard_map/psum | solution.py:553
  1184.7 78.6 %copy-start.124 = (f32[1024]{0:T(1024)S(1)}, f32[1024]{0:T(1024)}, u32[]{:S(2)}) copy-start(f32[1024]{0:T(1024)} %copy-done.123) | copy-start | bytes 12292
  1184.8 78.6 %copy-start.130 = (f32[256]{0:T(256)S(1)}, f32[256]{0:T(256)}, u32[]{:S(2)}) copy-start(f32[256]{0:T(256)} %copy-done.129) | copy-start | bytes 3076
  1184.8 78.6 %copy-start.132 = (f32[256]{0:T(256)S(1)}, f32[256]{0:T(256)}, u32[]{:S(2)}) copy-start(f32[256]{0:T(256)} %copy-done.131) | copy-start | bytes 3076
  1187.1 120.2 %copy-start.45 = (f32[256,1024]{1,0:T(8,128)S(1)}, f32[256,1024]{1,0:T(8,128)}, u32[]{:S(2)}) copy-start(f32[256,1024]{1,0:T(8,128)} %get-tuple-element.220) | copy-start | bytes 3145732
  1190.5 116.8 %copy-start.47 = (f32[256,1024]{1,0:T(8,128)S(1)}, f32[256,1024]{1,0:T(8,128)}, u32[]{:S(2)}) copy-start(f32[256,1024]{1,0:T(8,128)} %copy-done.46) | copy-start | bytes 3145732
  (231 other events, 2010.7 us)
Sparse Core Ops, SparseCore 0:
  14.6 23.9 all-gather.16
  40.8 21.2 all-gather.24
  64.9 20.3 reduce-scatter.16
  88.1 20.3 reduce-scatter.24
  113.8 21.2 all-gather.18
  137.2 21.2 all-gather.26
  255.4 20.3 reduce-scatter.26
  348.3 20.6 reduce-scatter.18
  373.6 21.3 all-gather.20
  396.9 21.2 all-gather.28
  436.2 20.3 reduce-scatter.20
  459.3 20.3 reduce-scatter.28
  482.8 21.2 all-gather.30
  506.1 21.2 all-gather.22
  530.1 20.3 reduce-scatter.30
  553.3 20.3 reduce-scatter.22
  582.7 21.2 all-gather.32
  606.1 21.2 all-gather.40
  629.6 20.3 reduce-scatter.32
  652.2 20.3 reduce-scatter.40
  679.0 21.2 all-gather.42
  701.9 21.2 all-gather.34
  757.1 20.3 reduce-scatter.34
  780.2 20.3 reduce-scatter.42
  805.5 21.2 all-gather.36
  828.8 21.2 all-gather.44
  1051.2 20.2 reduce-scatter.36
  1074.4 20.3 reduce-scatter.44
  1102.7 21.2 all-gather.46
  1126.0 21.2 all-gather.38
  1150.1 20.3 reduce-scatter.46
  1173.4 20.3 reduce-scatter.38
  1202.3 430.5 all-reduce.17
where the time goes:
time: 1690 us; the launch traced here: 1670 us
  waiting for transfers between devices  724 us (43%)
  local copies, waits for them, and re-layouts  366 us (22%)
  matrix products  258 us (15%)
  other arithmetic  186 us (11%)
  blocking collectives  116 us (7%)
  between operations  19.5 us (1%)
    psum x1, waiting for transfers between devices, per_device(): lax.psum(first_total[2].astype(jnp.bfloat16), 'dp').astype(jnp.float32)  310 us
    unnamed x516, local copies, waits for them, and re-layouts  168 us
    all_gather x8, waiting for transfers between devices, gather_rows(): return lax.all_gather(values, 'tensor', axis=0, tiled=True)  141 us
    reduce_scatter x8, waiting for transfers between devices, sum_rows(): lax.psum_scatter(term(jnp.int32(0), count * lax.axis_size('tensor')).asty...  129 us
    all_gather x8, waiting for transfers between devices, spread_grads(): return lax.all_gather(values, 'tensor', axis=0, tiled=True)  85.3 us
    dot_general x22, matrix products, product_left(): lax.dot_general(left, right, (((0,), (0,)), ((), ())), preferred_element_...  74 us
    dot_general x22, matrix products, product_right(): lax.dot_general(left, right, (((1,), (1,)), ((), ())), preferred_element_...  70.4 us
    psum x1, blocking collectives, per_device(): lax.psum(first_total[3].astype(jnp.bfloat16), 'dp').astype(jnp.float32)  64.4 us
  transfers between devices with their start and end apart: 33, of which 27 were waited for; matrix products, arithmetic and copies ran while one was open for 27% of the time, Pallas kernels for 0%

commit v1 on v0

v1 whole, which is shorter than its diff:
```python
import math

import jax
import jax.numpy as jnp
from jax import lax
from jax.experimental import pallas as pl
from jax.experimental.pallas import tpu as pltpu
from jax.sharding import PartitionSpec as P

D = 1024
HEAD_DIM = 64
CONV_K = 31
BACK = 64
AHEAD = 8
VMEM_LIMIT = 32 << 20

epsilon = 1e-05


def product(left, right):
    return jnp.dot(left, right, preferred_element_type=jnp.float32)


def product_left(left, right):
    return lax.dot_general(
        left, right, (((0,), (0,)), ((), ())), preferred_element_type=jnp.float32
    )


def product_right(left, right):
    return lax.dot_general(
        left, right, (((1,), (1,)), ((), ())), preferred_element_type=jnp.float32
    )


def widen(value):
    return value.astype(jnp.float32)


def narrow(value):
    return value.astype(jnp.bfloat16)


def norm_stats(values):
    center = jnp.mean(values, axis=-1, keepdims=True)
    offset = values - center
    inverse = lax.rsqrt(jnp.mean(offset * offset, axis=-1, keepdims=True) + epsilon)
    return center, inverse


def layer_norm(values, gain, shift):
    center, inverse = norm_stats(values)
    normal = (values - center) * inverse
    return normal * gain + shift, center, inverse


def norm_back(incoming, normal, inverse, gain):
    scaled = incoming * gain
    first_mean = jnp.mean(scaled, axis=-1, keepdims=True)
    second_mean = jnp.mean(scaled * normal, axis=-1, keepdims=True)
    result = inverse * (scaled - first_mean - normal * second_mean)
    return (result, jnp.sum(incoming * normal, axis=0), jnp.sum(incoming, axis=0))


def paired():
    return lax.axis_size("tensor") == 2


def swap(values):
    return lax.ppermute(values, "tensor", [(0, 1), (1, 0)])


def rows_of(values, which):
    count = values.shape[0] // lax.axis_size("tensor")
    return lax.dynamic_slice_in_dim(values, which * count, count, 0)


def own_rows(values):
    return rows_of(values, lax.axis_index("tensor"))


def wide_sum(share):
    if paired():
        return share + swap(share)
    return lax.psum(share, "tensor")


class Gathered:
    def __init__(self, values):
        self.sent = values

    def move(self, sent):
        if paired():
            return swap(sent)
        return lax.all_gather(sent, "tensor", axis=0, tiled=True)

    def finish(self, sent, got):
        if not paired():
            return got
        first = lax.axis_index("tensor") == 0
        return jnp.concatenate(
            [jnp.where(first, sent, got), jnp.where(first, got, sent)], axis=0
        )


class Summed:
    def __init__(self, share):
        self.sent = narrow(share)

    def move(self, sent):
        if paired():
            return swap(sent)
        return lax.psum(sent, "tensor")

    def finish(self, sent, got):
        if not paired():
            return widen(got)
        return widen(sent) + widen(got)


class Scattered:
    def __init__(self, share):
        self.own = None
        if paired():
            self.own = own_rows(share)
            self.sent = narrow(rows_of(share, 1 - lax.axis_index("tensor")))
        else:
            self.sent = narrow(share)

    def move(self, sent):
        if paired():
            return swap(sent)
        return lax.psum_scatter(sent, "tensor", scatter_dimension=0, tiled=True)

    def finish(self, sent, got):
        if self.own is None:
            return widen(got)
        return self.own + widen(got)


class Job:
    def __init__(self, steps):
        self.steps = steps
        self.result = None
        self.waiting = []
        self.active = True
        self.advance(None)

    def advance(self, values):
        try:
            self.waiting = list(self.steps.send(values))
        except StopIteration as ended:
            self.active = False
            self.waiting = []
            self.result = ended.value


class Flow:
    def __init__(self):
        self.jobs = []

    def launch(self, steps):
        job = Job(steps)
        self.jobs.append(job)
        return job

    def turn(self, held):
        active = [job for job in self.jobs if job.active]
        flat = list(held)
        for job in active:
            flat.extend(job.waiting)
        if len(flat) > 1:
            flat = list(lax.optimization_barrier(tuple(flat)))
        begin = len(held)
        moved = []
        for job in active:
            moved.append(flat[begin : begin + len(job.waiting)])
            begin += len(job.waiting)
        return flat[: len(held)], list(zip(active, moved))

    def run(self, clips):
        under_way = None
        got = {}

        def settle(held):
            extra = [] if under_way is None else [under_way[1].sent, under_way[2]]
            out, moved = self.turn(held + extra)
            if under_way is not None:
                got[under_way[0]] = under_way[1].finish(out[-2], out[-1])
            for job, values in moved:
                job.advance(values)
            return out[: len(held)]

        queue = list(range(len(clips)))
        started = set()
        while queue:
            place = queue.pop(0)
            if under_way is not None and under_way[0] == place:
                settle([])
                under_way = None
            try:
                if place in started:
                    request = clips[place].send(got.pop(place))
                else:
                    started.add(place)
                    request = next(clips[place])
            except StopIteration:
                continue
            (sent,) = settle([request.sent])
            request.sent = sent
            under_way = (place, request, request.move(sent))
            queue.append(place)

    def drain(self):
        while any(job.active for job in self.jobs):
            _, moved = self.turn([])
            for job, values in moved:
                job.advance(values)


def dp_grid():
    return lax.axis_size("dp") == 16


def dp_bit(bit):
    return (lax.axis_index("dp") // bit) % 2


def dp_swap(values, bit):
    return lax.ppermute(values, "dp", [(place, place ^ bit) for place in range(16)])


def piece_of(values, which, axis):
    return lax.dynamic_index_in_dim(values, which, axis, keepdims=False)


def add_low(left, right):
    return narrow(widen(left) + widen(right))


def unstack_columns(shards, values):
    width = shards.shape[-1]
    results = []
    begin = 0
    for value in values:
        size = value.shape[0] // shards.shape[0]
        pieces = []
        for _ in range(0, value.shape[1], width):
            pieces.append(shards[:, begin : begin + size].reshape(value.shape[0], width))
            begin += size
        results.append(jnp.concatenate(pieces, axis=1) if len(pieces) > 1 else pieces[0])
    return results


def split_rows(value):
    return value.reshape(2, 2, 2, 2, value.shape[0] // 16, value.shape[1])


def scatter_job(make, delay, width):
    yield []
    values = yield [narrow(value) for value in make()]
    if not dp_grid():
        return values, [lax.psum(value, "dp") for value in values]
    for _ in range(delay):
        yield []
    parts = []
    for value in values:
        for start in range(0, value.shape[1], width):
            parts.append(split_rows(value[:, start : start + width]))
    core, side, near, far = [dp_bit(bit) for bit in (1, 2, 4, 8)]
    sent = jnp.concatenate([piece_of(part, 1 - core, 3) for part in parts], axis=3)
    kept = jnp.concatenate([piece_of(part, core, 3) for part in parts], axis=3)
    part = add_low(kept, dp_swap(sent, 1))
    (got,) = yield [dp_swap(piece_of(part, 1 - side, 2), 2)]
    part = add_low(piece_of(part, side, 2), got)
    got = dp_swap(piece_of(part, 1 - near, 1), 4)
    part = add_low(piece_of(part, near, 1), got)
    (got,) = yield [dp_swap(piece_of(part, 1 - far, 0), 8)]
    return values, add_low(piece_of(part, far, 0), got)


def gather_job(jobs):
    while any(job.active for job in jobs):
        yield []
    if not dp_grid():
        return [value for job in jobs for value in job.result[1]]
    shards = jnp.concatenate([job.result[1] for job in jobs], axis=0)
    whole = lax.all_gather(shards, "dp", axis=0)
    return unstack_columns(whole, [value for job in jobs for value in job.result[0]])


def small_job(values):
    flat = jnp.concatenate([value.reshape(-1) for value in values])
    if dp_grid():
        for bit in (1, 2, 4, 8):
            (got,) = yield [dp_swap(flat, bit)]
            flat = flat + got
    else:
        flat = lax.psum(flat, "dp")
    results = []
    start = 0
    for value in values:
        results.append(flat[start : start + value.size].reshape(value.shape))
        start += value.size
    return results


SCALE = 1.0 / math.sqrt(HEAD_DIM)
PAIR = 2 * HEAD_DIM
QB = 128
WINDOW = 3 * QB


def keep_head(block, head):
    inside = lax.broadcasted_iota(jnp.int32, block.shape, 1) < HEAD_DIM
    if head == 1:
        inside = jnp.logical_not(inside)
    return jnp.where(inside, block, jnp.zeros_like(block))


def window_place():
    return lax.broadcasted_iota(jnp.int32, (QB, WINDOW), 1) - lax.broadcasted_iota(
        jnp.int32, (QB, WINDOW), 0
    )


def spread_rows(relative, block, blocks):
    low = max(block - 1, 0)
    high = min(block + 2, blocks)
    before = relative[:, 0:1]
    after = relative[:, BACK + AHEAD : BACK + AHEAD + 1]
    wide = jnp.concatenate([relative, jnp.zeros((QB, WINDOW - QB), jnp.float32)], axis=1)
    skewed = pltpu.roll(wide, QB - BACK, 1, stride=1, stride_axis=0)
    place = window_place()
    skewed = jnp.where(place < QB - BACK, before, skewed)
    skewed = jnp.where(place > QB + AHEAD, after, skewed)
    parts = []
    if low > 0:
        parts.append(jnp.broadcast_to(before, (QB, low * QB)))
    parts.append(skewed[:, (low - block + 1) * QB : (high - block + 1) * QB])
    if high < blocks:
        parts.append(jnp.broadcast_to(after, (QB, (blocks - high) * QB)))
    return jnp.concatenate(parts, axis=1)


def gather_rows_back(incoming, block, blocks, flip):
    low = max(block - 1, 0)
    high = min(block + 2, blocks)
    wide = widen(incoming)
    place = lax.broadcasted_iota(jnp.int32, wide.shape, 1) - lax.broadcasted_iota(
        jnp.int32, wide.shape, 0
    )
    back = jnp.sum(
        jnp.where(place <= block * QB - BACK, wide, 0.0), axis=-1, keepdims=True
    )
    ahead = jnp.sum(
        jnp.where(place >= block * QB + AHEAD, wide, 0.0), axis=-1, keepdims=True
    )
    parts = []
    if block == 0:
        parts.append(jnp.zeros((QB, QB), jnp.bfloat16))
    parts.append(incoming[:, low * QB : high * QB])
    if block == blocks - 1:
        parts.append(jnp.zeros((QB, QB), jnp.bfloat16))
    window = jnp.concatenate(parts, axis=1)
    reversed_rows = product(flip, window)
    moved = pltpu.roll(
        reversed_rows, WINDOW - (QB - BACK) - (QB - 1), 1, stride=1, stride_axis=0
    )[:, :QB]
    inner = product(flip, narrow(moved))
    lane = lax.broadcasted_iota(jnp.int32, (QB, QB), 1)
    inner = jnp.where(lane < BACK + AHEAD, inner, 0.0)
    inner = jnp.where(lane == 0, back, inner)
    return jnp.where(lane == BACK + AHEAD, ahead, inner)


def block_rows(block):
    return slice(block * QB, (block + 1) * QB)


def softmax_rows(content, relative, block, blocks):
    scores = (content + spread_rows(relative, block, blocks)) * SCALE
    weights = jnp.exp(scores - jnp.max(scores, axis=-1, keepdims=True))
    return weights * (1.0 / jnp.sum(weights, axis=-1, keepdims=True))


def scores_of(query_head, key_block, table_block, blocks):
    content = product_right(query_head, key_block)
    relative = product(query_head, table_block)
    rows = [
        spread_rows(relative[block * QB : (block + 1) * QB], block, blocks)
        for block in range(blocks)
    ]
    return (content + jnp.concatenate(rows, axis=0)) * SCALE


def softmax_of(scores):
    weights = jnp.exp(scores - jnp.max(scores, axis=-1, keepdims=True))
    return weights * (1.0 / jnp.sum(weights, axis=-1, keepdims=True))


def attend_kernel(query_ref, key_ref, value_ref, table_ref, context_ref):
    blocks = query_ref.shape[0] // QB
    query = query_ref[...]
    keys = key_ref[...]
    values = value_ref[...]
    table = table_ref[...]
    parts = []
    for head in range(2):
        probs = softmax_of(scores_of(keep_head(query, head), keys, table, blocks))
        parts.append(product(probs.astype(jnp.bfloat16), values))
    lane = lax.broadcasted_iota(jnp.int32, parts[0].shape, 1)
    context_ref[...] = jnp.where(lane < HEAD_DIM, parts[0], parts[1]).astype(jnp.bfloat16)


def attend_back_kernel(
    query_ref,
    key_ref,
    value_ref,
    grad_ref,
    table_ref,
    rows_ref,
    query_grad_ref,
    key_grad_ref,
    value_grad_ref,
    query_sum_ref,
    value_sum_ref,
    table_grad_ref,
    score_ref,
    wide_ref,
    probs_ref,
    low_ref,
    band_ref,
):
    @pl.when(pl.program_id(0) == 0)
    def _():
        table_grad_ref[...] = jnp.zeros_like(table_grad_ref)

    blocks = query_ref.shape[0] // QB
    query_turned = narrow(widen(query_ref[...]).T)
    grad_turned = narrow(widen(grad_ref[...]).T)
    flip = narrow(
        (
            lax.broadcasted_iota(jnp.int32, (QB, QB), 0)
            + lax.broadcasted_iota(jnp.int32, (QB, QB), 1)
            == QB - 1
        ).astype(jnp.float32)
    )
    query_parts = []
    key_parts = []
    value_parts = []
    for head in range(2):
        piece = slice(head * HEAD_DIM, (head + 1) * HEAD_DIM)
        query = keep_head(query_ref[...], head)
        score_ref[head] = product_right(query, key_ref[...])
        relative = product(query, table_ref[...])
        wide_ref[head] = product_right(keep_head(grad_ref[...], head), value_ref[...])
        for block in range(blocks):
            rows = block_rows(block)
            probs = softmax_rows(score_ref[head, rows], relative[rows], block, blocks)
            probs_ref[head, rows] = narrow(probs)
            probs_grad = wide_ref[head, rows]
            delta = jnp.sum(probs * probs_grad, axis=-1, keepdims=True)
            score_grad = narrow(probs * (probs_grad - delta))
            low_ref[head, rows] = score_grad
            band_ref[head, rows] = gather_rows_back(score_grad, block, blocks, flip)
        value_parts.append(product(grad_turned[piece], probs_ref[head]))
        key_parts.append(product(query_turned[piece], low_ref[head]))
        band = band_ref[head]
        band_high = narrow(band)
        band_low = narrow(band - widen(band_high))
        query_parts.append(
            product(low_ref[head], key_ref[...])
            + product(band_high, rows_ref[...])
            + product(band_low, rows_ref[...])
        )
        table_grad_ref[...] += SCALE * (
            product(query_turned[piece], band_high) + product(query_turned[piece], band_low)
        )
    lane = lax.broadcasted_iota(jnp.int32, query_parts[0].shape, 1)
    query_grad = SCALE * jnp.where(lane < HEAD_DIM, query_parts[0], query_parts[1])
    query_grad_ref[...] = narrow(query_grad)
    query_sum_ref[...] = jnp.sum(query_grad, axis=0, keepdims=True)
    key_grad_ref[...] = narrow(SCALE * jnp.concatenate(key_parts, axis=0).T)
    value_grad = jnp.concatenate(value_parts, axis=0).T
    value_grad_ref[...] = narrow(value_grad)
    value_sum_ref[...] = jnp.sum(value_grad, axis=0, keepdims=True)


def pair_spec(length):
    return pl.BlockSpec((length, PAIR), lambda pair: (0, pair))


def fixed_spec(shape):
    return pl.BlockSpec(shape, lambda pair: tuple(0 for _ in shape))


def table_forms(relative_table):
    padded = jnp.pad(relative_table, ((0, QB - relative_table.shape[0]), (0, 0)))
    rows = jnp.concatenate([padded, padded], axis=1)
    return rows.T, rows


def attend_heads(query, keys, values, table):
    length, width = query.shape
    return pl.pallas_call(
        attend_kernel,
        out_shape=jax.ShapeDtypeStruct((length, width), jnp.bfloat16),
        grid=(width // PAIR,),
        in_specs=[pair_spec(length)] * 3 + [fixed_spec((PAIR, QB))],
        out_specs=pair_spec(length),
        compiler_params=pltpu.CompilerParams(vmem_limit_bytes=VMEM_LIMIT),
        name="attend_heads",
    )(query, keys, values, table)


def attend_heads_back(query, keys, values, grad, table, rows):
    length, width = query.shape
    sums = pl.BlockSpec((1, PAIR), lambda pair: (0, pair))
    return pl.pallas_call(
        attend_back_kernel,
        out_shape=(
            jax.ShapeDtypeStruct((length, width), jnp.bfloat16),
            jax.ShapeDtypeStruct((length, width), jnp.bfloat16),
            jax.ShapeDtypeStruct((length, width), jnp.bfloat16),
            jax.ShapeDtypeStruct((1, width), jnp.float32),
            jax.ShapeDtypeStruct((1, width), jnp.float32),
            jax.ShapeDtypeStruct((HEAD_DIM, QB), jnp.float32),
        ),
        grid=(width // PAIR,),
        in_specs=[pair_spec(length)] * 4 + [fixed_spec((PAIR, QB)), fixed_spec((QB, PAIR))],
        out_specs=(pair_spec(length),) * 3 + (sums, sums, fixed_spec((HEAD_DIM, QB))),
        scratch_shapes=[
            pltpu.VMEM((2, length, length), jnp.float32),
            pltpu.VMEM((2, length, length), jnp.float32),
            pltpu.VMEM((2, length, length), jnp.bfloat16),
            pltpu.VMEM((2, length, length), jnp.bfloat16),
            pltpu.VMEM((2, length, QB), jnp.float32),
        ],
        compiler_params=pltpu.CompilerParams(vmem_limit_bytes=VMEM_LIMIT),
        name="attend_heads_back",
    )(query, keys, values, grad, table, rows)
LANES = 128
STRIP = 64
EDGE = 32


def mix_kernel(linear_ref, gate_ref, taps_ref, mixed_ref, sums_ref, padded_ref, total_ref):
    length = linear_ref.shape[0]
    padded_ref[0:EDGE] = jnp.zeros((EDGE, LANES), jnp.float32)
    padded_ref[EDGE : EDGE + length] = linear_ref[...] * jax.nn.sigmoid(gate_ref[...])

    def strip(index, carry):
        begin = pl.multiple_of(index * STRIP, STRIP)
        total = jnp.zeros((STRIP, LANES), jnp.float32)
        for tap in range(CONV_K):
            total = total + padded_ref[
                pl.ds(begin + EDGE - CONV_K + 1 + tap, STRIP), :
            ] * taps_ref[tap : tap + 1, :]
        mixed_ref[pl.ds(begin, STRIP), :] = total
        return carry

    lax.fori_loop(0, length // STRIP, strip, 0)
    mixed = mixed_ref[...]

    @pl.when(pl.program_id(0) == 0)
    def _():
        total_ref[...] = jnp.zeros_like(total_ref)

    total_ref[0] += mixed
    total_ref[1] += mixed * mixed

    @pl.when(pl.program_id(0) == pl.num_programs(0) - 1)
    def _():
        ones = jnp.ones((8, LANES), jnp.float32)
        sums_ref[...] = jnp.concatenate(
            [
                lax.dot_general(
                    ones,
                    total_ref[place],
                    (((1,), (1,)), ((), ())),
                    precision=lax.Precision.HIGHEST,
                    preferred_element_type=jnp.float32,
                )
                for place in range(2)
            ],
            axis=0,
        )


def mix_channels(linear, gate, taps):
    length, width = linear.shape
    block = pl.BlockSpec((length, LANES), lambda part: (0, part))
    mixed, sums = pl.pallas_call(
        mix_kernel,
        out_shape=(
            jax.ShapeDtypeStruct((length, width), jnp.float32),
            jax.ShapeDtypeStruct((16, length), jnp.float32),
        ),
        grid=(width // LANES,),
        in_specs=[block, block, pl.BlockSpec((EDGE, LANES), lambda part: (0, part))],
        out_specs=(block, pl.BlockSpec((16, length), lambda part: (0, 0))),
        scratch_shapes=[
            pltpu.VMEM((EDGE + length, LANES), jnp.float32),
            pltpu.VMEM((2, length, LANES), jnp.float32),
        ],
        compiler_params=pltpu.CompilerParams(vmem_limit_bytes=VMEM_LIMIT),
        name="mix_channels",
    )(linear, gate, taps)
    return mixed, jnp.concatenate([sums[0:1], sums[8:9]], axis=0)


def mix_back_kernel(
    grad_ref,
    linear_ref,
    gate_ref,
    taps_ref,
    linear_grad_ref,
    gating_grad_ref,
    taps_grad_ref,
    padded_ref,
    tail_ref,
    total_ref,
):
    length = linear_ref.shape[0]
    padded_ref[0:EDGE] = jnp.zeros((EDGE, LANES), jnp.float32)
    padded_ref[EDGE : EDGE + length] = linear_ref[...] * jax.nn.sigmoid(gate_ref[...])
    tail_ref[0:length] = grad_ref[...]
    tail_ref[length : length + EDGE] = jnp.zeros((EDGE, LANES), jnp.float32)
    total_ref[...] = jnp.zeros_like(total_ref)

    def strip(index, carry):
        begin = pl.multiple_of(index * STRIP, STRIP)
        here = pl.ds(begin, STRIP)
        grad = tail_ref[here, :]
        total = jnp.zeros((STRIP, LANES), jnp.float32)
        for tap in range(CONV_K):
            total = total + tail_ref[
                pl.ds(begin + CONV_K - 1 - tap, STRIP), :
            ] * taps_ref[tap : tap + 1, :]
            weighed = grad * padded_ref[pl.ds(begin + EDGE - CONV_K + 1 + tap, STRIP), :]
            total_ref[tap] += jnp.sum(weighed.reshape(STRIP // 8, 8, LANES), axis=0)
        sigma = jax.nn.sigmoid(gate_ref[here, :])
        low = total * sigma
        linear_grad_ref[here, :] = narrow(low)
        gating_grad_ref[here, :] = narrow(low * linear_ref[here, :] * (1.0 - sigma))
        return carry

    lax.fori_loop(0, length // STRIP, strip, 0)
    for tap in range(CONV_K):
        taps_grad_ref[tap : tap + 1, :] = jnp.sum(total_ref[tap], axis=0, keepdims=True)
    taps_grad_ref[CONV_K:EDGE, :] = jnp.zeros((EDGE - CONV_K, LANES), jnp.float32)


def mix_channels_back(grad, linear, gate, taps):
    length, width = linear.shape
    block = pl.BlockSpec((length, LANES), lambda part: (0, part))
    edge = pl.BlockSpec((EDGE, LANES), lambda part: (0, part))
    return pl.pallas_call(
        mix_back_kernel,
        out_shape=(
            jax.ShapeDtypeStruct((length, width), jnp.bfloat16),
            jax.ShapeDtypeStruct((length, width), jnp.bfloat16),
            jax.ShapeDtypeStruct((EDGE, width), jnp.float32),
        ),
        grid=(width // LANES,),
        in_specs=[block, block, block, edge],
        out_specs=(block, block, edge),
        scratch_shapes=[
            pltpu.VMEM((EDGE + length, LANES), jnp.float32),
            pltpu.VMEM((EDGE + length, LANES), jnp.float32),
            pltpu.VMEM((EDGE, 8, LANES), jnp.float32),
        ],
        compiler_params=pltpu.CompilerParams(vmem_limit_bytes=VMEM_LIMIT),
        name="mix_channels_back",
    )(grad, linear, gate, taps)


def feed_forward(rows, gain, shift, up_weight, up_bias, down_weight):
    normed, center, inverse = layer_norm(rows, gain, shift)
    normed = narrow(normed)
    before = product(normed, up_weight) + up_bias
    hidden = narrow(before * jax.nn.sigmoid(before))
    return product(hidden, down_weight), (rows, center, inverse, normed, before, hidden)


def feed_back(incoming, kept, up_weight, down_weight):
    before = kept[4]
    branch_grad = 0.5 * incoming
    spread = narrow(branch_grad)
    sigma = jax.nn.sigmoid(before)
    before_grad = product_right(spread, down_weight) * sigma * (1.0 + before * (1.0 - sigma))
    before_low = narrow(before_grad)
    share = product_right(before_low, up_weight)
    return share, spread, before_low, jnp.sum(before_grad, axis=0), jnp.sum(branch_grad, axis=0)


def residual_back(incoming, normed_grad, kept, gain):
    rows, center, inverse = kept[:3]
    normal = (rows - center) * inverse
    result, gain_grad, shift_grad = norm_back(normed_grad, normal, inverse, gain)
    return incoming + result, gain_grad, shift_grad


def attend(
    rows, gain, shift, query_weight, query_bias, key_weight, value_weight, value_bias, output_weight, table
):
    normed, center, inverse = layer_norm(rows, gain, shift)
    normed = narrow(normed)
    query = narrow(product(normed, query_weight) + query_bias)
    keys = narrow(product(normed, key_weight))
    values = narrow(product(normed, value_weight) + value_bias)
    context = attend_heads(query, keys, values, table)
    return (
        product(context, output_weight),
        (rows, center, inverse, normed, query, keys, values, context),
    )


def attend_back(
    incoming, kept, query_weight, key_weight, value_weight, output_weight, table, table_rows
):
    query, keys, values = kept[4:7]
    spread = narrow(incoming)
    context_grad = narrow(product_right(spread, output_weight))
    query_low, key_low, value_low, query_sum, value_sum, table_grad = attend_heads_back(
        query, keys, values, context_grad, table, table_rows
    )
    share = (
        product_right(query_low, query_weight)
        + product_right(key_low, key_weight)
        + product_right(value_low, value_weight)
    )
    return (
        share,
        spread,
        (query_low, key_low, value_low),
        query_sum[0],
        value_sum[0],
        jnp.sum(incoming, axis=0),
        table_grad,
    )


def mix(rows, gain, shift, pointwise_in, taps):
    normed, center, inverse = layer_norm(rows, gain, shift)
    normed = narrow(normed)
    linear = product(normed, pointwise_in[0])
    gate = product(normed, pointwise_in[1])
    mixed, sums = mix_channels(linear, gate, taps)
    return mixed, wide_sum(sums), (rows, center, inverse, normed, linear, gate)


def convolve(mixed, sums, depth_gain, depth_shift, pointwise_out):
    center = (sums[0] / D)[:, None]
    channel_inverse = lax.rsqrt(sums[1][:, None] / D - center * center + epsilon)
    channel_normal = (mixed - center) * channel_inverse
    shaped = channel_normal * depth_gain + depth_shift
    active = narrow(shaped * jax.nn.sigmoid(shaped))
    return product(active, pointwise_out), (channel_inverse, channel_normal, shaped, active)


def shape_back(incoming, shape_kept, depth_gain, pointwise_out):
    channel_inverse, channel_normal, shaped, active = shape_kept
    spread = narrow(incoming)
    sigma = jax.nn.sigmoid(shaped)
    shaped_grad = product_right(spread, pointwise_out) * sigma * (1.0 + shaped * (1.0 - sigma))
    scaled = shaped_grad * depth_gain
    sums = wide_sum(
        jnp.stack([jnp.sum(scaled, axis=-1), jnp.sum(scaled * channel_normal, axis=-1)])
    )
    return (
        spread,
        scaled,
        sums,
        jnp.sum(shaped_grad * channel_normal, axis=0),
        jnp.sum(shaped_grad, axis=0),
    )


def convolve_back(scaled, sums, kept, shape_kept, pointwise_in, taps):
    linear, gate = kept[4:6]
    channel_inverse, channel_normal = shape_kept[:2]
    mixed_grad = channel_inverse * (
        scaled - (sums[0] / D)[:, None] - channel_normal * (sums[1] / D)[:, None]
    )
    linear_low, gating_low, taps_grad = mix_channels_back(mixed_grad, linear, gate, taps)
    share = product_right(linear_low, pointwise_in[0]) + product_right(gating_low, pointwise_in[1])
    return share, linear_low, gating_low, taps_grad[:CONV_K]


def total(parts):
    result = parts[0]
    for part in parts[1:]:
        result = result + part
    return result


def weight_grad(lefts, rights):
    return total([product_left(left, right) for left, right in zip(lefts, rights)])


class Gradients:
    def __init__(self, flow, count):
        self.flow = flow
        self.count = count
        self.parts = {}
        self.jobs = {}

    def add(self, name, part):
        parts = self.parts.setdefault(name, [])
        parts.append(part)
        return len(parts) == self.count

    def weights(self, name, pairs, width, delay=0):
        if self.add(name, pairs):
            parts = self.parts[name]

            def make():
                return [
                    weight_grad([part[place][0] for part in parts], [part[place][1] for part in parts])
                    for place in range(len(pairs))
                ]

            self.jobs[name] = self.flow.launch(scatter_job(make, delay, width))

    def sums(self, name, values):
        self.add(name, values)

    def reduce_sums(self, name, groups):
        values = []
        for group in groups:
            parts = self.parts[group]
            values.extend(total([part[place] for part in parts]) for place in range(len(parts[0])))
        self.jobs[name] = self.flow.launch(small_job(values))

    def gather(self, name, members):
        if members[-1] in self.jobs and name not in self.jobs:
            self.jobs[name] = self.flow.launch(
                gather_job([self.jobs[member] for member in members])
            )

    def result(self, name):
        return self.jobs[name].result


def per_device(
    tokens,
    clip_count,
    first_norm_gain,
    first_norm_shift,
    first_up_weight,
    first_up_bias,
    first_down_weight,
    first_down_bias,
    attend_norm_gain,
    attend_norm_shift,
    query_weight,
    query_bias,
    key_weight,
    value_weight,
    value_bias,
    output_weight,
    output_bias,
    relative_table,
    convolve_norm_gain,
    convolve_norm_shift,
    pointwise_in,
    depthwise_weight,
    depth_norm_gain,
    depth_norm_shift,
    pointwise_out,
    second_norm_gain,
    second_norm_shift,
    second_up_weight,
    second_up_bias,
    second_down_weight,
    second_down_bias,
    final_norm_gain,
    final_norm_shift,
    cotangent,
):
    slots = range(tokens.shape[0])
    live_count = clip_count[0]
    first_gain = widen(first_norm_gain)
    attend_gain = widen(attend_norm_gain)
    convolve_gain = widen(convolve_norm_gain)
    second_gain = widen(second_norm_gain)
    final_gain = widen(final_norm_gain)
    taps = jnp.pad(widen(depthwise_weight), ((0, EDGE - CONV_K), (0, 0)))
    depth_gain = widen(depth_norm_gain)
    table, table_rows = table_forms(relative_table)
    flow = Flow()
    grads = Gradients(flow, len(slots))
    outputs = {}
    input_grads = {}
    count_job = flow.launch(small_job([jnp.full((1, 128), widen(live_count), jnp.float32)]))

    def clip(slot):
        live = (live_count > slot).astype(jnp.float32)
        rows = widen((yield Gathered(tokens[slot])))
        share, first_kept = feed_forward(
            rows,
            first_gain,
            widen(first_norm_shift),
            first_up_weight,
            widen(first_up_bias),
            first_down_weight,
        )
        rows = rows + 0.5 * ((yield Summed(share)) + widen(first_down_bias))
        share, attend_kept = attend(
            rows,
            attend_gain,
            widen(attend_norm_shift),
            query_weight,
            widen(query_bias),
            key_weight,
            value_weight,
            widen(value_bias),
            output_weight,
            table,
        )
        rows = rows + (yield Summed(share)) + widen(output_bias)
        mixed, sums, convolve_kept = mix(
            rows, convolve_gain, widen(convolve_norm_shift), pointwise_in, taps
        )
        share, shape_kept = convolve(
            mixed, sums, depth_gain, widen(depth_norm_shift), pointwise_out
        )
        rows = rows + (yield Summed(share))
        share, second_kept = feed_forward(
            rows,
            second_gain,
            widen(second_norm_shift),
            second_up_weight,
            widen(second_up_bias),
            second_down_weight,
        )
        last = own_rows(rows) + 0.5 * ((yield Scattered(share)) + widen(second_down_bias))
        normed, center, inverse = layer_norm(last, final_gain, widen(final_norm_shift))
        outputs[slot] = narrow(normed * live)
        grad, gain_grad, shift_grad = norm_back(
            widen(cotangent[slot]) * live, (last - center) * inverse, inverse, final_gain
        )
        grads.sums("final", [gain_grad, shift_grad])

        grad = widen((yield Gathered(narrow(grad))))
        share, spread, before_low, up_sum, down_sum = feed_back(
            grad, second_kept, second_up_weight, second_down_weight
        )
        grads.weights("second_down", [(second_kept[5], spread)], spread.shape[1])
        grads.weights("second_up", [(second_kept[3], before_low)], spread.shape[1], 1)
        grads.gather("second", ["second_down", "second_up"])
        normed_grad = yield Summed(share)
        grad, gain_grad, shift_grad = residual_back(grad, normed_grad, second_kept, second_gain)
        grads.sums("second", [up_sum, down_sum, gain_grad, shift_grad])

        spread, scaled, sums, depth_gain_sum, depth_shift_sum = shape_back(
            grad, shape_kept, depth_gain, pointwise_out
        )
        share, linear_low, gating_low, depthwise_sum = convolve_back(
            scaled, sums, convolve_kept, shape_kept, pointwise_in, taps
        )
        grads.weights(
            "convolve",
            [
                (convolve_kept[3], linear_low),
                (convolve_kept[3], gating_low),
                (shape_kept[3], spread),
            ],
            linear_low.shape[1],
        )
        normed_grad = yield Summed(share)
        grad, gain_grad, shift_grad = residual_back(
            grad, normed_grad, convolve_kept, convolve_gain
        )
        grads.sums(
            "convolve_sums", [depth_gain_sum, depth_shift_sum, depthwise_sum, gain_grad, shift_grad]
        )

        share, spread, lows, query_sum, value_sum, output_sum, table_sum = attend_back(
            grad,
            attend_kept,
            query_weight,
            key_weight,
            value_weight,
            output_weight,
            table,
            table_rows,
        )
        grads.weights(
            "attend",
            [(attend_kept[7], spread)] + [(attend_kept[3], low) for low in lows],
            lows[0].shape[1],
        )
        grads.sums("attend_sums", [query_sum, value_sum, output_sum, table_sum])
        if slot == slots[-1]:
            grads.parts["final"] = [
                list(wide_sum(total([jnp.stack(part) for part in grads.parts["final"]])))
            ]
            grads.reduce_sums("early", ["final", "second", "convolve_sums", "attend_sums"])
        grads.gather("middle", ["convolve", "attend"])
        normed_grad = yield Summed(share)
        grad, gain_grad, shift_grad = residual_back(grad, normed_grad, attend_kept, attend_gain)
        grads.sums("attend_norm", [gain_grad, shift_grad])

        share, spread, before_low, up_sum, down_sum = feed_back(
            grad, first_kept, first_up_weight, first_down_weight
        )
        grads.weights("first_down", [(first_kept[5], spread)], spread.shape[1])
        grads.weights("first_up", [(first_kept[3], before_low)], spread.shape[1], 1)
        grads.gather("first_both", ["first_down", "first_up"])
        normed_grad = yield Scattered(share)
        input_grads[slot], gain_grad, shift_grad = residual_back(
            own_rows(grad),
            normed_grad,
            [own_rows(kept) for kept in first_kept[:3]],
            first_gain,
        )
        grads.sums("first", [up_sum, down_sum])
        grads.sums("first_norm", [gain_grad, shift_grad])

    flow.run([clip(slot) for slot in slots])
    grads.parts["first_norm"] = [
        list(wide_sum(total([jnp.stack(part) for part in grads.parts["first_norm"]])))
    ]
    grads.reduce_sums("late", ["attend_norm", "first", "first_norm"])
    flow.drain()

    clips = count_job.result[0][0, 0]
    early = grads.result("early")
    late = grads.result("late")
    second_down, second_up = grads.result("second")
    linear, gating, point_out, output_grad, query_grad, key_grad, value_grad = grads.result("middle")
    first_down, first_up = grads.result("first_both")
    table_grad = wide_sum(early[14]).T[: relative_table.shape[0]]
    every = (
        late[4],
        late[5],
        first_up,
        late[2],
        first_down,
        late[3],
        late[0],
        late[1],
        query_grad,
        early[11],
        key_grad,
        value_grad,
        early[12],
        output_grad,
        early[13],
        table_grad,
        early[9],
        early[10],
        jnp.stack([linear, gating]),
        early[8],
        early[6],
        early[7],
        point_out,
        early[4],
        early[5],
        second_up,
        early[2],
        second_down,
        early[3],
        early[0],
        early[1],
    )
    return (
        jnp.stack([outputs[slot] for slot in slots]),
        jnp.stack([input_grads[slot] for slot in slots]),
    ) + tuple(widen(value) / clips for value in every)


def solution(mesh):
    placed = (
        P("dp", "tensor", None),
        P("dp"),
        P(),
        P(),
        P(None, "tensor"),
        P("tensor"),
        P("tensor", None),
        P(),
        P(),
        P(),
        P(None, "tensor"),
        P("tensor"),
        P(None, "tensor"),
        P(None, "tensor"),
        P("tensor"),
        P("tensor", None),
        P(),
        P(),
        P(),
        P(),
        P(None, None, "tensor"),
        P(None, "tensor"),
        P("tensor"),
        P("tensor"),
        P("tensor", None),
        P(),
        P(),
        P(None, "tensor"),
        P("tensor"),
        P("tensor", None),
        P(),
        P(),
        P(),
        P("dp", "tensor", None),
    )
    return jax.shard_map(
        per_device,
        mesh=mesh,
        in_specs=placed,
        out_specs=(
            P("dp", "tensor", None),
            P("dp", "tensor", None),
            P(),
            P(),
            P(None, "tensor"),
            P("tensor"),
            P("tensor", None),
            P(),
            P(),
            P(),
            P(None, "tensor"),
            P("tensor"),
            P(None, "tensor"),
            P(None, "tensor"),
            P("tensor"),
            P("tensor", None),
            P(),
            P(),
            P(),
            P(),
            P(None, None, "tensor"),
            P(None, "tensor"),
            P("tensor"),
            P("tensor"),
            P("tensor", None),
            P(),
            P(),
            P(None, "tensor"),
            P("tensor"),
            P("tensor", None),
            P(),
            P(),
            P(),
        ),
        check_vma=False,
    )
```

time: 1690 us -> 852 us (0.50)
  waiting for transfers between devices: 724 us -> 343 us
  local copies, waits for them, and re-layouts: 366 us -> 55.1 us
  blocking collectives: 116 us -> 0 us
  matrix products: 258 us -> 143 us
  Pallas kernels: 0 us -> 106 us
  other arithmetic: 186 us -> 103 us
  starting transfers between devices: 3.35 us -> 74 us
    ppermute x0 -> x63, waiting for transfers between devices: none -> 313 us  [the longest x36 193 us: dp_swap(): lax.ppermute(values, 'dp', [(place, place ^ bit) for place in range(16)])]
    psum x1 -> x0, waiting for transfers between devices: 310 us -> none  [per_device(): lax.psum(first_total[2].astype(jnp.bfloat16), 'dp').astype(jnp.float32)]
    all_gather x16 -> x3, waiting for transfers between devices: 227 us -> 30.2 us  [gather_job(): whole = lax.all_gather(shards, 'dp', axis=0)]
    reduce_scatter x16 -> x0, waiting for transfers between devices: 185 us -> none  [the longest x8 129 us: sum_rows(): lax.psum_scatter(term(jnp.int32(0), count * lax.axis_size('tensor')).asty...]
    unnamed x516 -> x389, local copies, waits for them, and re-layouts: 168 us -> 34.9 us
    psum x4 -> x0, blocking collectives: 116 us -> none  [the longest x1 64.4 us: per_device(): lax.psum(first_total[3].astype(jnp.bfloat16), 'dp').astype(jnp.float32)]
    pallas_call x0 -> x8, Pallas kernels: none -> 106 us  [the longest x2 41.6 us: attend_heads_back(): pl.pallas_call(attend_back_kernel, out_shape=(jax.ShapeDtypeStruct((lengt...]
    reshape x8 -> x2, local copies, waits for them, and re-layouts: 90.6 us -> 0.01 us  [small_job(): flat = jnp.concatenate([value.reshape(-1) for value in values])]
  transfers between devices with their start and end apart: 33 -> 66, of which waited for: 27 -> 42; matrix products, arithmetic and copies ran while one was open for 27% -> 25% of each run, Pallas kernels for 0% -> 10%
where the time goes in v1:
time: 852 us; the launch traced here: 842 us
  waiting for transfers between devices  343 us (40%)
  matrix products  143 us (17%)
  Pallas kernels  106 us (12%)
  other arithmetic  103 us (12%)
  starting transfers between devices  74 us (9%)
  local copies, waits for them, and re-layouts  55.1 us (6%)
  between operations  18.8 us (2%)
    ppermute x36, waiting for transfers between devices, dp_swap(): lax.ppermute(values, 'dp', [(place, place ^ bit) for place in range(16)])  193 us
    ppermute x27, waiting for transfers between devices, swap(): return lax.ppermute(values, 'tensor', [(0, 1), (1, 0)])  120 us
    dot_general x22, matrix products, product_left(): lax.dot_general(left, right, (((0,), (0,)), ((), ())), preferred_element_...  69.3 us
    pallas_call x2, Pallas kernels, attend_heads_back(): pl.pallas_call(attend_back_kernel, out_shape=(jax.ShapeDtypeStruct((lengt...  41.6 us
    dot_general x22, matrix products, product_right(): lax.dot_general(left, right, (((1,), (1,)), ((), ())), preferred_element_...  41 us
    ppermute x36, starting transfers between devices, dp_swap(): lax.ppermute(values, 'dp', [(place, place ^ bit) for place in range(16)])  38.7 us
    unnamed x389, local copies, waits for them, and re-layouts  34.9 us
    ppermute x27, starting transfers between devices, swap(): return lax.ppermute(values, 'tensor', [(0, 1), (1, 0)])  34.5 us
  transfers between devices with their start and end apart: 66, of which 42 were waited for; matrix products, arithmetic and copies ran while one was open for 25% of the time, Pallas kernels for 10%

profile of v1, /device:TPU:0, one launch (start us, length us, event | category | flops | bytes accessed | tf_op | source)
XLA Modules:
  0.0 842.3 jit_solution(17042961037787359707)
XLA Ops:
  16.8 8.3 collective-permute-done.1
  34.2 5.5 collective-permute-done.3
  49.7 17.5 %collective-permute-done.5 = bf16[512,1024]{1,0:T(8,128)(2,1)S(1)} collective-permute-done((bf16[512,1024]{1,0:T(8,128)(2,1)S(1)}, bf16[512,1024]{1,0:T(8,128)(2,1)S(1)}, u32[]{:S(2)}, u32[]{:S(2)}) %collective-permute-start.5) | collective-permute-done | bytes 1048608 | tf_op jit(solution)/shard_map/ppermute | solution.py:70
  73.8 16.0 %attend_heads.2 = bf16[512,512]{1,0:T(8,128)(2,1)S(1)} custom-call(bf16[512,512]{1,0:T(8,128)(2,1)S(1)} %fusion.32.query_ref, bf16[512,512]{1,0:T(8,128)(2,1)S(1)} %convolution_convert_fusion.11.key_ref, bf16[512,512]{1,0:T(8,128)(2,1)S(1)} %fusion.33.value_ref, bf16[128,128]{1,0:T(8,128)(2,1)S(1)} %copy.68.table_ref), custom_call_target="tpu_custom_call" | custom-call | tf_op jit(solution)/shard_map/attend_heads/pallas_call | solution.py:506
  96.8 16.0 %attend_heads.3 = bf16[512,512]{1,0:T(8,128)(2,1)S(1)} custom-call(bf16[512,512]{1,0:T(8,128)(2,1)S(1)} %fusion.34.query_ref, bf16[512,512]{1,0:T(8,128)(2,1)S(1)} %convolution_convert_fusion.10.key_ref, bf16[512,512]{1,0:T(8,128)(2,1)S(1)} %fusion.35.value_ref, bf16[128,128]{1,0:T(8,128)(2,1)S(1)} %copy.68.table_ref), custom_call_target="tpu_custom_call" | custom-call | tf_op jit(solution)/shard_map/attend_heads/pallas_call | solution.py:506
  120.3 15.5 %mix_channels.2 = (f32[512,512]{1,0:T(8,128)S(1)}, f32[16,512]{1,0:T(8,128)S(1)}) custom-call(f32[512,512]{1,0:T(8,128)S(1)} %fusion.55.linear_ref, f32[512,512]{1,0:T(8,128)S(1)} %fusion.47.gate_ref, f32[32,512]{1,0:T(8,128)S(1)} %pad_convert_fusion.taps_ref), custom_call_target="tpu_custom_call" | custom-call | tf_op jit(solution)/shard_map/mix_channels/pallas_call | solution.py:594
  141.6 16.2 %collective-permute-done.10 = bf16[512,1024]{1,0:T(8,128)(2,1)} collective-permute-done((bf16[512,1024]{1,0:T(8,128)(2,1)S(1)}, bf16[512,1024]{1,0:T(8,128)(2,1)}, u32[]{:S(2)}, u32[]{:S(2)}) %collective-permute-start.10) | collective-permute-done | bytes 1048608 | tf_op jit(solution)/shard_map/ppermute | solution.py:70
  163.6 4.2 mix_channels.3
  171.0 18.1 %collective-permute-done.11 = f32[2,512]{1,0:T(2,128)S(1)} collective-permute-done((f32[2,512]{1,0:T(2,128)S(1)}, f32[2,512]{1,0:T(2,128)S(1)}, u32[]{:S(2)}, u32[]{:S(2)}) %collective-permute-start.11) | collective-permute-done | bytes 4128 | tf_op jit(solution)/shard_map/ppermute | solution.py:70
  200.7 13.3 %collective-permute-done.13 = bf16[512,1024]{1,0:T(8,128)(2,1)S(1)} collective-permute-done((bf16[512,1024]{1,0:T(8,128)(2,1)S(1)}, bf16[512,1024]{1,0:T(8,128)(2,1)S(1)}, u32[]{:S(2)}, u32[]{:S(2)}) %collective-permute-start.13) | collective-permute-done | bytes 1048608 | tf_op jit(solution)/shard_map/ppermute | solution.py:70
  221.6 9.4 %collective-permute-done.14 = bf16[256,1024]{1,0:T(8,128)(2,1)S(1)} collective-permute-done((bf16[256,1024]{1,0:T(8,128)(2,1)S(1)}, bf16[256,1024]{1,0:T(8,128)(2,1)S(1)}, u32[]{:S(2)}, u32[]{:S(2)}) %collective-permute-start.14) | collective-permute-done | bytes 524320 | tf_op jit(solution)/shard_map/ppermute | solution.py:70
  235.4 10.7 %collective-permute-done.15 = bf16[256,1024]{1,0:T(8,128)(2,1)S(1)} collective-permute-done((bf16[256,1024]{1,0:T(8,128)(2,1)S(1)}, bf16[256,1024]{1,0:T(8,128)(2,1)S(1)}, u32[]{:S(2)}, u32[]{:S(2)}) %collective-permute-start.15) | collective-permute-done | bytes 524320 | tf_op jit(solution)/shard_map/ppermute | solution.py:70
  250.6 5.8 collective-permute-done.35
  262.0 6.0 fusion.75
  272.1 5.9 fusion.66
  279.8 5.9 fusion.150
  289.9 7.5 add_convert_fusion.3
  298.0 6.7 add_convert_fusion.2
  313.5 6.0 mix_channels_back.2
  326.5 4.4 collective-permute-done.20
  350.5 6.4 mix_channels_back.3
  374.7 16.9 %collective-permute-done.24 = bf16[2,2,128,1024]{3,2,1,0:T(8,128)(2,1)S(1)} collective-permute-done((bf16[2,2,128,1024]{3,2,1,0:T(8,128)(2,1)S(1)}, bf16[2,2,128,1024]{3,2,1,0:T(8,128)(2,1)S(1)}, u32[]{:S(2)}, u32[]{:S(2)}) %collective-permute-start.24) | collective-permute-done | bytes 1048608 | tf_op jit(solution)/shard_map/ppermute | solution.py:230
  398.9 20.9 %attend_heads_back.2 = (bf16[512,512]{1,0:T(8,128)(2,1)S(1)}, bf16[512,512]{1,0:T(8,128)(2,1)S(1)}, bf16[512,512]{1,0:T(8,128)(2,1)S(1)}, f32[1,512]{1,0:T(1,128...) custom-call(bf16[512,512]{1,0:T(8,128)(2,1)S(1)} %copy-done.17, bf16[512,512]{1,0:T(8,128)(2,1)S(1)} %copy-done.15, ...), custom_call_target="tpu_custom_call" | custom-call | tf_op jit(solution)/shard_map/attend_heads_back/pallas_call | solution.py:520
  426.1 7.1 collective-permute-done.26
  438.4 7.3 collective-permute-done.27
  454.8 20.7 %attend_heads_back.3 = (bf16[512,512]{1,0:T(8,128)(2,1)S(1)}, bf16[512,512]{1,0:T(8,128)(2,1)S(1)}, bf16[512,512]{1,0:T(8,128)(2,1)S(1)}, f32[1,512]{1,0:T(1,128...) custom-call(bf16[512,512]{1,0:T(8,128)(2,1)S(1)} %copy-done.11, bf16[512,512]{1,0:T(8,128)(2,1)S(1)} %copy-done.9, ...), custom_call_target="tpu_custom_call" | custom-call | tf_op jit(solution)/shard_map/attend_heads_back/pallas_call | solution.py:520
  490.8 10.3 %collective-permute-done.32 = bf16[128,1024]{1,0:T(8,128)(2,1)S(1)} collective-permute-done((bf16[128,1024]{1,0:T(8,128)(2,1)S(1)}, bf16[128,1024]{1,0:T(8,128)(2,1)S(1)}, u32[]{:S(2)}, u32[]{:S(2)}) %collective-permute-start.32) | collective-permute-done | bytes 262176 | tf_op jit(solution)/shard_map/ppermute | solution.py:230
  531.9 9.5 %collective-permute-done.38 = bf16[2,192,512]{2,1,0:T(8,128)(2,1)S(1)} collective-permute-done((bf16[2,192,512]{2,1,0:T(8,128)(2,1)S(1)}, bf16[2,192,512]{2,1,0:T(8,128)(2,1)S(1)}, u32[]{:S(2)}, u32[]{:S(2)}) %collective-permute-start.38) | collective-permute-done | bytes 393248 | tf_op jit(solution)/shard_map/ppermute | solution.py:230
  542.1 6.6 fusion.60
  548.8 13.4 %collective-permute-done.39 = bf16[192,512]{1,0:T(8,128)(2,1)S(1)} collective-permute-done((bf16[192,512]{1,0:T(8,128)(2,1)S(1)}, bf16[192,512]{1,0:T(8,128)(2,1)S(1)}, u32[]{:S(2)}, u32[]{:S(2)}) %collective-permute-start.39) | collective-permute-done | bytes 196640 | tf_op jit(solution)/shard_map/ppermute | solution.py:230
  562.8 5.9 fusion.104
  581.4 8.9 %collective-permute-done.44 = f32[36352]{0:T(1024)S(1)} collective-permute-done((f32[36352]{0:T(1024)S(1)}, f32[36352]{0:T(1024)S(1)}, u32[]{:S(2)}, u32[]{:S(2)}) %collective-permute-start.44) | collective-permute-done | bytes 145440 | tf_op jit(solution)/shard_map/ppermute | solution.py:230
  591.6 5.6 collective-permute-done.43
  598.4 8.7 %add_convert_fusion.1 = bf16[2048,1024]{1,0:T(8,128)(2,1)} fusion(f32[2048,1024]{1,0:T(8,128)} %fusion.104, f32[512,1024]{1,0:T(8,128)S(1)} %get-tuple-element.306, f32[512,2048]{1,0:T(8,128)S(1)} %copy-done.182, f32[2048]{0:T(1024)S(1)} %copy-done.142), kind=kOutput, calls=%fused_computation.5 | convolution fusion | flops 2159017984 | bytes 18882560 | tf_op jit(solution)/shard_map/dot_general | solution.py:25
  615.3 4.9 add_convert_fusion
  620.4 12.4 %collective-permute-done.48 = f32[36352]{0:T(1024)S(1)} collective-permute-done((f32[36352]{0:T(1024)S(1)}, f32[36352]{0:T(1024)S(1)}, u32[]{:S(2)}, u32[]{:S(2)}) %collective-permute-start.48) | collective-permute-done | bytes 145440 | tf_op jit(solution)/shard_map/ppermute | solution.py:230
  651.7 26.9 %collective-permute-done.51 = bf16[2,2,128,1024]{3,2,1,0:T(8,128)(2,1)S(1)} collective-permute-done((bf16[2,2,128,1024]{3,2,1,0:T(8,128)(2,1)S(1)}, bf16[2,2,128,1024]{3,2,1,0:T(8,128)(2,1)S(1)}, u32[]{:S(2)}, u32[]{:S(2)}) %collective-permute-start.51) | collective-permute-done | bytes 1048608 | tf_op jit(solution)/shard_map/ppermute | solution.py:230
  681.4 14.8 %collective-permute-done.53 = bf16[2,128,1024]{2,1,0:T(8,128)(2,1)S(1)} collective-permute-done((bf16[2,128,1024]{2,1,0:T(8,128)(2,1)S(1)}, bf16[2,128,1024]{2,1,0:T(8,128)(2,1)S(1)}, u32[]{:S(2)}, u32[]{:S(2)}) %collective-permute-start.53) | collective-permute-done | bytes 524320 | tf_op jit(solution)/shard_map/ppermute | solution.py:230
  700.9 13.7 %collective-permute-done.56 = bf16[2,2,128,1024]{3,2,0,1:T(8,128)(2,1)S(1)} collective-permute-done((bf16[2,2,128,1024]{3,2,0,1:T(8,128)(2,1)S(1)}, bf16[2,2,128,1024]{3,2,0,1:T(8,128)(2,1)S(1)}, u32[]{:S(2)}, u32[]{:S(2)}) %collective-permute-start.56) | collective-permute-done | bytes 1048608 | tf_op jit(solution)/shard_map/ppermute | solution.py:230
  714.9 4.9 collective-permute-done.54
  720.4 13.9 %collective-permute-done.58 = bf16[2,128,1024]{2,1,0:T(8,128)(2,1)S(1)} collective-permute-done((bf16[2,128,1024]{2,1,0:T(8,128)(2,1)S(1)}, bf16[2,128,1024]{2,1,0:T(8,128)(2,1)S(1)}, u32[]{:S(2)}, u32[]{:S(2)}) %collective-permute-start.58) | collective-permute-done | bytes 524320 | tf_op jit(solution)/shard_map/ppermute | solution.py:230
  735.1 5.5 collective-permute-done.60
  740.6 8.1 collective-permute-done.59
  761.3 5.7 collective-permute-done.61
  771.1 4.3 convert_divide_fusion.1
  775.4 4.6 convert_divide_fusion
  791.7 30.2 %all-gather.7.cloned.1.call-done = bf16[4096,1024]{1,0:T(8,128)(2,1)} async-done(((bf16[256,1024]{1,0:T(8,128)(2,1)}), bf16[4096,1024]{1,0:T(8,128)(2,1)}) %all-gather.7.cloned.1.call-update) | async-done | bytes 8388624 | tf_op jit(solution)/shard_map/all_gather | solution.py:288
  826.6 4.6 convert_divide_fusion.2
  (822 shorter events, 321.8 us)
Async XLA Ops:
  7.4 760.9 %all-gather.11.cloned.1.call-start = ((), (), s32[]{:S(2)}) async-start(), calls=%async_computation.2 | async-start | bytes 8912896 | tf_op jit(solution)/shard_map/all_gather | solution.py:288
  9.9 15.2 %collective-permute-start.1 = (bf16[256,1024]{1,0:T(8,128)(2,1)S(1)}, bf16[256,1024]{1,0:T(8,128)(2,1)S(1)}, u32[]{:S(2)}, u32[]{:S(2)}) collective-permute-start(bf16[256,1024]{1,0:T(8,128)(2,1)S(1)} %get-tuple-element.147), channel_id=1, source_target_pairs={{0,1},{1,0},{2,3},{3,2},{4,5},{5,4},{6,7},{7,6},{8,9},{9,8},{10,11... | collective-permute-start | bytes 1572872 | tf_op jit(solution)/shard_map/ppermute | solution.py:70
  25.9 13.8 %collective-permute-start.3 = (bf16[256,1024]{1,0:T(8,128)(2,1)S(1)}, bf16[256,1024]{1,0:T(8,128)(2,1)S(1)}, u32[]{:S(2)}, u32[]{:S(2)}) collective-permute-start(bf16[256,1024]{1,0:T(8,128)(2,1)S(1)} %get-tuple-element.151), channel_id=1, source_target_pairs={{0,1},{1,0},{2,3},{3,2},{4,5},{5,4},{6,7},{7,6},{8,9},{9,8},{10,11... | collective-permute-start | bytes 1572872 | tf_op jit(solution)/shard_map/ppermute | solution.py:70
  43.0 24.2 %collective-permute-start.5 = (bf16[512,1024]{1,0:T(8,128)(2,1)S(1)}, bf16[512,1024]{1,0:T(8,128)(2,1)S(1)}, u32[]{:S(2)}, u32[]{:S(2)}) collective-permute-start(bf16[512,1024]{1,0:T(8,128)(2,1)S(1)} %convolution_convert_fusion.7), channel_id=1, source_target_pairs={{0,1},{1,0},{2,3},{3,2},{4,5},{5,4},{6,7},{7,6},{8,9},{9,8},{10,11... | collective-permute-start | bytes 3145736 | tf_op jit(solution)/shard_map/ppermute | solution.py:70
  68.2 23.3 %collective-permute-start.7 = (bf16[512,1024]{1,0:T(8,128)(2,1)S(1)}, bf16[512,1024]{1,0:T(8,128)(2,1)S(1)}, u32[]{:S(2)}, u32[]{:S(2)}) collective-permute-start(bf16[512,1024]{1,0:T(8,128)(2,1)S(1)} %convolution_convert_fusion.6), channel_id=1, source_target_pairs={{0,1},{1,0},{2,3},{3,2},{4,5},{5,4},{6,7},{7,6},{8,9},{9,8},{10,11... | collective-permute-start | bytes 3145736 | tf_op jit(solution)/shard_map/ppermute | solution.py:70
  93.5 22.3 %collective-permute-start.8 = (bf16[512,1024]{1,0:T(8,128)(2,1)S(1)}, bf16[512,1024]{1,0:T(8,128)(2,1)S(1)}, u32[]{:S(2)}, u32[]{:S(2)}) collective-permute-start(bf16[512,1024]{1,0:T(8,128)(2,1)S(1)} %convolution_convert_fusion.3), channel_id=1, source_target_pairs={{0,1},{1,0},{2,3},{3,2},{4,5},{5,4},{6,7},{7,6},{8,9},{9,8},{10,11... | collective-permute-start | bytes 3145736 | tf_op jit(solution)/shard_map/ppermute | solution.py:70
  136.8 21.0 %collective-permute-start.10 = (bf16[512,1024]{1,0:T(8,128)(2,1)S(1)}, bf16[512,1024]{1,0:T(8,128)(2,1)}, u32[]{:S(2)}, u32[]{:S(2)}) collective-permute-start(bf16[512,1024]{1,0:T(8,128)(2,1)S(1)} %convolution_convert_fusion.2), channel_id=1, source_target_pairs={{0,1},{1,0},{2,3},{3,2},{4,5},{5,4},{6,7},{7,6},{8,9},{9,8},{10,11... | collective-permute-start | bytes 3145736 | tf_op jit(solution)/shard_map/ppermute | solution.py:70
  168.8 22.7 %collective-permute-start.12 = (bf16[512,1024]{1,0:T(8,128)(2,1)}, bf16[512,1024]{1,0:T(8,128)(2,1)}, u32[]{:S(2)}, u32[]{:S(2)}) collective-permute-start(bf16[512,1024]{1,0:T(8,128)(2,1)} %convolution_convert_fusion.1), channel_id=1, source_target_pairs={{0,1},{1,0},{2,3},{3,2},{4,5},{5,4},{6,7},{7,6},{8,9},{9,8},{10,11... | collective-permute-start | bytes 3145736 | tf_op jit(solution)/shard_map/ppermute | solution.py:70
  170.2 18.9 %collective-permute-start.11 = (f32[2,512]{1,0:T(2,128)S(1)}, f32[2,512]{1,0:T(2,128)S(1)}, u32[]{:S(2)}, u32[]{:S(2)}) collective-permute-start(f32[2,512]{1,0:T(2,128)S(1)} %pad_maximum_fusion.14), channel_id=1, source_target_pairs={{0,1},{1,0},{2,3},{3,2},{4,5},{5,4},{6,7},{7,6},{8,9},{9,8},{10,11... | collective-permute-start | bytes 12296 | tf_op jit(solution)/shard_map/ppermute | solution.py:70
  194.0 20.0 %collective-permute-start.13 = (bf16[512,1024]{1,0:T(8,128)(2,1)S(1)}, bf16[512,1024]{1,0:T(8,128)(2,1)S(1)}, u32[]{:S(2)}, u32[]{:S(2)}) collective-permute-start(bf16[512,1024]{1,0:T(8,128)(2,1)S(1)} %convolution_convert_fusion), channel_id=1, source_target_pairs={{0,1},{1,0},{2,3},{3,2},{4,5},{5,4},{6,7},{7,6},{8,9},{9,8},{10,11... | collective-permute-start | bytes 3145736 | tf_op jit(solution)/shard_map/ppermute | solution.py:70
  217.3 13.8 %collective-permute-start.14 = (bf16[256,1024]{1,0:T(8,128)(2,1)S(1)}, bf16[256,1024]{1,0:T(8,128)(2,1)S(1)}, u32[]{:S(2)}, u32[]{:S(2)}) collective-permute-start(bf16[256,1024]{1,0:T(8,128)(2,1)S(1)} %dynamic-slice_convert_fusion.3), channel_id=1, source_target_pairs={{0,1},{1,0},{2,3},{3,2},{4,5},{5,4},{6,7},{7,6},{8,9},{9,8},{10,11... | collective-permute-start | bytes 1572872 | tf_op jit(solution)/shard_map/ppermute | solution.py:70
  231.6 14.5 %collective-permute-start.15 = (bf16[256,1024]{1,0:T(8,128)(2,1)S(1)}, bf16[256,1024]{1,0:T(8,128)(2,1)S(1)}, u32[]{:S(2)}, u32[]{:S(2)}) collective-permute-start(bf16[256,1024]{1,0:T(8,128)(2,1)S(1)} %dynamic-slice_convert_fusion.2), channel_id=1, source_target_pairs={{0,1},{1,0},{2,3},{3,2},{4,5},{5,4},{6,7},{7,6},{8,9},{9,8},{10,11... | collective-permute-start | bytes 1572872 | tf_op jit(solution)/shard_map/ppermute | solution.py:70
  288.1 17.0 %collective-permute-start.18 = (bf16[512,1024]{1,0:T(8,128)(2,1)S(1)}, bf16[512,1024]{1,0:T(8,128)(2,1)S(1)}, u32[]{:S(2)}, u32[]{:S(2)}) collective-permute-start(bf16[512,1024]{1,0:T(8,128)(2,1)S(1)} %convolution_convert_fusion.5), channel_id=1, source_target_pairs={{0,1},{1,0},{2,3},{3,2},{4,5},{5,4},{6,7},{7,6},{8,9},{9,8},{10,11... | collective-permute-start | bytes 3145736 | tf_op jit(solution)/shard_map/ppermute | solution.py:70
  312.0 19.0 %collective-permute-start.20 = (bf16[512,1024]{1,0:T(8,128)(2,1)S(1)}, bf16[512,1024]{1,0:T(8,128)(2,1)S(1)}, u32[]{:S(2)}, u32[]{:S(2)}) collective-permute-start(bf16[512,1024]{1,0:T(8,128)(2,1)S(1)} %convolution_convert_fusion.4), channel_id=1, source_target_pairs={{0,1},{1,0},{2,3},{3,2},{4,5},{5,4},{6,7},{7,6},{8,9},{9,8},{10,11... | collective-permute-start | bytes 3145736 | tf_op jit(solution)/shard_map/ppermute | solution.py:70
  334.9 15.2 %collective-permute-start.21 = (f32[2,512]{1,0:T(2,128)S(1)}, f32[2,512]{1,0:T(2,128)S(1)}, u32[]{:S(2)}, u32[]{:S(2)}) collective-permute-start(f32[2,512]{1,0:T(2,128)S(1)} %pad_maximum_fusion.16), channel_id=1, source_target_pairs={{0,1},{1,0},{2,3},{3,2},{4,5},{5,4},{6,7},{7,6},{8,9},{9,8},{10,11... | collective-permute-start | bytes 12296 | tf_op jit(solution)/shard_map/ppermute | solution.py:70
  335.4 39.2 %collective-permute-start.22 = (bf16[512,1024]{1,0:T(8,128)(2,1)}, bf16[512,1024]{1,0:T(8,128)(2,1)}, u32[]{:S(2)}, u32[]{:S(2)}) collective-permute-start(bf16[512,1024]{1,0:T(8,128)(2,1)} %add_convert_fusion.18), channel_id=1, source_target_pairs={{0,1},{1,0},{2,3},{3,2},{4,5},{5,4},{6,7},{7,6},{8,9},{9,8},{10,11... | collective-permute-start | bytes 3145736 | tf_op jit(solution)/shard_map/ppermute | solution.py:70
  338.5 22.9 %collective-permute-start.23 = (bf16[2,2,2,128,1024]{4,3,2,1,0:T(8,128)(2,1)}, bf16[2,2,2,128,1024]{4,3,2,1,0:T(8,128)(2,1)}, u32[]{:S(2)}, u32[]{:S(2)}) collective-permute-start(bf16[2,2,2,128,1024]{4,3,2,1,0:T(8,128)(2,1)} %dynamic-slice_bitcast_fusion.1), channel_id=1, source_target_pairs={{0,2},{2,0},{4,6},{6,4},{8,10},{10,8},{12,14},{14,12},{16,18},{18,... | collective-permute-start | bytes 6291464 | tf_op jit(solution)/shard_map/ppermute | solution.py:230
  341.2 28.4 %collective-permute-start.28 = (bf16[2,2,2,128,1024]{4,3,0,1,2:T(8,128)(2,1)}, bf16[2,2,2,128,1024]{4,3,0,1,2:T(8,128)(2,1)}, u32[]{:S(2)}, u32[]{:S(2)}) collective-permute-start(bf16[2,2,2,128,1024]{4,3,0,1,2:T(8,128)(2,1)} %pad_maximum_fusion), channel_id=1, source_target_pairs={{0,2},{2,0},{4,6},{6,4},{8,10},{10,8},{12,14},{14,12},{16,18},{18,... | collective-permute-start | bytes 6291464 | tf_op jit(solution)/shard_map/ppermute | solution.py:230
  365.5 26.1 %collective-permute-start.24 = (bf16[2,2,128,1024]{3,2,1,0:T(8,128)(2,1)S(1)}, bf16[2,2,128,1024]{3,2,1,0:T(8,128)(2,1)S(1)}, u32[]{:S(2)}, u32[]{:S(2)}) collective-permute-start(bf16[2,2,128,1024]{3,2,1,0:T(8,128)(2,1)S(1)} %dynamic-slice_bitcast_fusion.6), channel_id=1, source_target_pairs={{0,4},{2,6},{4,0},{6,2},{8,12},{10,14},{12,8},{14,10},{16,20},{18,... | collective-permute-start | bytes 3145736 | tf_op jit(solution)/shard_map/ppermute | solution.py:230
  373.2 65.2 %collective-permute-start.29 = (bf16[2,2,128,1024]{3,2,0,1:T(8,128)(2,1)S(1)}, bf16[2,2,128,1024]{3,2,0,1:T(8,128)(2,1)S(1)}, u32[]{:S(2)}, u32[]{:S(2)}) collective-permute-start(bf16[2,2,128,1024]{3,2,0,1:T(8,128)(2,1)S(1)} %dynamic-slice_bitcast_fusion.5), channel_id=1, source_target_pairs={{0,4},{2,6},{4,0},{6,2},{8,12},{10,14},{12,8},{14,10},{16,20},{18,... | collective-permute-start | bytes 3145736 | tf_op jit(solution)/shard_map/ppermute | solution.py:230
  421.0 12.2 %collective-permute-start.26 = (bf16[2,128,1024]{2,1,0:T(8,128)(2,1)S(1)}, bf16[2,128,1024]{2,1,0:T(8,128)(2,1)S(1)}, u32[]{:S(2)}, u32[]{:S(2)}) collective-permute-start(bf16[2,128,1024]{2,1,0:T(8,128)(2,1)S(1)} %dynamic-slice_bitcast_fusion.16), channel_id=1, source_target_pairs={{0,8},{2,10},{4,12},{6,14},{8,0},{10,2},{12,4},{14,6},{16,24},{18,... | collective-permute-start | bytes 1572872 | tf_op jit(solution)/shard_map/ppermute | solution.py:230
  423.6 23.1 %collective-permute-start.25 = (bf16[512,1024]{1,0:T(8,128)(2,1)S(1)}, bf16[512,1024]{1,0:T(8,128)(2,1)S(1)}, u32[]{:S(2)}, u32[]{:S(2)}) collective-permute-start(bf16[512,1024]{1,0:T(8,128)(2,1)S(1)} %add_convert_fusion.17), channel_id=1, source_target_pairs={{0,1},{1,0},{2,3},{3,2},{4,5},{5,4},{6,7},{7,6},{8,9},{9,8},{10,11... | collective-permute-start | bytes 3145736 | tf_op jit(solution)/shard_map/ppermute | solution.py:70
  433.5 12.2 %collective-permute-start.27 = (bf16[128,1024]{1,0:T(8,128)(2,1)S(1)}, bf16[128,1024]{1,0:T(8,128)(2,1)S(1)}, u32[]{:S(2)}, u32[]{:S(2)}) collective-permute-start(bf16[128,1024]{1,0:T(8,128)(2,1)S(1)} %dynamic-slice_bitcast_fusion.26), channel_id=1, source_target_pairs={{0,16},{2,18},{4,20},{6,22},{8,24},{10,26},{12,28},{14,30},{16,0},... | collective-permute-start | bytes 786440 | tf_op jit(solution)/shard_map/ppermute | solution.py:230
  449.6 51.5 %collective-permute-start.30 = (bf16[512,1024]{1,0:T(8,128)(2,1)S(1)}, bf16[512,1024]{1,0:T(8,128)(2,1)S(1)}, u32[]{:S(2)}, u32[]{:S(2)}) collective-permute-start(bf16[512,1024]{1,0:T(8,128)(2,1)S(1)} %add_convert_fusion.16), channel_id=1, source_target_pairs={{0,1},{1,0},{2,3},{3,2},{4,5},{5,4},{6,7},{7,6},{8,9},{9,8},{10,11... | collective-permute-start | bytes 3145736 | tf_op jit(solution)/shard_map/ppermute | solution.py:70
  451.7 34.5 %collective-permute-start.31 = (bf16[2,128,1024]{2,1,0:T(8,128)(2,1)S(1)}, bf16[2,128,1024]{2,1,0:T(8,128)(2,1)S(1)}, u32[]{:S(2)}, u32[]{:S(2)}) collective-permute-start(bf16[2,128,1024]{2,1,0:T(8,128)(2,1)S(1)} %dynamic-slice_bitcast_fusion.15), channel_id=1, source_target_pairs={{0,8},{2,10},{4,12},{6,14},{8,0},{10,2},{12,4},{14,6},{16,24},{18,... | collective-permute-start | bytes 1572872 | tf_op jit(solution)/shard_map/ppermute | solution.py:230
  453.3 30.7 %collective-permute-start.33 = (bf16[2,2,2,192,512]{4,3,2,1,0:T(8,128)(2,1)S(1)}, bf16[2,2,2,192,512]{4,3,2,1,0:T(8,128)(2,1)S(1)}, u32[]{:S(2)}, u32[]{:S(2)}) collective-permute-start(bf16[2,2,2,192,512]{4,3,2,1,0:T(8,128)(2,1)S(1)} %pad_maximum_fusion.3), channel_id=1, source_target_pairs={{0,2},{2,0},{4,6},{6,4},{8,10},{10,8},{12,14},{14,12},{16,18},{18,... | collective-permute-start | bytes 4718600 | tf_op jit(solution)/shard_map/ppermute | solution.py:230
  484.5 19.6 %collective-permute-start.34 = (bf16[2,2,192,512]{3,2,1,0:T(8,128)(2,1)S(1)}, bf16[2,2,192,512]{3,2,1,0:T(8,128)(2,1)S(1)}, u32[]{:S(2)}, u32[]{:S(2)}) collective-permute-start(bf16[2,2,192,512]{3,2,1,0:T(8,128)(2,1)S(1)} %dynamic-slice_bitcast_fusion.7), channel_id=1, source_target_pairs={{0,4},{2,6},{4,0},{6,2},{8,12},{10,14},{12,8},{14,10},{16,20},{18,... | collective-permute-start | bytes 2359304 | tf_op jit(solution)/shard_map/ppermute | solution.py:230
  486.5 14.6 %collective-permute-start.32 = (bf16[128,1024]{1,0:T(8,128)(2,1)S(1)}, bf16[128,1024]{1,0:T(8,128)(2,1)S(1)}, u32[]{:S(2)}, u32[]{:S(2)}) collective-permute-start(bf16[128,1024]{1,0:T(8,128)(2,1)S(1)} %dynamic-slice_bitcast_fusion.25), channel_id=1, source_target_pairs={{0,16},{2,18},{4,20},{6,22},{8,24},{10,26},{12,28},{14,30},{16,0},... | collective-permute-start | bytes 786440 | tf_op jit(solution)/shard_map/ppermute | solution.py:230
  505.1 275.0 %all-gather.9.cloned.1.call-start = ((), (), s32[]{:S(2)}) async-start(), calls=%async_computation.1 | async-start | bytes 7798784 | tf_op jit(solution)/shard_map/all_gather | solution.py:288
  516.0 46.3 %collective-permute-start.37 = (bf16[512,1024]{1,0:T(8,128)(2,1)S(1)}, bf16[512,1024]{1,0:T(8,128)(2,1)S(1)}, u32[]{:S(2)}, u32[]{:S(2)}) collective-permute-start(bf16[512,1024]{1,0:T(8,128)(2,1)S(1)} %copy-done.64), channel_id=1, source_target_pairs={{0,1},{1,0},{2,3},{3,2},{4,5},{5,4},{6,7},{7,6},{8,9},{9,8},{10,11... | collective-permute-start | bytes 3145736 | tf_op jit(solution)/shard_map/ppermute | solution.py:70
  516.8 24.6 %collective-permute-start.38 = (bf16[2,192,512]{2,1,0:T(8,128)(2,1)S(1)}, bf16[2,192,512]{2,1,0:T(8,128)(2,1)S(1)}, u32[]{:S(2)}, u32[]{:S(2)}) collective-permute-start(bf16[2,192,512]{2,1,0:T(8,128)(2,1)S(1)} %dynamic-slice_bitcast_fusion.17), channel_id=1, source_target_pairs={{0,8},{2,10},{4,12},{6,14},{8,0},{10,2},{12,4},{14,6},{16,24},{18,... | collective-permute-start | bytes 1179656 | tf_op jit(solution)/shard_map/ppermute | solution.py:230
  530.3 18.5 %collective-permute-start.40 = (f32[36352]{0:T(1024)S(1)}, f32[36352]{0:T(1024)S(1)}, u32[]{:S(2)}, u32[]{:S(2)}) collective-permute-start(f32[36352]{0:T(1024)S(1)} %add.980), channel_id=1, source_target_pairs={{0,4},{2,6},{4,0},{6,2},{8,12},{10,14},{12,8},{14,10},{16,20},{18,... | collective-permute-start | bytes 436232 | tf_op jit(solution)/shard_map/ppermute | solution.py:230
  541.6 20.7 %collective-permute-start.39 = (bf16[192,512]{1,0:T(8,128)(2,1)S(1)}, bf16[192,512]{1,0:T(8,128)(2,1)S(1)}, u32[]{:S(2)}, u32[]{:S(2)}) collective-permute-start(bf16[192,512]{1,0:T(8,128)(2,1)S(1)} %dynamic-slice_bitcast_fusion.27), channel_id=1, source_target_pairs={{0,16},{2,18},{4,20},{6,22},{8,24},{10,26},{12,28},{14,30},{16,0},... | collective-permute-start | bytes 589832 | tf_op jit(solution)/shard_map/ppermute | solution.py:230
  571.6 25.6 %collective-permute-start.43 = (bf16[2,2,256,512]{3,2,1,0:T(8,128)(2,1)S(1)}, bf16[2,2,256,512]{3,2,1,0:T(8,128)(2,1)S(1)}, u32[]{:S(2)}, u32[]{:S(2)}) collective-permute-start(bf16[2,2,256,512]{3,2,1,0:T(8,128)(2,1)S(1)} %dynamic-slice_bitcast_fusion.4), channel_id=1, source_target_pairs={{0,4},{2,6},{4,0},{6,2},{8,12},{10,14},{12,8},{14,10},{16,20},{18,... | collective-permute-start | bytes 3145736 | tf_op jit(solution)/shard_map/ppermute | solution.py:230
  577.3 14.3 %collective-permute-start.41 = (bf16[256,1024]{1,0:T(8,128)(2,1)S(1)}, bf16[256,1024]{1,0:T(8,128)(2,1)S(1)}, u32[]{:S(2)}, u32[]{:S(2)}) collective-permute-start(bf16[256,1024]{1,0:T(8,128)(2,1)S(1)} %dynamic-slice_convert_fusion.1), channel_id=1, source_target_pairs={{0,1},{1,0},{2,3},{3,2},{4,5},{5,4},{6,7},{7,6},{8,9},{9,8},{10,11... | collective-permute-start | bytes 1572872 | tf_op jit(solution)/shard_map/ppermute | solution.py:70
  578.7 11.7 %collective-permute-start.44 = (f32[36352]{0:T(1024)S(1)}, f32[36352]{0:T(1024)S(1)}, u32[]{:S(2)}, u32[]{:S(2)}) collective-permute-start(f32[36352]{0:T(1024)S(1)} %add.985), channel_id=1, source_target_pairs={{0,8},{2,10},{4,12},{6,14},{8,0},{10,2},{12,4},{14,6},{16,24},{18,... | collective-permute-start | bytes 436232 | tf_op jit(solution)/shard_map/ppermute | solution.py:230
  597.6 13.6 %collective-permute-start.46 = (bf16[2,256,512]{2,1,0:T(8,128)(2,1)S(1)}, bf16[2,256,512]{2,1,0:T(8,128)(2,1)S(1)}, u32[]{:S(2)}, u32[]{:S(2)}) collective-permute-start(bf16[2,256,512]{2,1,0:T(8,128)(2,1)S(1)} %dynamic-slice_bitcast_fusion.10), channel_id=1, source_target_pairs={{0,8},{2,10},{4,12},{6,14},{8,0},{10,2},{12,4},{14,6},{16,24},{18,... | collective-permute-start | bytes 1572872 | tf_op jit(solution)/shard_map/ppermute | solution.py:230
  607.1 25.8 %collective-permute-start.45 = (bf16[256,1024]{1,0:T(8,128)(2,1)S(1)}, bf16[256,1024]{1,0:T(8,128)(2,1)S(1)}, u32[]{:S(2)}, u32[]{:S(2)}) collective-permute-start(bf16[256,1024]{1,0:T(8,128)(2,1)S(1)} %dynamic-slice_convert_fusion), channel_id=1, source_target_pairs={{0,1},{1,0},{2,3},{3,2},{4,5},{5,4},{6,7},{7,6},{8,9},{9,8},{10,11... | collective-permute-start | bytes 1572872 | tf_op jit(solution)/shard_map/ppermute | solution.py:70
  611.4 21.5 %collective-permute-start.47 = (bf16[256,512]{1,0:T(8,128)(2,1)S(1)}, bf16[256,512]{1,0:T(8,128)(2,1)S(1)}, u32[]{:S(2)}, u32[]{:S(2)}) collective-permute-start(bf16[256,512]{1,0:T(8,128)(2,1)S(1)} %dynamic-slice_bitcast_fusion.20), channel_id=1, source_target_pairs={{0,16},{2,18},{4,20},{6,22},{8,24},{10,26},{12,28},{14,30},{16,0},... | collective-permute-start | bytes 786440 | tf_op jit(solution)/shard_map/ppermute | solution.py:230
  620.2 12.6 %collective-permute-start.48 = (f32[36352]{0:T(1024)S(1)}, f32[36352]{0:T(1024)S(1)}, u32[]{:S(2)}, u32[]{:S(2)}) collective-permute-start(f32[36352]{0:T(1024)S(1)} %add.990), channel_id=1, source_target_pairs={{0,16},{2,18},{4,20},{6,22},{8,24},{10,26},{12,28},{14,30},{16,0},... | collective-permute-start | bytes 436232 | tf_op jit(solution)/shard_map/ppermute | solution.py:230
  634.5 187.5 %all-gather.7.cloned.1.call-start = ((), (), s32[]{:S(2)}) async-start(), calls=%async_computation | async-start | bytes 8912896 | tf_op jit(solution)/shard_map/all_gather | solution.py:288
  648.1 30.5 %collective-permute-start.51 = (bf16[2,2,128,1024]{3,2,1,0:T(8,128)(2,1)S(1)}, bf16[2,2,128,1024]{3,2,1,0:T(8,128)(2,1)S(1)}, u32[]{:S(2)}, u32[]{:S(2)}) collective-permute-start(bf16[2,2,128,1024]{3,2,1,0:T(8,128)(2,1)S(1)} %dynamic-slice_bitcast_fusion.3), channel_id=1, source_target_pairs={{0,4},{2,6},{4,0},{6,2},{8,12},{10,14},{12,8},{14,10},{16,20},{18,... | collective-permute-start | bytes 3145736 | tf_op jit(solution)/shard_map/ppermute | solution.py:230
  679.0 17.2 %collective-permute-start.53 = (bf16[2,128,1024]{2,1,0:T(8,128)(2,1)S(1)}, bf16[2,128,1024]{2,1,0:T(8,128)(2,1)S(1)}, u32[]{:S(2)}, u32[]{:S(2)}) collective-permute-start(bf16[2,128,1024]{2,1,0:T(8,128)(2,1)S(1)} %dynamic-slice_bitcast_fusion.9), channel_id=1, source_target_pairs={{0,8},{2,10},{4,12},{6,14},{8,0},{10,2},{12,4},{14,6},{16,24},{18,... | collective-permute-start | bytes 1572872 | tf_op jit(solution)/shard_map/ppermute | solution.py:230
  680.0 34.6 %collective-permute-start.56 = (bf16[2,2,128,1024]{3,2,0,1:T(8,128)(2,1)S(1)}, bf16[2,2,128,1024]{3,2,0,1:T(8,128)(2,1)S(1)}, u32[]{:S(2)}, u32[]{:S(2)}) collective-permute-start(bf16[2,2,128,1024]{3,2,0,1:T(8,128)(2,1)S(1)} %dynamic-slice_bitcast_fusion.2), channel_id=1, source_target_pairs={{0,4},{2,6},{4,0},{6,2},{8,12},{10,14},{12,8},{14,10},{16,20},{18,... | collective-permute-start | bytes 3145736 | tf_op jit(solution)/shard_map/ppermute | solution.py:230
  696.5 23.4 %collective-permute-start.54 = (bf16[128,1024]{1,0:T(8,128)(2,1)S(1)}, bf16[128,1024]{1,0:T(8,128)(2,1)S(1)}, u32[]{:S(2)}, u32[]{:S(2)}) collective-permute-start(bf16[128,1024]{1,0:T(8,128)(2,1)S(1)} %dynamic-slice_bitcast_fusion.19), channel_id=1, source_target_pairs={{0,16},{2,18},{4,20},{6,22},{8,24},{10,26},{12,28},{14,30},{16,0},... | collective-permute-start | bytes 786440 | tf_op jit(solution)/shard_map/ppermute | solution.py:230
  699.0 16.0 %collective-permute-start.57 = (f32[7168]{0:T(1024)S(1)}, f32[7168]{0:T(1024)S(1)}, u32[]{:S(2)}, u32[]{:S(2)}) collective-permute-start(f32[7168]{0:T(1024)S(1)} %add.1002), channel_id=1, source_target_pairs={{0,4},{2,6},{4,0},{6,2},{8,12},{10,14},{12,8},{14,10},{16,20},{18,... | collective-permute-start | bytes 86024 | tf_op jit(solution)/shard_map/ppermute | solution.py:230
  720.3 14.0 %collective-permute-start.58 = (bf16[2,128,1024]{2,1,0:T(8,128)(2,1)S(1)}, bf16[2,128,1024]{2,1,0:T(8,128)(2,1)S(1)}, u32[]{:S(2)}, u32[]{:S(2)}) collective-permute-start(bf16[2,128,1024]{2,1,0:T(8,128)(2,1)S(1)} %dynamic-slice_bitcast_fusion.8), channel_id=1, source_target_pairs={{0,8},{2,10},{4,12},{6,14},{8,0},{10,2},{12,4},{14,6},{16,24},{18,... | collective-permute-start | bytes 1572872 | tf_op jit(solution)/shard_map/ppermute | solution.py:230
  734.6 14.1 %collective-permute-start.59 = (bf16[128,1024]{1,0:T(8,128)(2,1)S(1)}, bf16[128,1024]{1,0:T(8,128)(2,1)S(1)}, u32[]{:S(2)}, u32[]{:S(2)}) collective-permute-start(bf16[128,1024]{1,0:T(8,128)(2,1)S(1)} %dynamic-slice_bitcast_fusion.18), channel_id=1, source_target_pairs={{0,16},{2,18},{4,20},{6,22},{8,24},{10,26},{12,28},{14,30},{16,0},... | collective-permute-start | bytes 786440 | tf_op jit(solution)/shard_map/ppermute | solution.py:230
  (207 other events, 2134.1 us)
Sparse Core Ops, SparseCore 0:
  505.2 86.5 all-gather.10
  634.6 88.2 all-gather.8
  749.7 72.1 all-gather.6

commit v2 on v1

--- a/solution.py
+++ b/solution.py
@@ -1,3 +1,4 @@
+import functools
 import math
 
 import jax
@@ -12,7 +13,6 @@
 CONV_K = 31
 BACK = 64
 AHEAD = 8
-VMEM_LIMIT = 32 << 20
 
 epsilon = 1e-05
 
@@ -81,7 +81,9 @@
 
 def wide_sum(share):
     if paired():
-        return share + swap(share)
+        count = 2 * lax.axis_size("dp")
+        pairs = [(place, place ^ 1) for place in reversed(range(count))]
+        return share + lax.ppermute(share, ("dp", "tensor"), pairs)
     return lax.psum(share, "tensor")
 
 
@@ -138,6 +140,11 @@
         return self.own + widen(got)
 
 
+class Met:
+    def __init__(self, values):
+        self.values = list(values)
+
+
 class Job:
     def __init__(self, steps):
         self.steps = steps
@@ -164,8 +171,8 @@
         self.jobs.append(job)
         return job
 
-    def turn(self, held):
-        active = [job for job in self.jobs if job.active]
+    def turn(self, held, jobs=True):
+        active = [job for job in self.jobs if jobs and job.active]
         flat = list(held)
         for job in active:
             flat.extend(job.waiting)
@@ -182,9 +189,9 @@
         under_way = None
         got = {}
 
-        def settle(held):
+        def settle(held, jobs=True):
             extra = [] if under_way is None else [under_way[1].sent, under_way[2]]
-            out, moved = self.turn(held + extra)
+            out, moved = self.turn(held + extra, jobs)
             if under_way is not None:
                 got[under_way[0]] = under_way[1].finish(out[-2], out[-1])
             for job, values in moved:
@@ -204,6 +211,10 @@
                 else:
                     started.add(place)
                     request = next(clips[place])
+                while isinstance(request, Met):
+                    values = settle(request.values, False)
+                    under_way = None
+                    request = clips[place].send(values)
             except StopIteration:
                 continue
             (sent,) = settle([request.sent])
@@ -256,13 +267,12 @@
     return value.reshape(2, 2, 2, 2, value.shape[0] // 16, value.shape[1])
 
 
-def scatter_job(make, delay, width):
-    yield []
-    values = yield [narrow(value) for value in make()]
+def scatter_job(make, delay, width, eager):
+    if not eager:
+        yield []
+    values = [narrow(value) for value in make()]
     if not dp_grid():
         return values, [lax.psum(value, "dp") for value in values]
-    for _ in range(delay):
-        yield []
     parts = []
     for value in values:
         for start in range(0, value.shape[1], width):
@@ -271,22 +281,38 @@
     sent = jnp.concatenate([piece_of(part, 1 - core, 3) for part in parts], axis=3)
     kept = jnp.concatenate([piece_of(part, core, 3) for part in parts], axis=3)
     part = add_low(kept, dp_swap(sent, 1))
-    (got,) = yield [dp_swap(piece_of(part, 1 - side, 2), 2)]
-    part = add_low(piece_of(part, side, 2), got)
-    got = dp_swap(piece_of(part, 1 - near, 1), 4)
-    part = add_low(piece_of(part, near, 1), got)
-    (got,) = yield [dp_swap(piece_of(part, 1 - far, 0), 8)]
-    return values, add_low(piece_of(part, far, 0), got)
-
-
-def gather_job(jobs):
+    sent, kept = yield [piece_of(part, 1 - side, 2), piece_of(part, side, 2)]
+    for _ in range(delay):
+        yield []
+    part = add_low(kept, dp_swap(sent, 2))
+    sent, kept = yield [piece_of(part, 1 - near, 1), piece_of(part, near, 1)]
+    part = add_low(kept, dp_swap(sent, 4))
+    shard = add_low(piece_of(part, far, 0), dp_swap(piece_of(part, 1 - far, 0), 8))
+    (shard,) = yield [shard]
+    return values, shard
+
+
+def sum_job(make):
+    values = yield [narrow(value) for value in make()]
+    summed = [lax.psum(value, "dp") for value in values]
+    for _ in range(4):
+        yield []
+    return (yield summed)
+
+
+def gather_job(jobs, turns):
     while any(job.active for job in jobs):
         yield []
+    values = [value for job in jobs for value in job.result[0]]
     if not dp_grid():
         return [value for job in jobs for value in job.result[1]]
     shards = jnp.concatenate([job.result[1] for job in jobs], axis=0)
     whole = lax.all_gather(shards, "dp", axis=0)
-    return unstack_columns(whole, [value for job in jobs for value in job.result[0]])
+    if turns is not None:
+        for _ in range(turns):
+            yield []
+        (whole,) = yield [whole]
+    return unstack_columns(whole, values)
 
 
 def small_job(values):
@@ -309,6 +335,7 @@
 PAIR = 2 * HEAD_DIM
 QB = 128
 WINDOW = 3 * QB
+ROWS = 32
 
 
 def keep_head(block, head):
@@ -318,99 +345,74 @@
     return jnp.where(inside, block, jnp.zeros_like(block))
 
 
-def window_place():
-    return lax.broadcasted_iota(jnp.int32, (QB, WINDOW), 1) - lax.broadcasted_iota(
-        jnp.int32, (QB, WINDOW), 0
-    )
-
-
-def spread_rows(relative, block, blocks):
+def strip_place(begin, length):
+    return (
+        lax.broadcasted_iota(jnp.int32, (ROWS, length), 1)
+        - lax.broadcasted_iota(jnp.int32, (ROWS, length), 0)
+        - begin
+    )
+
+
+def strip_probs(content, relative, begin, place):
+    length = content.shape[1]
+    block = begin // QB
+    low = max(block - 1, 0) * QB
+    high = min(block + 2, length // QB) * QB
+    before = relative[:, 0:1]
+    after = relative[:, BACK + AHEAD : BACK + AHEAD + 1]
+    turned = pltpu.roll(relative, (begin + QB - BACK) % QB, 1, stride=1, stride_axis=0)
+    parts = []
+    for start in range(0, length, QB):
+        if start < low:
+            parts.append(jnp.broadcast_to(before, (ROWS, QB)))
+        elif start >= high:
+            parts.append(jnp.broadcast_to(after, (ROWS, QB)))
+        else:
+            here = place[:, start : start + QB]
+            parts.append(
+                jnp.where(here < -BACK, before, jnp.where(here > AHEAD, after, turned))
+            )
+    scores = (content + jnp.concatenate(parts, axis=1)) * SCALE
+    weights = jnp.exp(scores - jnp.max(scores, axis=-1, keepdims=True))
+    return weights * (1.0 / jnp.sum(weights, axis=-1, keepdims=True))
+
+
+def attend_kernel(query_ref, key_ref, value_ref, table_ref, context_ref, score_ref, probs_ref, band_ref):
+    length = query_ref.shape[0]
+    parts = []
+    for head in range(2):
+        query = keep_head(query_ref[...], head)
+        score_ref[head] = product_right(query, key_ref[...])
+        band_ref[head] = product(query, table_ref[...])
+        for begin in range(0, length, ROWS):
+            rows = slice(begin, begin + ROWS)
+            probs_ref[head, rows] = narrow(
+                strip_probs(
+                    score_ref[head, rows],
+                    band_ref[head, rows],
+                    begin,
+                    strip_place(begin, length),
+                )
+            )
+        parts.append(product(probs_ref[head], value_ref[...]))
+    lane = lax.broadcasted_iota(jnp.int32, parts[0].shape, 1)
+    context_ref[...] = narrow(jnp.where(lane < HEAD_DIM, parts[0], parts[1]))
+
+
+def gather_block(low_block, block, blocks, flip):
     low = max(block - 1, 0)
     high = min(block + 2, blocks)
-    before = relative[:, 0:1]
-    after = relative[:, BACK + AHEAD : BACK + AHEAD + 1]
-    wide = jnp.concatenate([relative, jnp.zeros((QB, WINDOW - QB), jnp.float32)], axis=1)
-    skewed = pltpu.roll(wide, QB - BACK, 1, stride=1, stride_axis=0)
-    place = window_place()
-    skewed = jnp.where(place < QB - BACK, before, skewed)
-    skewed = jnp.where(place > QB + AHEAD, after, skewed)
-    parts = []
-    if low > 0:
-        parts.append(jnp.broadcast_to(before, (QB, low * QB)))
-    parts.append(skewed[:, (low - block + 1) * QB : (high - block + 1) * QB])
-    if high < blocks:
-        parts.append(jnp.broadcast_to(after, (QB, (blocks - high) * QB)))
-    return jnp.concatenate(parts, axis=1)
-
-
-def gather_rows_back(incoming, block, blocks, flip):
-    low = max(block - 1, 0)
-    high = min(block + 2, blocks)
-    wide = widen(incoming)
-    place = lax.broadcasted_iota(jnp.int32, wide.shape, 1) - lax.broadcasted_iota(
-        jnp.int32, wide.shape, 0
-    )
-    back = jnp.sum(
-        jnp.where(place <= block * QB - BACK, wide, 0.0), axis=-1, keepdims=True
-    )
-    ahead = jnp.sum(
-        jnp.where(place >= block * QB + AHEAD, wide, 0.0), axis=-1, keepdims=True
-    )
     parts = []
     if block == 0:
         parts.append(jnp.zeros((QB, QB), jnp.bfloat16))
-    parts.append(incoming[:, low * QB : high * QB])
+    parts.append(low_block[:, low * QB : high * QB])
     if block == blocks - 1:
         parts.append(jnp.zeros((QB, QB), jnp.bfloat16))
-    window = jnp.concatenate(parts, axis=1)
-    reversed_rows = product(flip, window)
+    reversed_rows = product(flip, jnp.concatenate(parts, axis=1))
     moved = pltpu.roll(
         reversed_rows, WINDOW - (QB - BACK) - (QB - 1), 1, stride=1, stride_axis=0
     )[:, :QB]
-    inner = product(flip, narrow(moved))
-    lane = lax.broadcasted_iota(jnp.int32, (QB, QB), 1)
-    inner = jnp.where(lane < BACK + AHEAD, inner, 0.0)
-    inner = jnp.where(lane == 0, back, inner)
-    return jnp.where(lane == BACK + AHEAD, ahead, inner)
-
-
-def block_rows(block):
-    return slice(block * QB, (block + 1) * QB)
-
-
-def softmax_rows(content, relative, block, blocks):
-    scores = (content + spread_rows(relative, block, blocks)) * SCALE
-    weights = jnp.exp(scores - jnp.max(scores, axis=-1, keepdims=True))
-    return weights * (1.0 / jnp.sum(weights, axis=-1, keepdims=True))
-
-
-def scores_of(query_head, key_block, table_block, blocks):
-    content = product_right(query_head, key_block)
-    relative = product(query_head, table_block)
-    rows = [
-        spread_rows(relative[block * QB : (block + 1) * QB], block, blocks)
-        for block in range(blocks)
-    ]
-    return (content + jnp.concatenate(rows, axis=0)) * SCALE
-
-
-def softmax_of(scores):
-    weights = jnp.exp(scores - jnp.max(scores, axis=-1, keepdims=True))
-    return weights * (1.0 / jnp.sum(weights, axis=-1, keepdims=True))
-
-
-def attend_kernel(query_ref, key_ref, value_ref, table_ref, context_ref):
-    blocks = query_ref.shape[0] // QB
-    query = query_ref[...]
-    keys = key_ref[...]
-    values = value_ref[...]
-    table = table_ref[...]
-    parts = []
-    for head in range(2):
-        probs = softmax_of(scores_of(keep_head(query, head), keys, table, blocks))
-        parts.append(product(probs.astype(jnp.bfloat16), values))
-    lane = lax.broadcasted_iota(jnp.int32, parts[0].shape, 1)
-    context_ref[...] = jnp.where(lane < HEAD_DIM, parts[0], parts[1]).astype(jnp.bfloat16)
+    return product(flip, narrow(moved))
 
 
 def attend_back_kernel(
@@ -431,12 +433,14 @@
     probs_ref,
     low_ref,
     band_ref,
+    ends_ref,
 ):
     @pl.when(pl.program_id(0) == 0)
     def _():
         table_grad_ref[...] = jnp.zeros_like(table_grad_ref)
 
-    blocks = query_ref.shape[0] // QB
+    length = query_ref.shape[0]
+    blocks = length // QB
     query_turned = narrow(widen(query_ref[...]).T)
     grad_turned = narrow(widen(grad_ref[...]).T)
     flip = narrow(
@@ -446,6 +450,7 @@
             == QB - 1
         ).astype(jnp.float32)
     )
+    lane = lax.broadcasted_iota(jnp.int32, (ROWS, QB), 1)
     query_parts = []
     key_parts = []
     value_parts = []
@@ -453,17 +458,29 @@
         piece = slice(head * HEAD_DIM, (head + 1) * HEAD_DIM)
         query = keep_head(query_ref[...], head)
         score_ref[head] = product_right(query, key_ref[...])
-        relative = product(query, table_ref[...])
+        band_ref[head] = product(query, table_ref[...])
         wide_ref[head] = product_right(keep_head(grad_ref[...], head), value_ref[...])
-        for block in range(blocks):
-            rows = block_rows(block)
-            probs = softmax_rows(score_ref[head, rows], relative[rows], block, blocks)
+        for begin in range(0, length, ROWS):
+            rows = slice(begin, begin + ROWS)
+            place = strip_place(begin, length)
+            probs = strip_probs(score_ref[head, rows], band_ref[head, rows], begin, place)
             probs_ref[head, rows] = narrow(probs)
             probs_grad = wide_ref[head, rows]
             delta = jnp.sum(probs * probs_grad, axis=-1, keepdims=True)
             score_grad = narrow(probs * (probs_grad - delta))
             low_ref[head, rows] = score_grad
-            band_ref[head, rows] = gather_rows_back(score_grad, block, blocks, flip)
+            wide = widen(score_grad)
+            back = jnp.sum(jnp.where(place <= -BACK, wide, 0.0), axis=-1, keepdims=True)
+            ahead = jnp.sum(jnp.where(place >= AHEAD, wide, 0.0), axis=-1, keepdims=True)
+            ends_ref[head, rows] = jnp.where(
+                lane == 0, back, jnp.where(lane == BACK + AHEAD, ahead, 0.0)
+            )
+        for block in range(blocks):
+            rows = slice(block * QB, (block + 1) * QB)
+            inner = gather_block(low_ref[head, rows], block, blocks, flip)
+            column = lax.broadcasted_iota(jnp.int32, (QB, QB), 1)
+            inside = jnp.logical_and(column > 0, column < BACK + AHEAD)
+            band_ref[head, rows] = jnp.where(inside, inner, ends_ref[head, rows])
         value_parts.append(product(grad_turned[piece], probs_ref[head]))
         key_parts.append(product(query_turned[piece], low_ref[head]))
         band = band_ref[head]
@@ -509,7 +526,12 @@
         grid=(width // PAIR,),
         in_specs=[pair_spec(length)] * 3 + [fixed_spec((PAIR, QB))],
         out_specs=pair_spec(length),
-        compiler_params=pltpu.CompilerParams(vmem_limit_bytes=VMEM_LIMIT),
+        scratch_shapes=[
+            pltpu.VMEM((2, length, length), jnp.float32),
+            pltpu.VMEM((2, length, length), jnp.bfloat16),
+            pltpu.VMEM((2, length, QB), jnp.float32),
+        ],
+        compiler_params=pltpu.CompilerParams(vmem_limit_bytes=16 << 20),
         name="attend_heads",
     )(query, keys, values, table)
 
@@ -536,8 +558,9 @@
             pltpu.VMEM((2, length, length), jnp.bfloat16),
             pltpu.VMEM((2, length, length), jnp.bfloat16),
             pltpu.VMEM((2, length, QB), jnp.float32),
+            pltpu.VMEM((2, length, QB), jnp.float32),
         ],
-        compiler_params=pltpu.CompilerParams(vmem_limit_bytes=VMEM_LIMIT),
+        compiler_params=pltpu.CompilerParams(vmem_limit_bytes=20 << 20),
         name="attend_heads_back",
     )(query, keys, values, grad, table, rows)
 LANES = 128
@@ -604,7 +627,7 @@
             pltpu.VMEM((EDGE + length, LANES), jnp.float32),
             pltpu.VMEM((2, length, LANES), jnp.float32),
         ],
-        compiler_params=pltpu.CompilerParams(vmem_limit_bytes=VMEM_LIMIT),
+        compiler_params=pltpu.CompilerParams(vmem_limit_bytes=8 << 20),
         name="mix_channels",
     )(linear, gate, taps)
     return mixed, jnp.concatenate([sums[0:1], sums[8:9]], axis=0)
@@ -671,7 +694,7 @@
             pltpu.VMEM((EDGE + length, LANES), jnp.float32),
             pltpu.VMEM((EDGE, 8, LANES), jnp.float32),
         ],
-        compiler_params=pltpu.CompilerParams(vmem_limit_bytes=VMEM_LIMIT),
+        compiler_params=pltpu.CompilerParams(vmem_limit_bytes=8 << 20),
         name="mix_channels_back",
     )(grad, linear, gate, taps)
 
@@ -726,6 +749,7 @@
     query_low, key_low, value_low, query_sum, value_sum, table_grad = attend_heads_back(
         query, keys, values, context_grad, table, table_rows
     )
+    query_low, key_low, value_low = yield Met([query_low, key_low, value_low])
     share = (
         product_right(query_low, query_weight)
         + product_right(key_low, key_weight)
@@ -747,7 +771,7 @@
     normed = narrow(normed)
     linear = product(normed, pointwise_in[0])
     gate = product(normed, pointwise_in[1])
-    mixed, sums = mix_channels(linear, gate, taps)
+    mixed, sums = yield Met(mix_channels(linear, gate, taps))
     return mixed, wide_sum(sums), (rows, center, inverse, normed, linear, gate)
 
 
@@ -796,8 +820,38 @@
     return result
 
 
+def weight_grad_kernel(count, *refs):
+    total = product_left(refs[0][...], refs[1][...])
+    for place in range(1, count):
+        total = total + product_left(refs[2 * place][...], refs[2 * place + 1][...])
+    refs[2 * count][...] = narrow(total)
+
+
+def tile_of(size, limit):
+    tile = size
+    while tile > limit:
+        tile //= 2
+    return tile
+
+
 def weight_grad(lefts, rights):
-    return total([product_left(left, right) for left, right in zip(lefts, rights)])
+    length, rows = lefts[0].shape
+    columns = rights[0].shape[1]
+    row_tile, column_tile = tile_of(rows, 1024), tile_of(columns, 1024)
+    operands = [value for pair in zip(lefts, rights) for value in pair]
+    return pl.pallas_call(
+        functools.partial(weight_grad_kernel, len(lefts)),
+        out_shape=jax.ShapeDtypeStruct((rows, columns), jnp.bfloat16),
+        grid=(rows // row_tile, columns // column_tile),
+        in_specs=[
+            pl.BlockSpec((length, row_tile), lambda row, column: (0, row)),
+            pl.BlockSpec((length, column_tile), lambda row, column: (0, column)),
+        ]
+        * len(lefts),
+        out_specs=pl.BlockSpec((row_tile, column_tile), lambda row, column: (row, column)),
+        compiler_params=pltpu.CompilerParams(vmem_limit_bytes=24 << 20),
+        name="weight_grad",
+    )(*operands)
 
 
 class Gradients:
@@ -812,17 +866,16 @@
         parts.append(part)
         return len(parts) == self.count
 
-    def weights(self, name, pairs, width, delay=0):
+    def maker(self, name):
+        parts = self.parts[name]
+        return lambda: [
+            weight_grad([part[place][0] for part in parts], [part[place][1] for part in parts])
+            for place in range(len(parts[0]))
+        ]
+
+    def weights(self, name, pairs, width, delay=0, eager=False):
         if self.add(name, pairs):
-            parts = self.parts[name]
-
-            def make():
-                return [
-                    weight_grad([part[place][0] for part in parts], [part[place][1] for part in parts])
-                    for place in range(len(pairs))
-                ]
-
-            self.jobs[name] = self.flow.launch(scatter_job(make, delay, width))
+            self.jobs[name] = self.flow.launch(scatter_job(self.maker(name), delay, width, eager))
 
     def sums(self, name, values):
         self.add(name, values)
@@ -834,10 +887,14 @@
             values.extend(total([part[place] for part in parts]) for place in range(len(parts[0])))
         self.jobs[name] = self.flow.launch(small_job(values))
 
-    def gather(self, name, members):
+    def whole(self, name, pairs):
+        if self.add(name, pairs):
+            self.jobs[name] = self.flow.launch(sum_job(self.maker(name)))
+
+    def gather(self, name, members, turns=None):
         if members[-1] in self.jobs and name not in self.jobs:
             self.jobs[name] = self.flow.launch(
-                gather_job([self.jobs[member] for member in members])
+                gather_job([self.jobs[member] for member in members], turns)
             )
 
     def result(self, name):
@@ -921,7 +978,7 @@
             table,
         )
         rows = rows + (yield Summed(share)) + widen(output_bias)
-        mixed, sums, convolve_kept = mix(
+        mixed, sums, convolve_kept = yield from mix(
             rows, convolve_gain, widen(convolve_norm_shift), pointwise_in, taps
         )
         share, shape_kept = convolve(
@@ -948,9 +1005,7 @@
         share, spread, before_low, up_sum, down_sum = feed_back(
             grad, second_kept, second_up_weight, second_down_weight
         )
-        grads.weights("second_down", [(second_kept[5], spread)], spread.shape[1])
-        grads.weights("second_up", [(second_kept[3], before_low)], spread.shape[1], 1)
-        grads.gather("second", ["second_down", "second_up"])
+        grads.whole("second_both", [(second_kept[5], spread), (second_kept[3], before_low)])
         normed_grad = yield Summed(share)
         grad, gain_grad, shift_grad = residual_back(grad, normed_grad, second_kept, second_gain)
         grads.sums("second", [up_sum, down_sum, gain_grad, shift_grad])
@@ -978,7 +1033,7 @@
             "convolve_sums", [depth_gain_sum, depth_shift_sum, depthwise_sum, gain_grad, shift_grad]
         )
 
-        share, spread, lows, query_sum, value_sum, output_sum, table_sum = attend_back(
+        share, spread, lows, query_sum, value_sum, output_sum, table_sum = yield from attend_back(
             grad,
             attend_kept,
             query_weight,
@@ -1007,8 +1062,8 @@
         share, spread, before_low, up_sum, down_sum = feed_back(
             grad, first_kept, first_up_weight, first_down_weight
         )
-        grads.weights("first_down", [(first_kept[5], spread)], spread.shape[1])
-        grads.weights("first_up", [(first_kept[3], before_low)], spread.shape[1], 1)
+        grads.weights("first_down", [(first_kept[5], spread)], spread.shape[1], eager=True)
+        grads.weights("first_up", [(first_kept[3], before_low)], spread.shape[1], 1, eager=True)
         grads.gather("first_both", ["first_down", "first_up"])
         normed_grad = yield Scattered(share)
         input_grads[slot], gain_grad, shift_grad = residual_back(
@@ -1030,7 +1085,7 @@
     clips = count_job.result[0][0, 0]
     early = grads.result("early")
     late = grads.result("late")
-    second_down, second_up = grads.result("second")
+    second_down, second_up = grads.result("second_both")
     linear, gating, point_out, output_grad, query_grad, key_grad, value_grad = grads.result("middle")
     first_down, first_up = grads.result("first_both")
     table_grad = wide_sum(early[14]).T[: relative_table.shape[0]]

time: 852 us -> 778 us (0.913)
  matrix products: 143 us -> 82.7 us
  waiting for transfers between devices: 343 us -> 327 us
  Pallas kernels: 106 us -> 120 us
  starting transfers between devices: 74 us -> 63.3 us
    dot_general x22 -> x0, matrix products: 69.3 us -> none  [product_left(): lax.dot_general(left, right, (((0,), (0,)), ((), ())), preferred_element_...]
    pallas_call x0 -> x11, Pallas kernels: none -> 30.4 us  [weight_grad(): pl.pallas_call(functools.partial(weight_grad_kernel, len(lefts)), out_sha...]
    ppermute x27 -> x20, waiting for transfers between devices: 120 us -> 103 us  [swap(): return lax.ppermute(values, 'tensor', [(0, 1), (1, 0)])]
    ppermute x36 -> x28, starting transfers between devices: 38.7 us -> 25 us  [dp_swap(): lax.ppermute(values, 'dp', [(place, place ^ bit) for place in range(16)])]
    pallas_call x2, Pallas kernels: 19.6 us -> 8.49 us  [mix_channels(): pl.pallas_call(mix_kernel, out_shape=(jax.ShapeDtypeStruct((length, width...]
    ppermute x36 -> x28, waiting for transfers between devices: 193 us -> 182 us  [dp_swap(): lax.ppermute(values, 'dp', [(place, place ^ bit) for place in range(16)])]
    ppermute x0 -> x7, waiting for transfers between devices: none -> 10.1 us  [wide_sum(): return share + lax.ppermute(share, ('dp', 'tensor'), pairs)]
    ppermute x0 -> x7, starting transfers between devices: none -> 9.22 us  [wide_sum(): return share + lax.ppermute(share, ('dp', 'tensor'), pairs)]
  transfers between devices with their start and end apart: 66 -> 58, of which waited for: 42 -> 30; matrix products, arithmetic and copies ran while one was open for 25% -> 20% of each run, Pallas kernels for 10% -> 15%
where the time goes in v2:
time: 778 us; the launch traced here: 769 us
  waiting for transfers between devices  327 us (42%)
  Pallas kernels  120 us (15%)
  other arithmetic  106 us (14%)
  matrix products  82.7 us (11%)
  starting transfers between devices  63.3 us (8%)
  local copies, waits for them, and re-layouts  50.5 us (6%)
  between operations  18.9 us (2%)
    ppermute x28, waiting for transfers between devices, dp_swap(): lax.ppermute(values, 'dp', [(place, place ^ bit) for place in range(16)])  182 us
    ppermute x20, waiting for transfers between devices, swap(): return lax.ppermute(values, 'tensor', [(0, 1), (1, 0)])  103 us
    dot_general x22, matrix products, product_right(): lax.dot_general(left, right, (((1,), (1,)), ((), ())), preferred_element_...  46.1 us
    pallas_call x2, Pallas kernels, attend_heads_back(): pl.pallas_call(attend_back_kernel, out_shape=(jax.ShapeDtypeStruct((lengt...  41.5 us
    dot_general x22, matrix products, product(): return jnp.dot(left, right, preferred_element_type=jnp.float32)  36.6 us
    div x15, other arithmetic, per_device(): widen(value) / clips  36.4 us
    unnamed x423, local copies, waits for them, and re-layouts  34.6 us
    all_gather x2, waiting for transfers between devices, gather_job(): whole = lax.all_gather(shards, 'dp', axis=0)  31.5 us
  transfers between devices with their start and end apart: 58, of which 30 were waited for; matrix products, arithmetic and copies ran while one was open for 20% of the time, Pallas kernels for 15%

profile of v2, /device:TPU:0, one launch (start us, length us, event | category | flops | bytes accessed | tf_op | source)
XLA Modules:
  0.0 768.6 jit_solution(1871264434278356374)
XLA Ops:
  17.5 8.0 %collective-permute-done.1 = bf16[256,1024]{1,0:T(8,128)(2,1)} collective-permute-done((bf16[256,1024]{1,0:T(8,128)(2,1)S(1)}, bf16[256,1024]{1,0:T(8,128)(2,1)}, u32[]{:S(2)}, u32[]{:S(2)}) %collective-permute-start.1) | collective-permute-done | bytes 524320 | tf_op jit(solution)/shard_map/ppermute | solution.py:70
  31.2 4.8 multiply_convert_fusion.3
  38.4 4.1 collective-permute-done.3
  45.3 4.8 multiply_convert_fusion.2
  55.7 11.7 %collective-permute-done.5 = bf16[512,1024]{1,0:T(8,128)(2,1)S(1)} collective-permute-done((bf16[512,1024]{1,0:T(8,128)(2,1)S(1)}, bf16[512,1024]{1,0:T(8,128)(2,1)S(1)}, u32[]{:S(2)}, u32[]{:S(2)}) %collective-permute-start.5) | collective-permute-done | bytes 1048608 | tf_op jit(solution)/shard_map/ppermute | solution.py:70
  74.6 13.8 %attend_heads.2.refs_0_ = bf16[512,512]{1,0:T(8,128)(2,1)S(1)} custom-call(bf16[512,512]{1,0:T(8,128)(2,1)S(1)} %fusion.25.query_ref, bf16[512,512]{1,0:T(8,128)(2,1)S(1)} %convolution_convert_fusion.11.key_ref, bf16[512,512]{1,0:T(8,128)(2,1)S(1)} %fusion.26.value_ref, bf16[128,128]{1,0:T(8,128)(2,1)S(1)} %copy.76.table_ref), custom_call_target="tpu_custom_call" | custom-call | tf_op jit(solution)/shard_map/attend_heads/pallas_call | solution.py:523
  97.1 13.8 %attend_heads.3.refs_2_ = bf16[512,512]{1,0:T(8,128)(2,1)S(1)} custom-call(bf16[512,512]{1,0:T(8,128)(2,1)S(1)} %fusion.27.query_ref, bf16[512,512]{1,0:T(8,128)(2,1)S(1)} %convolution_convert_fusion.10.key_ref, bf16[512,512]{1,0:T(8,128)(2,1)S(1)} %fusion.28.value_ref, bf16[128,128]{1,0:T(8,128)(2,1)S(1)} %copy.76.table_ref), custom_call_target="tpu_custom_call" | custom-call | tf_op jit(solution)/shard_map/attend_heads/pallas_call | solution.py:523
  111.7 4.0 collective-permute-done.8
  120.1 4.3 mix_channels.2
  124.5 13.1 %collective-permute-done.9 = bf16[512,1024]{1,0:T(8,128)(2,1)S(1)} collective-permute-done((bf16[512,1024]{1,0:T(8,128)(2,1)S(1)}, bf16[512,1024]{1,0:T(8,128)(2,1)S(1)}, u32[]{:S(2)}, u32[]{:S(2)}) %collective-permute-start.9) | collective-permute-done | bytes 1048608 | tf_op jit(solution)/shard_map/ppermute | solution.py:70
  146.0 4.2 mix_channels.3
  150.3 11.6 %collective-permute-done.11 = bf16[512,1024]{1,0:T(8,128)(2,1)S(1)} collective-permute-done((bf16[512,1024]{1,0:T(8,128)(2,1)S(1)}, bf16[512,1024]{1,0:T(8,128)(2,1)S(1)}, u32[]{:S(2)}, u32[]{:S(2)}) %collective-permute-start.11) | collective-permute-done | bytes 1048608 | tf_op jit(solution)/shard_map/ppermute | solution.py:70
  168.4 4.8 multiply_convert_fusion.1
  175.6 10.5 %collective-permute-done.13 = bf16[512,1024]{1,0:T(8,128)(2,1)S(1)} collective-permute-done((bf16[512,1024]{1,0:T(8,128)(2,1)S(1)}, bf16[512,1024]{1,0:T(8,128)(2,1)S(1)}, u32[]{:S(2)}, u32[]{:S(2)}) %collective-permute-start.13) | collective-permute-done | bytes 1048608 | tf_op jit(solution)/shard_map/ppermute | solution.py:70
  194.2 10.0 %collective-permute-done.14 = bf16[256,1024]{1,0:T(8,128)(2,1)S(1)} collective-permute-done((bf16[256,1024]{1,0:T(8,128)(2,1)S(1)}, bf16[256,1024]{1,0:T(8,128)(2,1)S(1)}, u32[]{:S(2)}, u32[]{:S(2)}) %collective-permute-start.14) | collective-permute-done | bytes 524320 | tf_op jit(solution)/shard_map/ppermute | solution.py:70
  208.7 9.9 %collective-permute-done.15 = bf16[256,1024]{1,0:T(8,128)(2,1)S(1)} collective-permute-done((bf16[256,1024]{1,0:T(8,128)(2,1)S(1)}, bf16[256,1024]{1,0:T(8,128)(2,1)S(1)}, u32[]{:S(2)}, u32[]{:S(2)}) %collective-permute-start.15) | collective-permute-done | bytes 524320 | tf_op jit(solution)/shard_map/ppermute | solution.py:70
  223.2 6.9 collective-permute-done.27
  231.6 6.1 fusion.89
  242.6 10.0 %collective-permute-done.17 = bf16[256,1024]{1,0:T(8,128)(2,1)S(1)} collective-permute-done((bf16[256,1024]{1,0:T(8,128)(2,1)S(1)}, bf16[256,1024]{1,0:T(8,128)(2,1)S(1)}, u32[]{:S(2)}, u32[]{:S(2)}) %collective-permute-start.17) | collective-permute-done | bytes 524320 | tf_op jit(solution)/shard_map/ppermute | solution.py:70
  254.2 4.3 fusion.88
  258.5 5.4 weight_grad.12
  266.2 5.3 weight_grad.11
  273.5 6.3 convolution_convert_fusion.4
  282.6 3.8 fusion.73
  294.1 6.0 mix_channels_back.2
  303.4 7.9 %collective-permute-done.20 = bf16[512,1024]{1,0:T(8,128)(2,1)} collective-permute-done((bf16[512,1024]{1,0:T(8,128)(2,1)}, bf16[512,1024]{1,0:T(8,128)(2,1)}, u32[]{:S(2)}, u32[]{:S(2)}) %collective-permute-start.20) | collective-permute-done | bytes 1048608 | tf_op jit(solution)/shard_map/ppermute | solution.py:70
  313.9 3.8 fusion.72
  330.9 6.2 mix_channels_back.3
  358.8 20.8 %attend_heads_back.2 = (bf16[512,512]{1,0:T(8,128)(2,1)S(1)}, bf16[512,512]{1,0:T(8,128)(2,1)S(1)}, bf16[512,512]{1,0:T(8,128)(2,1)S(1)}, f32[1,512]{1,0:T(1,128...) custom-call(bf16[512,512]{1,0:T(8,128)(2,1)S(1)} %copy-done.40, bf16[512,512]{1,0:T(8,128)(2,1)S(1)} %copy-done.38, ...), custom_call_target="tpu_custom_call" | custom-call | tf_op jit(solution)/shard_map/attend_heads_back/pallas_call | solution.py:542
  387.7 20.6 %attend_heads_back.3 = (bf16[512,512]{1,0:T(8,128)(2,1)S(1)}, bf16[512,512]{1,0:T(8,128)(2,1)S(1)}, bf16[512,512]{1,0:T(8,128)(2,1)S(1)}, f32[1,512]{1,0:T(1,128...) custom-call(bf16[512,512]{1,0:T(8,128)(2,1)S(1)} %copy-done.36, bf16[512,512]{1,0:T(8,128)(2,1)S(1)} %copy-done.32, ...), custom_call_target="tpu_custom_call" | custom-call | tf_op jit(solution)/shard_map/attend_heads_back/pallas_call | solution.py:542
  415.3 31.4 %collective-permute-done.26 = bf16[2,2,192,512]{3,2,1,0:T(8,128)(2,1)S(1)} collective-permute-done((bf16[2,2,192,512]{3,2,1,0:T(8,128)(2,1)S(1)}, bf16[2,2,192,512]{3,2,1,0:T(8,128)(2,1)S(1)}, u32[]{:S(2)}, u32[]{:S(2)}) %collective-permute-start.26) | collective-permute-done | bytes 786464 | tf_op jit(solution)/shard_map/ppermute | solution.py:241
  473.8 9.3 %collective-permute-done.31 = bf16[192,512]{1,0:T(8,128)(2,1)S(1)} collective-permute-done((bf16[192,512]{1,0:T(8,128)(2,1)S(1)}, bf16[192,512]{1,0:T(8,128)(2,1)S(1)}, u32[]{:S(2)}, u32[]{:S(2)}) %collective-permute-start.31) | collective-permute-done | bytes 196640 | tf_op jit(solution)/shard_map/ppermute | solution.py:241
  497.1 5.8 weight_grad.21
  506.2 5.1 weight_grad.20
  518.3 19.3 %collective-permute-done.35 = bf16[2,2,256,512]{3,2,1,0:T(8,128)(2,1)S(1)} collective-permute-done((bf16[2,2,256,512]{3,2,1,0:T(8,128)(2,1)S(1)}, bf16[2,2,256,512]{3,2,1,0:T(8,128)(2,1)S(1)}, u32[]{:S(2)}, u32[]{:S(2)}) %collective-permute-start.35) | collective-permute-done | bytes 1048608 | tf_op jit(solution)/shard_map/ppermute | solution.py:241
  543.1 11.4 %collective-permute-done.40 = bf16[2,256,512]{2,1,0:T(8,128)(2,1)S(1)} collective-permute-done((bf16[2,256,512]{2,1,0:T(8,128)(2,1)S(1)}, bf16[2,256,512]{2,1,0:T(8,128)(2,1)S(1)}, u32[]{:S(2)}, u32[]{:S(2)}) %collective-permute-start.40) | collective-permute-done | bytes 524320 | tf_op jit(solution)/shard_map/ppermute | solution.py:241
  558.2 12.8 %collective-permute-done.41 = bf16[256,512]{1,0:T(8,128)(2,1)S(1)} collective-permute-done((bf16[256,512]{1,0:T(8,128)(2,1)S(1)}, bf16[256,512]{1,0:T(8,128)(2,1)S(1)}, u32[]{:S(2)}, u32[]{:S(2)}) %collective-permute-start.41) | collective-permute-done | bytes 262176 | tf_op jit(solution)/shard_map/ppermute | solution.py:241
  584.1 23.4 %collective-permute-done.47 = bf16[2,2,128,1024]{3,2,1,0:T(8,128)(2,1)S(1)} collective-permute-done((bf16[2,2,128,1024]{3,2,1,0:T(8,128)(2,1)S(1)}, bf16[2,2,128,1024]{3,2,1,0:T(8,128)(2,1)S(1)}, u32[]{:S(2)}, u32[]{:S(2)}) %collective-permute-start.47) | collective-permute-done | bytes 1048608 | tf_op jit(solution)/shard_map/ppermute | solution.py:241
  608.5 25.6 %collective-permute-done.46 = bf16[128,1024]{1,0:T(8,128)(2,1)S(1)} collective-permute-done((bf16[128,1024]{1,0:T(8,128)(2,1)S(1)}, bf16[128,1024]{1,0:T(8,128)(2,1)S(1)}, u32[]{:S(2)}, u32[]{:S(2)}) %collective-permute-start.46) | collective-permute-done | bytes 262176 | tf_op jit(solution)/shard_map/ppermute | solution.py:241
  635.5 23.9 %collective-permute-done.49 = bf16[2,128,1024]{2,1,0:T(8,128)(2,1)S(1)} collective-permute-done((bf16[2,128,1024]{2,1,0:T(8,128)(2,1)S(1)}, bf16[2,128,1024]{2,1,0:T(8,128)(2,1)S(1)}, u32[]{:S(2)}, u32[]{:S(2)}) %collective-permute-start.49) | collective-permute-done | bytes 524320 | tf_op jit(solution)/shard_map/ppermute | solution.py:241
  662.1 11.4 %collective-permute-done.50 = bf16[128,1024]{1,0:T(8,128)(2,1)S(1)} collective-permute-done((bf16[128,1024]{1,0:T(8,128)(2,1)S(1)}, bf16[128,1024]{1,0:T(8,128)(2,1)S(1)}, u32[]{:S(2)}, u32[]{:S(2)}) %collective-permute-start.50) | collective-permute-done | bytes 262176 | tf_op jit(solution)/shard_map/ppermute | solution.py:241
  675.6 7.0 convert_divide_fusion
  682.6 5.5 convert_divide_fusion.1
  695.3 5.5 collective-permute-done.52
  701.6 4.3 collective-permute-done.53
  718.8 31.5 %all-gather.5.cloned.1.call-done = bf16[4096,1024]{1,0:T(8,128)(2,1)} async-done(((bf16[256,1024]{1,0:T(8,128)(2,1)}), bf16[4096,1024]{1,0:T(8,128)(2,1)}) %all-gather.5.cloned.1.call-update) | async-done | bytes 8388624 | tf_op jit(solution)/shard_map/all_gather | solution.py:310
  750.3 7.0 convert_divide_fusion.2
  757.9 4.0 convert_divide_fusion.3
  (828 shorter events, 258.7 us)
Async XLA Ops:
  7.5 477.9 %all-reduce.5.cloned.1.call-start = ((), (), s32[]{:S(2)}) async-start(), calls=%async_computation.2 | async-start | bytes 16777216 | tf_op jit(solution)/shard_map/psum | solution.py:297
  10.2 15.3 %collective-permute-start.1 = (bf16[256,1024]{1,0:T(8,128)(2,1)S(1)}, bf16[256,1024]{1,0:T(8,128)(2,1)}, u32[]{:S(2)}, u32[]{:S(2)}) collective-permute-start(bf16[256,1024]{1,0:T(8,128)(2,1)S(1)} %get-tuple-element.155), channel_id=1, source_target_pairs={{0,1},{1,0},{2,3},{3,2},{4,5},{5,4},{6,7},{7,6},{8,9},{9,8},{10,11... | collective-permute-start | bytes 1572872 | tf_op jit(solution)/shard_map/ppermute | solution.py:70
  27.4 11.0 %collective-permute-start.4 = (f32[128]{0:T(128)S(1)}, f32[128]{0:T(128)S(1)}, u32[]{:S(2)}, u32[]{:S(2)}) collective-permute-start(f32[128]{0:T(128)S(1)} %fusion.184), channel_id=1, source_target_pairs={{0,8},{2,10},{4,12},{6,14},{8,0},{10,2},{12,4},{14,6},{16,24},{18,... | collective-permute-start | bytes 1544 | tf_op jit(solution)/shard_map/ppermute | solution.py:241
  29.2 13.3 %collective-permute-start.3 = (bf16[256,1024]{1,0:T(8,128)(2,1)S(1)}, bf16[256,1024]{1,0:T(8,128)(2,1)S(1)}, u32[]{:S(2)}, u32[]{:S(2)}) collective-permute-start(bf16[256,1024]{1,0:T(8,128)(2,1)S(1)} %get-tuple-element.159), channel_id=1, source_target_pairs={{0,1},{1,0},{2,3},{3,2},{4,5},{5,4},{6,7},{7,6},{8,9},{9,8},{10,11... | collective-permute-start | bytes 1572872 | tf_op jit(solution)/shard_map/ppermute | solution.py:70
  43.7 23.6 %collective-permute-start.5 = (bf16[512,1024]{1,0:T(8,128)(2,1)S(1)}, bf16[512,1024]{1,0:T(8,128)(2,1)S(1)}, u32[]{:S(2)}, u32[]{:S(2)}) collective-permute-start(bf16[512,1024]{1,0:T(8,128)(2,1)S(1)} %convolution_convert_fusion.7), channel_id=1, source_target_pairs={{0,1},{1,0},{2,3},{3,2},{4,5},{5,4},{6,7},{7,6},{8,9},{9,8},{10,11... | collective-permute-start | bytes 3145736 | tf_op jit(solution)/shard_map/ppermute | solution.py:70
  68.8 22.7 %collective-permute-start.7 = (bf16[512,1024]{1,0:T(8,128)(2,1)S(1)}, bf16[512,1024]{1,0:T(8,128)(2,1)S(1)}, u32[]{:S(2)}, u32[]{:S(2)}) collective-permute-start(bf16[512,1024]{1,0:T(8,128)(2,1)S(1)} %convolution_convert_fusion.6), channel_id=1, source_target_pairs={{0,1},{1,0},{2,3},{3,2},{4,5},{5,4},{6,7},{7,6},{8,9},{9,8},{10,11... | collective-permute-start | bytes 3145736 | tf_op jit(solution)/shard_map/ppermute | solution.py:70
  93.4 22.4 %collective-permute-start.8 = (bf16[512,1024]{1,0:T(8,128)(2,1)S(1)}, bf16[512,1024]{1,0:T(8,128)(2,1)S(1)}, u32[]{:S(2)}, u32[]{:S(2)}) collective-permute-start(bf16[512,1024]{1,0:T(8,128)(2,1)S(1)} %convolution_convert_fusion.3), channel_id=1, source_target_pairs={{0,1},{1,0},{2,3},{3,2},{4,5},{5,4},{6,7},{7,6},{8,9},{9,8},{10,11... | collective-permute-start | bytes 3145736 | tf_op jit(solution)/shard_map/ppermute | solution.py:70
  116.6 21.0 %collective-permute-start.9 = (bf16[512,1024]{1,0:T(8,128)(2,1)S(1)}, bf16[512,1024]{1,0:T(8,128)(2,1)S(1)}, u32[]{:S(2)}, u32[]{:S(2)}) collective-permute-start(bf16[512,1024]{1,0:T(8,128)(2,1)S(1)} %convolution_convert_fusion.2), channel_id=1, source_target_pairs={{0,1},{1,0},{2,3},{3,2},{4,5},{5,4},{6,7},{7,6},{8,9},{9,8},{10,11... | collective-permute-start | bytes 3145736 | tf_op jit(solution)/shard_map/ppermute | solution.py:70
  142.6 19.2 %collective-permute-start.11 = (bf16[512,1024]{1,0:T(8,128)(2,1)S(1)}, bf16[512,1024]{1,0:T(8,128)(2,1)S(1)}, u32[]{:S(2)}, u32[]{:S(2)}) collective-permute-start(bf16[512,1024]{1,0:T(8,128)(2,1)S(1)} %convolution_convert_fusion.1), channel_id=1, source_target_pairs={{0,1},{1,0},{2,3},{3,2},{4,5},{5,4},{6,7},{7,6},{8,9},{9,8},{10,11... | collective-permute-start | bytes 3145736 | tf_op jit(solution)/shard_map/ppermute | solution.py:70
  166.9 19.2 %collective-permute-start.13 = (bf16[512,1024]{1,0:T(8,128)(2,1)S(1)}, bf16[512,1024]{1,0:T(8,128)(2,1)S(1)}, u32[]{:S(2)}, u32[]{:S(2)}) collective-permute-start(bf16[512,1024]{1,0:T(8,128)(2,1)S(1)} %convolution_convert_fusion), channel_id=1, source_target_pairs={{0,1},{1,0},{2,3},{3,2},{4,5},{5,4},{6,7},{7,6},{8,9},{9,8},{10,11... | collective-permute-start | bytes 3145736 | tf_op jit(solution)/shard_map/ppermute | solution.py:70
  190.2 14.0 %collective-permute-start.14 = (bf16[256,1024]{1,0:T(8,128)(2,1)S(1)}, bf16[256,1024]{1,0:T(8,128)(2,1)S(1)}, u32[]{:S(2)}, u32[]{:S(2)}) collective-permute-start(bf16[256,1024]{1,0:T(8,128)(2,1)S(1)} %dynamic-slice_convert_fusion.3), channel_id=1, source_target_pairs={{0,1},{1,0},{2,3},{3,2},{4,5},{5,4},{6,7},{7,6},{8,9},{9,8},{10,11... | collective-permute-start | bytes 1572872 | tf_op jit(solution)/shard_map/ppermute | solution.py:70
  204.8 13.8 %collective-permute-start.15 = (bf16[256,1024]{1,0:T(8,128)(2,1)S(1)}, bf16[256,1024]{1,0:T(8,128)(2,1)S(1)}, u32[]{:S(2)}, u32[]{:S(2)}) collective-permute-start(bf16[256,1024]{1,0:T(8,128)(2,1)S(1)} %dynamic-slice_convert_fusion.2), channel_id=1, source_target_pairs={{0,1},{1,0},{2,3},{3,2},{4,5},{5,4},{6,7},{7,6},{8,9},{9,8},{10,11... | collective-permute-start | bytes 1572872 | tf_op jit(solution)/shard_map/ppermute | solution.py:70
  219.7 11.6 %collective-permute-start.16 = (bf16[256,1024]{1,0:T(8,128)(2,1)S(1)}, bf16[256,1024]{1,0:T(8,128)(2,1)S(1)}, u32[]{:S(2)}, u32[]{:S(2)}) collective-permute-start(bf16[256,1024]{1,0:T(8,128)(2,1)S(1)} %multiply_convert_fusion.8), channel_id=1, source_target_pairs={{0,1},{1,0},{2,3},{3,2},{4,5},{5,4},{6,7},{7,6},{8,9},{9,8},{10,11... | collective-permute-start | bytes 1572872 | tf_op jit(solution)/shard_map/ppermute | solution.py:70
  237.7 14.9 %collective-permute-start.17 = (bf16[256,1024]{1,0:T(8,128)(2,1)S(1)}, bf16[256,1024]{1,0:T(8,128)(2,1)S(1)}, u32[]{:S(2)}, u32[]{:S(2)}) collective-permute-start(bf16[256,1024]{1,0:T(8,128)(2,1)S(1)} %get-tuple-element.194), channel_id=1, source_target_pairs={{0,1},{1,0},{2,3},{3,2},{4,5},{5,4},{6,7},{7,6},{8,9},{9,8},{10,11... | collective-permute-start | bytes 1572872 | tf_op jit(solution)/shard_map/ppermute | solution.py:70
  252.6 27.2 %collective-permute-start.18 = (bf16[512,1024]{1,0:T(8,128)(2,1)}, bf16[512,1024]{1,0:T(8,128)(2,1)}, u32[]{:S(2)}, u32[]{:S(2)}) collective-permute-start(bf16[512,1024]{1,0:T(8,128)(2,1)} %convolution_convert_fusion.5), channel_id=1, source_target_pairs={{0,1},{1,0},{2,3},{3,2},{4,5},{5,4},{6,7},{7,6},{8,9},{9,8},{10,11... | collective-permute-start | bytes 3145736 | tf_op jit(solution)/shard_map/ppermute | solution.py:70
  289.7 21.6 %collective-permute-start.20 = (bf16[512,1024]{1,0:T(8,128)(2,1)}, bf16[512,1024]{1,0:T(8,128)(2,1)}, u32[]{:S(2)}, u32[]{:S(2)}) collective-permute-start(bf16[512,1024]{1,0:T(8,128)(2,1)} %convolution_convert_fusion.4), channel_id=1, source_target_pairs={{0,1},{1,0},{2,3},{3,2},{4,5},{5,4},{6,7},{7,6},{8,9},{9,8},{10,11... | collective-permute-start | bytes 3145736 | tf_op jit(solution)/shard_map/ppermute | solution.py:70
  291.2 415.9 %all-gather.7.cloned.1.call-start = ((), (), s32[]{:S(2)}) async-start(), calls=%async_computation.1 | async-start | bytes 7798784 | tf_op jit(solution)/shard_map/all_gather | solution.py:310
  320.6 9.3 %collective-permute-start.21 = (f32[2,512]{1,0:T(2,128)S(1)}, f32[2,512]{1,0:T(2,128)S(1)}, u32[]{:S(2)}, u32[]{:S(2)}) collective-permute-start(f32[2,512]{1,0:T(2,128)S(1)} %pad_maximum_fusion.14), channel_id=1, source_target_pairs={{31,30},{30,31},{29,28},{28,29},{27,26},{26,27},{25,24},{24,25},{2... | collective-permute-start | bytes 12296 | tf_op jit(solution)/shard_map/ppermute | solution.py:86
  323.1 25.9 %collective-permute-start.22 = (bf16[512,1024]{1,0:T(8,128)(2,1)}, bf16[512,1024]{1,0:T(8,128)(2,1)}, u32[]{:S(2)}, u32[]{:S(2)}) collective-permute-start(bf16[512,1024]{1,0:T(8,128)(2,1)} %add_convert_fusion.9), channel_id=1, source_target_pairs={{0,1},{1,0},{2,3},{3,2},{4,5},{5,4},{6,7},{7,6},{8,9},{9,8},{10,11... | collective-permute-start | bytes 3145736 | tf_op jit(solution)/shard_map/ppermute | solution.py:70
  346.4 33.2 %collective-permute-start.24 = (bf16[2,2,2,192,512]{4,3,1,0,2:T(8,128)(2,1)S(1)}, bf16[2,2,2,192,512]{4,3,1,0,2:T(8,128)(2,1)S(1)}, u32[]{:S(2)}, u32[]{:S(2)}) collective-permute-start(bf16[2,2,2,192,512]{4,3,1,0,2:T(8,128)(2,1)S(1)} %pad_maximum_fusion.2), channel_id=1, source_target_pairs={{0,2},{2,0},{4,6},{6,4},{8,10},{10,8},{12,14},{14,12},{16,18},{18,... | collective-permute-start | bytes 4718600 | tf_op jit(solution)/shard_map/ppermute | solution.py:241
  349.1 31.2 %collective-permute-start.23 = (bf16[512,1024]{1,0:T(8,128)(2,1)S(1)}, bf16[512,1024]{1,0:T(8,128)(2,1)S(1)}, u32[]{:S(2)}, u32[]{:S(2)}) collective-permute-start(bf16[512,1024]{1,0:T(8,128)(2,1)S(1)} %add_convert_fusion.8), channel_id=1, source_target_pairs={{0,1},{1,0},{2,3},{3,2},{4,5},{5,4},{6,7},{7,6},{8,9},{9,8},{10,11... | collective-permute-start | bytes 3145736 | tf_op jit(solution)/shard_map/ppermute | solution.py:70
  408.5 45.6 %collective-permute-start.28 = (f32[36352]{0:T(1024)S(1)}, f32[36352]{0:T(1024)S(1)}, u32[]{:S(2)}, u32[]{:S(2)}) collective-permute-start(f32[36352]{0:T(1024)S(1)} %bitcast_dynamic-update-slice_fusion.10), channel_id=1, source_target_pairs={{0,2},{2,0},{4,6},{6,4},{8,10},{10,8},{12,14},{14,12},{16,18},{18,... | collective-permute-start | bytes 436232 | tf_op jit(solution)/shard_map/ppermute | solution.py:241
  411.7 34.9 %collective-permute-start.26 = (bf16[2,2,192,512]{3,2,1,0:T(8,128)(2,1)S(1)}, bf16[2,2,192,512]{3,2,1,0:T(8,128)(2,1)S(1)}, u32[]{:S(2)}, u32[]{:S(2)}) collective-permute-start(bf16[2,2,192,512]{3,2,1,0:T(8,128)(2,1)S(1)} %get-tuple-element.228), channel_id=1, source_target_pairs={{0,4},{2,6},{4,0},{6,2},{8,12},{10,14},{12,8},{14,10},{16,20},{18,... | collective-permute-start | bytes 2359304 | tf_op jit(solution)/shard_map/ppermute | solution.py:241
  413.5 33.4 %collective-permute-start.25 = (bf16[512,1024]{1,0:T(8,128)(2,1)S(1)}, bf16[512,1024]{1,0:T(8,128)(2,1)S(1)}, u32[]{:S(2)}, u32[]{:S(2)}) collective-permute-start(bf16[512,1024]{1,0:T(8,128)(2,1)S(1)} %add_convert_fusion.7), channel_id=1, source_target_pairs={{0,1},{1,0},{2,3},{3,2},{4,5},{5,4},{6,7},{7,6},{8,9},{9,8},{10,11... | collective-permute-start | bytes 3145736 | tf_op jit(solution)/shard_map/ppermute | solution.py:70
  454.2 31.2 %collective-permute-start.33 = (f32[36352]{0:T(1024)S(1)}, f32[36352]{0:T(1024)}, u32[]{:S(2)}, u32[]{:S(2)}) collective-permute-start(f32[36352]{0:T(1024)S(1)} %add.889), channel_id=1, source_target_pairs={{0,4},{2,6},{4,0},{6,2},{8,12},{10,14},{12,8},{14,10},{16,20},{18,... | collective-permute-start | bytes 436232 | tf_op jit(solution)/shard_map/ppermute | solution.py:241
  455.1 28.1 %collective-permute-start.32 = (bf16[2,2,2,256,512]{4,3,1,0,2:T(8,128)(2,1)S(1)}, bf16[2,2,2,256,512]{4,3,1,0,2:T(8,128)(2,1)S(1)}, u32[]{:S(2)}, u32[]{:S(2)}) collective-permute-start(bf16[2,2,2,256,512]{4,3,1,0,2:T(8,128)(2,1)S(1)} %bitcast_dynamic-update-slice_fusion), channel_id=1, source_target_pairs={{0,2},{2,0},{4,6},{6,4},{8,10},{10,8},{12,14},{14,12},{16,18},{18,... | collective-permute-start | bytes 6291464 | tf_op jit(solution)/shard_map/ppermute | solution.py:241
  455.2 16.0 %collective-permute-start.30 = (bf16[2,192,512]{2,1,0:T(8,128)(2,1)S(1)}, bf16[2,192,512]{2,1,0:T(8,128)(2,1)S(1)}, u32[]{:S(2)}, u32[]{:S(2)}) collective-permute-start(bf16[2,192,512]{2,1,0:T(8,128)(2,1)S(1)} %get-tuple-element.241), channel_id=1, source_target_pairs={{0,8},{2,10},{4,12},{6,14},{8,0},{10,2},{12,4},{14,6},{16,24},{18,... | collective-permute-start | bytes 1179656 | tf_op jit(solution)/shard_map/ppermute | solution.py:241
  456.9 28.5 %collective-permute-start.29 = (bf16[512,1024]{1,0:T(8,128)(2,1)}, bf16[512,1024]{1,0:T(8,128)(2,1)}, u32[]{:S(2)}, u32[]{:S(2)}) collective-permute-start(bf16[512,1024]{1,0:T(8,128)(2,1)} %add_convert_fusion.6), channel_id=1, source_target_pairs={{0,1},{1,0},{2,3},{3,2},{4,5},{5,4},{6,7},{7,6},{8,9},{9,8},{10,11... | collective-permute-start | bytes 3145736 | tf_op jit(solution)/shard_map/ppermute | solution.py:70
  471.3 11.8 %collective-permute-start.31 = (bf16[192,512]{1,0:T(8,128)(2,1)S(1)}, bf16[192,512]{1,0:T(8,128)(2,1)S(1)}, u32[]{:S(2)}, u32[]{:S(2)}) collective-permute-start(bf16[192,512]{1,0:T(8,128)(2,1)S(1)} %dynamic-slice_bitcast_fusion.20), channel_id=1, source_target_pairs={{0,16},{2,18},{4,20},{6,22},{8,24},{10,26},{12,28},{14,30},{16,0},... | collective-permute-start | bytes 589832 | tf_op jit(solution)/shard_map/ppermute | solution.py:241
  504.2 33.7 %collective-permute-start.38 = (bf16[2,2,2,128,1024]{4,3,1,0,2:T(8,128)(2,1)S(1)}, bf16[2,2,2,128,1024]{4,3,1,0,2:T(8,128)(2,1)S(1)}, u32[]{:S(2)}, u32[]{:S(2)}) collective-permute-start(bf16[2,2,2,128,1024]{4,3,1,0,2:T(8,128)(2,1)S(1)} %pad_maximum_fusion), channel_id=1, source_target_pairs={{0,2},{2,0},{4,6},{6,4},{8,10},{10,8},{12,14},{14,12},{16,18},{18,... | collective-permute-start | bytes 6291464 | tf_op jit(solution)/shard_map/ppermute | solution.py:241
  511.5 28.8 %collective-permute-start.37 = (bf16[2,2,2,128,1024]{4,3,2,1,0:T(8,128)(2,1)S(1)}, bf16[2,2,2,128,1024]{4,3,2,1,0:T(8,128)(2,1)S(1)}, u32[]{:S(2)}, u32[]{:S(2)}) collective-permute-start(bf16[2,2,2,128,1024]{4,3,2,1,0:T(8,128)(2,1)S(1)} %dynamic-slice_bitcast_fusion), channel_id=1, source_target_pairs={{0,2},{2,0},{4,6},{6,4},{8,10},{10,8},{12,14},{14,12},{16,18},{18,... | collective-permute-start | bytes 6291464 | tf_op jit(solution)/shard_map/ppermute | solution.py:241
  512.5 25.1 %collective-permute-start.35 = (bf16[2,2,256,512]{3,2,1,0:T(8,128)(2,1)S(1)}, bf16[2,2,256,512]{3,2,1,0:T(8,128)(2,1)S(1)}, u32[]{:S(2)}, u32[]{:S(2)}) collective-permute-start(bf16[2,2,256,512]{3,2,1,0:T(8,128)(2,1)S(1)} %copy-done.124), channel_id=1, source_target_pairs={{0,4},{2,6},{4,0},{6,2},{8,12},{10,14},{12,8},{14,10},{16,20},{18,... | collective-permute-start | bytes 3145736 | tf_op jit(solution)/shard_map/ppermute | solution.py:241
  515.1 26.3 %collective-permute-start.36 = (f32[36352]{0:T(1024)S(1)}, f32[36352]{0:T(1024)S(1)}, u32[]{:S(2)}, u32[]{:S(2)}) collective-permute-start(f32[36352]{0:T(1024)S(1)} %add.894), channel_id=1, source_target_pairs={{0,8},{2,10},{4,12},{6,14},{8,0},{10,2},{12,4},{14,6},{16,24},{18,... | collective-permute-start | bytes 436232 | tf_op jit(solution)/shard_map/ppermute | solution.py:241
  515.2 26.2 %collective-permute-start.34 = (bf16[256,1024]{1,0:T(8,128)(2,1)S(1)}, bf16[256,1024]{1,0:T(8,128)(2,1)S(1)}, u32[]{:S(2)}, u32[]{:S(2)}) collective-permute-start(bf16[256,1024]{1,0:T(8,128)(2,1)S(1)} %copy-done.128), channel_id=1, source_target_pairs={{0,1},{1,0},{2,3},{3,2},{4,5},{5,4},{6,7},{7,6},{8,9},{9,8},{10,11... | collective-permute-start | bytes 1572872 | tf_op jit(solution)/shard_map/ppermute | solution.py:70
  541.5 13.1 %collective-permute-start.40 = (bf16[2,256,512]{2,1,0:T(8,128)(2,1)S(1)}, bf16[2,256,512]{2,1,0:T(8,128)(2,1)S(1)}, u32[]{:S(2)}, u32[]{:S(2)}) collective-permute-start(bf16[2,256,512]{2,1,0:T(8,128)(2,1)S(1)} %get-tuple-element.252), channel_id=1, source_target_pairs={{0,8},{2,10},{4,12},{6,14},{8,0},{10,2},{12,4},{14,6},{16,24},{18,... | collective-permute-start | bytes 1572872 | tf_op jit(solution)/shard_map/ppermute | solution.py:241
  541.5 29.6 %collective-permute-start.43 = (bf16[2,2,128,1024]{3,2,1,0:T(8,128)(2,1)S(1)}, bf16[2,2,128,1024]{3,2,1,0:T(8,128)(2,1)S(1)}, u32[]{:S(2)}, u32[]{:S(2)}) collective-permute-start(bf16[2,2,128,1024]{3,2,1,0:T(8,128)(2,1)S(1)} %get-tuple-element.255), channel_id=1, source_target_pairs={{0,4},{2,6},{4,0},{6,2},{8,12},{10,14},{12,8},{14,10},{16,20},{18,... | collective-permute-start | bytes 3145736 | tf_op jit(solution)/shard_map/ppermute | solution.py:241
  554.7 16.3 %collective-permute-start.41 = (bf16[256,512]{1,0:T(8,128)(2,1)S(1)}, bf16[256,512]{1,0:T(8,128)(2,1)S(1)}, u32[]{:S(2)}, u32[]{:S(2)}) collective-permute-start(bf16[256,512]{1,0:T(8,128)(2,1)S(1)} %dynamic-slice_bitcast_fusion.19), channel_id=1, source_target_pairs={{0,16},{2,18},{4,20},{6,22},{8,24},{10,26},{12,28},{14,30},{16,0},... | collective-permute-start | bytes 786440 | tf_op jit(solution)/shard_map/ppermute | solution.py:241
  555.0 19.1 %collective-permute-start.42 = (f32[36352]{0:T(1024)S(1)}, f32[36352]{0:T(1024)S(1)}, u32[]{:S(2)}, u32[]{:S(2)}) collective-permute-start(f32[36352]{0:T(1024)S(1)} %add.901), channel_id=1, source_target_pairs={{0,16},{2,18},{4,20},{6,22},{8,24},{10,26},{12,28},{14,30},{16,0},... | collective-permute-start | bytes 436232 | tf_op jit(solution)/shard_map/ppermute | solution.py:241
  557.8 16.3 %collective-permute-start.39 = (bf16[256,1024]{1,0:T(8,128)(2,1)S(1)}, bf16[256,1024]{1,0:T(8,128)(2,1)S(1)}, u32[]{:S(2)}, u32[]{:S(2)}) collective-permute-start(bf16[256,1024]{1,0:T(8,128)(2,1)S(1)} %dynamic-slice_convert_fusion), channel_id=1, source_target_pairs={{0,1},{1,0},{2,3},{3,2},{4,5},{5,4},{6,7},{7,6},{8,9},{9,8},{10,11... | collective-permute-start | bytes 1572872 | tf_op jit(solution)/shard_map/ppermute | solution.py:70
  575.7 174.5 %all-gather.5.cloned.1.call-start = ((), (), s32[]{:S(2)}) async-start(), calls=%async_computation | async-start | bytes 8912896 | tf_op jit(solution)/shard_map/all_gather | solution.py:310
  577.5 30.0 %collective-permute-start.47 = (bf16[2,2,128,1024]{3,2,1,0:T(8,128)(2,1)S(1)}, bf16[2,2,128,1024]{3,2,1,0:T(8,128)(2,1)S(1)}, u32[]{:S(2)}, u32[]{:S(2)}) collective-permute-start(bf16[2,2,128,1024]{3,2,1,0:T(8,128)(2,1)S(1)} %copy-done.123), channel_id=1, source_target_pairs={{0,4},{2,6},{4,0},{6,2},{8,12},{10,14},{12,8},{14,10},{16,20},{18,... | collective-permute-start | bytes 3145736 | tf_op jit(solution)/shard_map/ppermute | solution.py:241
  579.0 29.1 %collective-permute-start.45 = (bf16[2,128,1024]{2,1,0:T(8,128)(2,1)S(1)}, bf16[2,128,1024]{2,1,0:T(8,128)(2,1)S(1)}, u32[]{:S(2)}, u32[]{:S(2)}) collective-permute-start(bf16[2,128,1024]{2,1,0:T(8,128)(2,1)S(1)} %copy-done.129), channel_id=1, source_target_pairs={{0,8},{2,10},{4,12},{6,14},{8,0},{10,2},{12,4},{14,6},{16,24},{18,... | collective-permute-start | bytes 1572872 | tf_op jit(solution)/shard_map/ppermute | solution.py:241
  583.7 24.4 %collective-permute-start.44 = (f32[2,1024]{1,0:T(2,128)S(1)}, f32[2,1024]{1,0:T(2,128)S(1)}, u32[]{:S(2)}, u32[]{:S(2)}) collective-permute-start(f32[2,1024]{1,0:T(2,128)S(1)} %maximum_add_fusion.1), channel_id=1, source_target_pairs={{31,30},{30,31},{29,28},{28,29},{27,26},{26,27},{25,24},{24,25},{2... | collective-permute-start | bytes 24584 | tf_op jit(solution)/shard_map/ppermute | solution.py:86
  608.3 25.8 %collective-permute-start.46 = (bf16[128,1024]{1,0:T(8,128)(2,1)S(1)}, bf16[128,1024]{1,0:T(8,128)(2,1)S(1)}, u32[]{:S(2)}, u32[]{:S(2)}) collective-permute-start(bf16[128,1024]{1,0:T(8,128)(2,1)S(1)} %dynamic-slice_bitcast_fusion.18), channel_id=1, source_target_pairs={{0,16},{2,18},{4,20},{6,22},{8,24},{10,26},{12,28},{14,30},{16,0},... | collective-permute-start | bytes 786440 | tf_op jit(solution)/shard_map/ppermute | solution.py:241
  608.5 25.8 %collective-permute-start.48 = (f32[7168]{0:T(1024)S(1)}, f32[7168]{0:T(1024)S(1)}, u32[]{:S(2)}, u32[]{:S(2)}) collective-permute-start(f32[7168]{0:T(1024)S(1)} %constant_dynamic-update-slice_fusion.3), channel_id=1, source_target_pairs={{0,2},{2,0},{4,6},{6,4},{8,10},{10,8},{12,14},{14,12},{16,18},{18,... | collective-permute-start | bytes 86024 | tf_op jit(solution)/shard_map/ppermute | solution.py:241
  634.3 25.1 %collective-permute-start.49 = (bf16[2,128,1024]{2,1,0:T(8,128)(2,1)S(1)}, bf16[2,128,1024]{2,1,0:T(8,128)(2,1)S(1)}, u32[]{:S(2)}, u32[]{:S(2)}) collective-permute-start(bf16[2,128,1024]{2,1,0:T(8,128)(2,1)S(1)} %get-tuple-element.263), channel_id=1, source_target_pairs={{0,8},{2,10},{4,12},{6,14},{8,0},{10,2},{12,4},{14,6},{16,24},{18,... | collective-permute-start | bytes 1572872 | tf_op jit(solution)/shard_map/ppermute | solution.py:241
  659.7 13.8 %collective-permute-start.50 = (bf16[128,1024]{1,0:T(8,128)(2,1)S(1)}, bf16[128,1024]{1,0:T(8,128)(2,1)S(1)}, u32[]{:S(2)}, u32[]{:S(2)}) collective-permute-start(bf16[128,1024]{1,0:T(8,128)(2,1)S(1)} %dynamic-slice_bitcast_fusion.17), channel_id=1, source_target_pairs={{0,16},{2,18},{4,20},{6,22},{8,24},{10,26},{12,28},{14,30},{16,0},... | collective-permute-start | bytes 786440 | tf_op jit(solution)/shard_map/ppermute | solution.py:241
  660.6 13.0 %collective-permute-start.51 = (f32[7168]{0:T(1024)S(1)}, f32[7168]{0:T(1024)S(1)}, u32[]{:S(2)}, u32[]{:S(2)}) collective-permute-start(f32[7168]{0:T(1024)S(1)} %add.914), channel_id=1, source_target_pairs={{0,4},{2,6},{4,0},{6,2},{8,12},{10,14},{12,8},{14,10},{16,20},{18,... | collective-permute-start | bytes 86024 | tf_op jit(solution)/shard_map/ppermute | solution.py:241
  (214 other events, 2129.4 us)
Sparse Core Ops, SparseCore 0:
  291.4 171.5 all-reduce.4
  575.9 78.0 all-gather.6
  674.6 75.6 all-gather.4

commit v3 on v2

--- a/solution.py
+++ b/solution.py
@@ -187,13 +187,18 @@
 
     def run(self, clips):
         under_way = None
-        got = {}
+        arrived = {}
 
         def settle(held, jobs=True):
             extra = [] if under_way is None else [under_way[1].sent, under_way[2]]
+            if under_way is not None:
+                arrived[under_way[0]] = (under_way[1], *extra)
+            waiting = list(arrived)
+            extra = [value for place in waiting for value in arrived[place][1:]]
             out, moved = self.turn(held + extra, jobs)
-            if under_way is not None:
-                got[under_way[0]] = under_way[1].finish(out[-2], out[-1])
+            for index, place in enumerate(waiting):
+                begin = len(held) + 2 * index
+                arrived[place] = (arrived[place][0], *out[begin : begin + 2])
             for job, values in moved:
                 job.advance(values)
             return out[: len(held)]
@@ -207,7 +212,8 @@
                 under_way = None
             try:
                 if place in started:
-                    request = clips[place].send(got.pop(place))
+                    earlier, sent, got = arrived.pop(place)
+                    request = clips[place].send(earlier.finish(sent, got))
                 else:
                     started.add(place)
                     request = next(clips[place])
@@ -295,7 +301,7 @@
 def sum_job(make):
     values = yield [narrow(value) for value in make()]
     summed = [lax.psum(value, "dp") for value in values]
-    for _ in range(4):
+    for _ in range(5):
         yield []
     return (yield summed)
 
@@ -1049,11 +1055,6 @@
             lows[0].shape[1],
         )
         grads.sums("attend_sums", [query_sum, value_sum, output_sum, table_sum])
-        if slot == slots[-1]:
-            grads.parts["final"] = [
-                list(wide_sum(total([jnp.stack(part) for part in grads.parts["final"]])))
-            ]
-            grads.reduce_sums("early", ["final", "second", "convolve_sums", "attend_sums"])
         grads.gather("middle", ["convolve", "attend"])
         normed_grad = yield Summed(share)
         grad, gain_grad, shift_grad = residual_back(grad, normed_grad, attend_kept, attend_gain)
@@ -1063,7 +1064,7 @@
             grad, first_kept, first_up_weight, first_down_weight
         )
         grads.weights("first_down", [(first_kept[5], spread)], spread.shape[1], eager=True)
-        grads.weights("first_up", [(first_kept[3], before_low)], spread.shape[1], 1, eager=True)
+        grads.weights("first_up", [(first_kept[3], before_low)], spread.shape[1], 0, eager=True)
         grads.gather("first_both", ["first_down", "first_up"])
         normed_grad = yield Scattered(share)
         input_grads[slot], gain_grad, shift_grad = residual_back(
@@ -1076,19 +1077,47 @@
         grads.sums("first_norm", [gain_grad, shift_grad])
 
     flow.run([clip(slot) for slot in slots])
-    grads.parts["first_norm"] = [
-        list(wide_sum(total([jnp.stack(part) for part in grads.parts["first_norm"]])))
+    own = [
+        total([part[place] for part in grads.parts[group]])
+        for group, place in (
+            ("final", 0),
+            ("final", 1),
+            ("first_norm", 0),
+            ("first_norm", 1),
+            ("attend_sums", 3),
+        )
     ]
-    grads.reduce_sums("late", ["attend_norm", "first", "first_norm"])
+    flat = wide_sum(jnp.concatenate([value.reshape(-1) for value in own]))
+    shared = []
+    for value in own:
+        shared.append(flat[: value.size].reshape(value.shape))
+        flat = flat[value.size :]
+    grads.parts["final"] = [shared[:2]]
+    grads.parts["first_norm"] = [shared[2:4]]
+    grads.parts["attend_sums"] = [
+        [total([part[place] for part in grads.parts["attend_sums"]]) for place in range(3)]
+        + shared[4:]
+    ]
+    grads.reduce_sums(
+        "sums",
+        [
+            "final",
+            "second",
+            "convolve_sums",
+            "attend_sums",
+            "attend_norm",
+            "first",
+            "first_norm",
+        ],
+    )
     flow.drain()
 
     clips = count_job.result[0][0, 0]
-    early = grads.result("early")
-    late = grads.result("late")
+    early, late = grads.result("sums")[:15], grads.result("sums")[15:]
     second_down, second_up = grads.result("second_both")
     linear, gating, point_out, output_grad, query_grad, key_grad, value_grad = grads.result("middle")
     first_down, first_up = grads.result("first_both")
-    table_grad = wide_sum(early[14]).T[: relative_table.shape[0]]
+    table_grad = early[14].T[: relative_table.shape[0]]
     every = (
         late[4],
         late[5],

time: 778 us -> 765 us (0.983)
  starting transfers between devices: 63.3 us -> 53.2 us
  local copies, waits for them, and re-layouts: 50.5 us -> 40.7 us
    unnamed x423 -> x390, local copies, waits for them, and re-layouts: 34.6 us -> 24.8 us
    ppermute x20, waiting for transfers between devices: 103 us -> 112 us  [swap(): return lax.ppermute(values, 'tensor', [(0, 1), (1, 0)])]
    ppermute x28 -> x24, starting transfers between devices: 25 us -> 20.4 us  [dp_swap(): lax.ppermute(values, 'dp', [(place, place ^ bit) for place in range(16)])]
    div x15 -> x13, other arithmetic: 36.4 us -> 35.3 us  [per_device(): widen(value) / clips]
    ppermute x28 -> x24, waiting for transfers between devices: 182 us -> 183 us  [dp_swap(): lax.ppermute(values, 'dp', [(place, place ^ bit) for place in range(16)])]
  transfers between devices with their start and end apart: 58 -> 52, of which waited for: 30 -> 34; matrix products, arithmetic and copies ran while one was open for 20% -> 22% of each run, Pallas kernels for 15% -> 16%
where the time goes in v3:
time: 765 us; the launch traced here: 755 us
  waiting for transfers between devices  331 us (43%)
  Pallas kernels  120 us (16%)
  other arithmetic  106 us (14%)
  matrix products  86.5 us (11%)
  starting transfers between devices  53.2 us (7%)
  local copies, waits for them, and re-layouts  40.7 us (5%)
  between operations  18.3 us (2%)
    ppermute x24, waiting for transfers between devices, dp_swap(): lax.ppermute(values, 'dp', [(place, place ^ bit) for place in range(16)])  183 us
    ppermute x20, waiting for transfers between devices, swap(): return lax.ppermute(values, 'tensor', [(0, 1), (1, 0)])  112 us
    dot_general x22, matrix products, product_right(): lax.dot_general(left, right, (((1,), (1,)), ((), ())), preferred_element_...  49.9 us
    pallas_call x2, Pallas kernels, attend_heads_back(): pl.pallas_call(attend_back_kernel, out_shape=(jax.ShapeDtypeStruct((lengt...  41.5 us
    dot_general x22, matrix products, product(): return jnp.dot(left, right, preferred_element_type=jnp.float32)  36.6 us
    div x13, other arithmetic, per_device(): widen(value) / clips  35.3 us
    pallas_call x11, Pallas kernels, weight_grad(): pl.pallas_call(functools.partial(weight_grad_kernel, len(lefts)), out_sha...  30.4 us
    all_gather x2, waiting for transfers between devices, gather_job(): whole = lax.all_gather(shards, 'dp', axis=0)  27.9 us
  transfers between devices with their start and end apart: 52, of which 34 were waited for; matrix products, arithmetic and copies ran while one was open for 22% of the time, Pallas kernels for 16%

profile of v3, /device:TPU:0, one launch (start us, length us, event | category | flops | bytes accessed | tf_op | source)
XLA Modules:
  0.0 755.5 jit_solution(11517800069354850989)
XLA Ops:
  16.6 8.5 %collective-permute-done.1 = bf16[256,1024]{1,0:T(8,128)(2,1)S(1)} collective-permute-done((bf16[256,1024]{1,0:T(8,128)(2,1)S(1)}, bf16[256,1024]{1,0:T(8,128)(2,1)S(1)}, u32[]{:S(2)}, u32[]{:S(2)}) %collective-permute-start.1) | collective-permute-done | bytes 524320 | tf_op jit(solution)/shard_map/ppermute | solution.py:70
  29.8 4.8 multiply_convert_fusion.3
  36.9 4.1 collective-permute-done.3
  43.8 4.8 multiply_convert_fusion.2
  53.7 12.2 %collective-permute-done.5 = bf16[512,1024]{1,0:T(8,128)(2,1)S(1)} collective-permute-done((bf16[512,1024]{1,0:T(8,128)(2,1)S(1)}, bf16[512,1024]{1,0:T(8,128)(2,1)S(1)}, u32[]{:S(2)}, u32[]{:S(2)}) %collective-permute-start.5) | collective-permute-done | bytes 1048608 | tf_op jit(solution)/shard_map/ppermute | solution.py:70
  73.2 13.8 %attend_heads.2.refs_0_ = bf16[512,512]{1,0:T(8,128)(2,1)S(1)} custom-call(bf16[512,512]{1,0:T(8,128)(2,1)S(1)} %fusion.25.query_ref, bf16[512,512]{1,0:T(8,128)(2,1)S(1)} %convolution_convert_fusion.11.key_ref, bf16[512,512]{1,0:T(8,128)(2,1)S(1)} %fusion.26.value_ref, bf16[128,128]{1,0:T(8,128)(2,1)S(1)} %copy.76.table_ref), custom_call_target="tpu_custom_call" | custom-call | tf_op jit(solution)/shard_map/attend_heads/pallas_call | solution.py:529
  95.2 13.8 %attend_heads.3.refs_2_ = bf16[512,512]{1,0:T(8,128)(2,1)S(1)} custom-call(bf16[512,512]{1,0:T(8,128)(2,1)S(1)} %fusion.27.query_ref, bf16[512,512]{1,0:T(8,128)(2,1)S(1)} %convolution_convert_fusion.10.key_ref, bf16[512,512]{1,0:T(8,128)(2,1)S(1)} %fusion.28.value_ref, bf16[128,128]{1,0:T(8,128)(2,1)S(1)} %copy.76.table_ref), custom_call_target="tpu_custom_call" | custom-call | tf_op jit(solution)/shard_map/attend_heads/pallas_call | solution.py:529
  109.9 4.0 collective-permute-done.8
  118.3 4.3 mix_channels.2
  122.7 13.1 %collective-permute-done.9 = bf16[512,1024]{1,0:T(8,128)(2,1)S(1)} collective-permute-done((bf16[512,1024]{1,0:T(8,128)(2,1)S(1)}, bf16[512,1024]{1,0:T(8,128)(2,1)S(1)}, u32[]{:S(2)}, u32[]{:S(2)}) %collective-permute-start.9) | collective-permute-done | bytes 1048608 | tf_op jit(solution)/shard_map/ppermute | solution.py:70
  145.9 4.2 mix_channels.3
  151.0 10.6 %collective-permute-done.11 = bf16[512,1024]{1,0:T(8,128)(2,1)S(1)} collective-permute-done((bf16[512,1024]{1,0:T(8,128)(2,1)S(1)}, bf16[512,1024]{1,0:T(8,128)(2,1)S(1)}, u32[]{:S(2)}, u32[]{:S(2)}) %collective-permute-start.11) | collective-permute-done | bytes 1048608 | tf_op jit(solution)/shard_map/ppermute | solution.py:70
  173.0 4.8 multiply_convert_fusion.1
  180.2 9.4 %collective-permute-done.13 = bf16[512,1024]{1,0:T(8,128)(2,1)S(1)} collective-permute-done((bf16[512,1024]{1,0:T(8,128)(2,1)S(1)}, bf16[512,1024]{1,0:T(8,128)(2,1)S(1)}, u32[]{:S(2)}, u32[]{:S(2)}) %collective-permute-start.13) | collective-permute-done | bytes 1048608 | tf_op jit(solution)/shard_map/ppermute | solution.py:70
  197.8 10.1 %collective-permute-done.14 = bf16[256,1024]{1,0:T(8,128)(2,1)S(1)} collective-permute-done((bf16[256,1024]{1,0:T(8,128)(2,1)S(1)}, bf16[256,1024]{1,0:T(8,128)(2,1)S(1)}, u32[]{:S(2)}, u32[]{:S(2)}) %collective-permute-start.14) | collective-permute-done | bytes 524320 | tf_op jit(solution)/shard_map/ppermute | solution.py:70
  212.9 8.9 %collective-permute-done.15 = bf16[256,1024]{1,0:T(8,128)(2,1)S(1)} collective-permute-done((bf16[256,1024]{1,0:T(8,128)(2,1)S(1)}, bf16[256,1024]{1,0:T(8,128)(2,1)S(1)}, u32[]{:S(2)}, u32[]{:S(2)}) %collective-permute-start.15) | collective-permute-done | bytes 524320 | tf_op jit(solution)/shard_map/ppermute | solution.py:70
  226.3 7.0 collective-permute-done.16
  233.7 6.6 fusion.88
  245.2 9.9 %collective-permute-done.17 = bf16[256,1024]{1,0:T(8,128)(2,1)S(1)} collective-permute-done((bf16[256,1024]{1,0:T(8,128)(2,1)S(1)}, bf16[256,1024]{1,0:T(8,128)(2,1)S(1)}, u32[]{:S(2)}, u32[]{:S(2)}) %collective-permute-start.17) | collective-permute-done | bytes 524320 | tf_op jit(solution)/shard_map/ppermute | solution.py:70
  256.8 4.8 fusion.87
  261.6 5.4 weight_grad.12
  269.3 5.3 weight_grad.11
  276.6 6.3 convolution_convert_fusion.4
  297.8 6.0 mix_channels_back.2
  305.3 9.8 %collective-permute-done.20 = bf16[512,1024]{1,0:T(8,128)(2,1)} collective-permute-done((bf16[512,1024]{1,0:T(8,128)(2,1)}, bf16[512,1024]{1,0:T(8,128)(2,1)}, u32[]{:S(2)}, u32[]{:S(2)}) %collective-permute-start.20) | collective-permute-done | bytes 1048608 | tf_op jit(solution)/shard_map/ppermute | solution.py:70
  327.8 6.2 mix_channels_back.3
  346.2 20.8 %attend_heads_back.2 = (bf16[512,512]{1,0:T(8,128)(2,1)S(1)}, bf16[512,512]{1,0:T(8,128)(2,1)S(1)}, bf16[512,512]{1,0:T(8,128)(2,1)S(1)}, f32[1,512]{1,0:T(1,128...) custom-call(bf16[512,512]{1,0:T(8,128)(2,1)S(1)} %copy-done.40, bf16[512,512]{1,0:T(8,128)(2,1)S(1)} %copy-done.38, ...), custom_call_target="tpu_custom_call" | custom-call | tf_op jit(solution)/shard_map/attend_heads_back/pallas_call | solution.py:548
  382.6 20.6 %attend_heads_back.3 = (bf16[512,512]{1,0:T(8,128)(2,1)S(1)}, bf16[512,512]{1,0:T(8,128)(2,1)S(1)}, bf16[512,512]{1,0:T(8,128)(2,1)S(1)}, f32[1,512]{1,0:T(1,128...) custom-call(bf16[512,512]{1,0:T(8,128)(2,1)S(1)} %copy-done.36, bf16[512,512]{1,0:T(8,128)(2,1)S(1)} %copy-done.32, ...), custom_call_target="tpu_custom_call" | custom-call | tf_op jit(solution)/shard_map/attend_heads_back/pallas_call | solution.py:548
  403.3 4.2 collective-permute-done.26
  419.9 6.3 fusion.86
  429.9 4.6 collective-permute-done.28
  437.3 13.3 %collective-permute-done.29 = bf16[192,512]{1,0:T(8,128)(2,1)S(1)} collective-permute-done((bf16[192,512]{1,0:T(8,128)(2,1)S(1)}, bf16[192,512]{1,0:T(8,128)(2,1)S(1)}, u32[]{:S(2)}, u32[]{:S(2)}) %collective-permute-start.29) | collective-permute-done | bytes 196640 | tf_op jit(solution)/shard_map/ppermute | solution.py:247
  462.1 5.3 weight_grad.21
  470.8 5.5 weight_grad.20
  481.7 20.4 %collective-permute-done.32 = bf16[2,2,256,512]{3,2,1,0:T(8,128)(2,1)S(1)} collective-permute-done((bf16[2,2,256,512]{3,2,1,0:T(8,128)(2,1)S(1)}, bf16[2,2,256,512]{3,2,1,0:T(8,128)(2,1)S(1)}, u32[]{:S(2)}, u32[]{:S(2)}) %collective-permute-start.32) | collective-permute-done | bytes 1048608 | tf_op jit(solution)/shard_map/ppermute | solution.py:247
  510.3 11.6 %collective-permute-done.36 = bf16[2,256,512]{2,1,0:T(8,128)(2,1)S(1)} collective-permute-done((bf16[2,256,512]{2,1,0:T(8,128)(2,1)}, bf16[2,256,512]{2,1,0:T(8,128)(2,1)S(1)}, u32[]{:S(2)}, u32[]{:S(2)}) %collective-permute-start.36) | collective-permute-done | bytes 524320 | tf_op jit(solution)/shard_map/ppermute | solution.py:247
  524.5 12.2 %collective-permute-done.37 = bf16[256,512]{1,0:T(8,128)(2,1)S(1)} collective-permute-done((bf16[256,512]{1,0:T(8,128)(2,1)S(1)}, bf16[256,512]{1,0:T(8,128)(2,1)S(1)}, u32[]{:S(2)}, u32[]{:S(2)}) %collective-permute-start.37) | collective-permute-done | bytes 262176 | tf_op jit(solution)/shard_map/ppermute | solution.py:247
  538.3 17.4 %collective-permute-done.38 = bf16[2,2,128,1024]{3,2,1,0:T(8,128)(2,1)S(1)} collective-permute-done((bf16[2,2,128,1024]{3,2,1,0:T(8,128)(2,1)}, bf16[2,2,128,1024]{3,2,1,0:T(8,128)(2,1)S(1)}, u32[]{:S(2)}, u32[]{:S(2)}) %collective-permute-start.38) | collective-permute-done | bytes 1048608 | tf_op jit(solution)/shard_map/ppermute | solution.py:247
  576.9 18.3 %collective-permute-done.43 = bf16[2,128,1024]{2,1,0:T(8,128)(2,1)S(1)} collective-permute-done((bf16[2,128,1024]{2,1,0:T(8,128)(2,1)}, bf16[2,128,1024]{2,1,0:T(8,128)(2,1)S(1)}, u32[]{:S(2)}, u32[]{:S(2)}) %collective-permute-start.43) | collective-permute-done | bytes 524320 | tf_op jit(solution)/shard_map/ppermute | solution.py:247
  595.6 25.1 %collective-permute-done.41 = bf16[2,128,1024]{2,1,0:T(8,128)(2,1)S(1)} collective-permute-done((bf16[2,128,1024]{2,1,0:T(8,128)(2,1)}, bf16[2,128,1024]{2,1,0:T(8,128)(2,1)S(1)}, u32[]{:S(2)}, u32[]{:S(2)}) %collective-permute-start.41) | collective-permute-done | bytes 524320 | tf_op jit(solution)/shard_map/ppermute | solution.py:247
  621.4 26.5 %collective-permute-done.42 = bf16[128,1024]{1,0:T(8,128)(2,1)S(1)} collective-permute-done((bf16[128,1024]{1,0:T(8,128)(2,1)S(1)}, bf16[128,1024]{1,0:T(8,128)(2,1)S(1)}, u32[]{:S(2)}, u32[]{:S(2)}) %collective-permute-start.42) | collective-permute-done | bytes 262176 | tf_op jit(solution)/shard_map/ppermute | solution.py:247
  649.9 7.2 convert_divide_fusion
  657.2 5.5 convert_divide_fusion.1
  665.2 7.5 collective-permute-done.46
  672.8 12.8 %collective-permute-done.47 = f32[43520]{0:T(1024)S(1)} collective-permute-done((f32[43520]{0:T(1024)S(1)}, f32[43520]{0:T(1024)S(1)}, u32[]{:S(2)}, u32[]{:S(2)}) %collective-permute-start.47) | collective-permute-done | bytes 174112 | tf_op jit(solution)/shard_map/ppermute | solution.py:247
  688.1 6.8 collective-permute-done.48
  709.3 27.9 %all-gather.5.cloned.1.call-done = bf16[4096,1024]{1,0:T(8,128)(2,1)} async-done(((bf16[256,1024]{1,0:T(8,128)(2,1)}), bf16[4096,1024]{1,0:T(8,128)(2,1)}) %all-gather.5.cloned.1.call-update) | async-done | bytes 8388624 | tf_op jit(solution)/shard_map/all_gather | solution.py:316
  737.2 7.0 convert_divide_fusion.2
  (775 shorter events, 251.6 us)
Async XLA Ops:
  7.4 500.9 %all-reduce.5.cloned.1.call-start = ((), (), s32[]{:S(2)}) async-start(), calls=%async_computation.2 | async-start | bytes 16777216 | tf_op jit(solution)/shard_map/psum | solution.py:303
  9.9 15.2 %collective-permute-start.1 = (bf16[256,1024]{1,0:T(8,128)(2,1)S(1)}, bf16[256,1024]{1,0:T(8,128)(2,1)S(1)}, u32[]{:S(2)}, u32[]{:S(2)}) collective-permute-start(bf16[256,1024]{1,0:T(8,128)(2,1)S(1)} %get-tuple-element.160), channel_id=1, source_target_pairs={{0,1},{1,0},{2,3},{3,2},{4,5},{5,4},{6,7},{7,6},{8,9},{9,8},{10,11... | collective-permute-start | bytes 1572872 | tf_op jit(solution)/shard_map/ppermute | solution.py:70
  25.9 11.0 %collective-permute-start.4 = (f32[128]{0:T(128)S(1)}, f32[128]{0:T(128)S(1)}, u32[]{:S(2)}, u32[]{:S(2)}) collective-permute-start(f32[128]{0:T(128)S(1)} %fusion.180), channel_id=1, source_target_pairs={{0,8},{2,10},{4,12},{6,14},{8,0},{10,2},{12,4},{14,6},{16,24},{18,... | collective-permute-start | bytes 1544 | tf_op jit(solution)/shard_map/ppermute | solution.py:247
  27.8 13.3 %collective-permute-start.3 = (bf16[256,1024]{1,0:T(8,128)(2,1)S(1)}, bf16[256,1024]{1,0:T(8,128)(2,1)S(1)}, u32[]{:S(2)}, u32[]{:S(2)}) collective-permute-start(bf16[256,1024]{1,0:T(8,128)(2,1)S(1)} %get-tuple-element.164), channel_id=1, source_target_pairs={{0,1},{1,0},{2,3},{3,2},{4,5},{5,4},{6,7},{7,6},{8,9},{9,8},{10,11... | collective-permute-start | bytes 1572872 | tf_op jit(solution)/shard_map/ppermute | solution.py:70
  42.3 23.6 %collective-permute-start.5 = (bf16[512,1024]{1,0:T(8,128)(2,1)S(1)}, bf16[512,1024]{1,0:T(8,128)(2,1)S(1)}, u32[]{:S(2)}, u32[]{:S(2)}) collective-permute-start(bf16[512,1024]{1,0:T(8,128)(2,1)S(1)} %convolution_convert_fusion.7), channel_id=1, source_target_pairs={{0,1},{1,0},{2,3},{3,2},{4,5},{5,4},{6,7},{7,6},{8,9},{9,8},{10,11... | collective-permute-start | bytes 3145736 | tf_op jit(solution)/shard_map/ppermute | solution.py:70
  48.7 5.0 collective-permute-start.6
  67.0 22.7 %collective-permute-start.7 = (bf16[512,1024]{1,0:T(8,128)(2,1)S(1)}, bf16[512,1024]{1,0:T(8,128)(2,1)S(1)}, u32[]{:S(2)}, u32[]{:S(2)}) collective-permute-start(bf16[512,1024]{1,0:T(8,128)(2,1)S(1)} %convolution_convert_fusion.6), channel_id=1, source_target_pairs={{0,1},{1,0},{2,3},{3,2},{4,5},{5,4},{6,7},{7,6},{8,9},{9,8},{10,11... | collective-permute-start | bytes 3145736 | tf_op jit(solution)/shard_map/ppermute | solution.py:70
  91.5 22.4 %collective-permute-start.8 = (bf16[512,1024]{1,0:T(8,128)(2,1)S(1)}, bf16[512,1024]{1,0:T(8,128)(2,1)S(1)}, u32[]{:S(2)}, u32[]{:S(2)}) collective-permute-start(bf16[512,1024]{1,0:T(8,128)(2,1)S(1)} %convolution_convert_fusion.3), channel_id=1, source_target_pairs={{0,1},{1,0},{2,3},{3,2},{4,5},{5,4},{6,7},{7,6},{8,9},{9,8},{10,11... | collective-permute-start | bytes 3145736 | tf_op jit(solution)/shard_map/ppermute | solution.py:70
  114.8 21.0 %collective-permute-start.9 = (bf16[512,1024]{1,0:T(8,128)(2,1)S(1)}, bf16[512,1024]{1,0:T(8,128)(2,1)S(1)}, u32[]{:S(2)}, u32[]{:S(2)}) collective-permute-start(bf16[512,1024]{1,0:T(8,128)(2,1)S(1)} %convolution_convert_fusion.2), channel_id=1, source_target_pairs={{0,1},{1,0},{2,3},{3,2},{4,5},{5,4},{6,7},{7,6},{8,9},{9,8},{10,11... | collective-permute-start | bytes 3145736 | tf_op jit(solution)/shard_map/ppermute | solution.py:70
  142.4 19.2 %collective-permute-start.11 = (bf16[512,1024]{1,0:T(8,128)(2,1)S(1)}, bf16[512,1024]{1,0:T(8,128)(2,1)S(1)}, u32[]{:S(2)}, u32[]{:S(2)}) collective-permute-start(bf16[512,1024]{1,0:T(8,128)(2,1)S(1)} %convolution_convert_fusion.1), channel_id=1, source_target_pairs={{0,1},{1,0},{2,3},{3,2},{4,5},{5,4},{6,7},{7,6},{8,9},{9,8},{10,11... | collective-permute-start | bytes 3145736 | tf_op jit(solution)/shard_map/ppermute | solution.py:70
  170.4 19.2 %collective-permute-start.13 = (bf16[512,1024]{1,0:T(8,128)(2,1)S(1)}, bf16[512,1024]{1,0:T(8,128)(2,1)S(1)}, u32[]{:S(2)}, u32[]{:S(2)}) collective-permute-start(bf16[512,1024]{1,0:T(8,128)(2,1)S(1)} %convolution_convert_fusion), channel_id=1, source_target_pairs={{0,1},{1,0},{2,3},{3,2},{4,5},{5,4},{6,7},{7,6},{8,9},{9,8},{10,11... | collective-permute-start | bytes 3145736 | tf_op jit(solution)/shard_map/ppermute | solution.py:70
  193.7 14.1 %collective-permute-start.14 = (bf16[256,1024]{1,0:T(8,128)(2,1)S(1)}, bf16[256,1024]{1,0:T(8,128)(2,1)S(1)}, u32[]{:S(2)}, u32[]{:S(2)}) collective-permute-start(bf16[256,1024]{1,0:T(8,128)(2,1)S(1)} %dynamic-slice_convert_fusion.3), channel_id=1, source_target_pairs={{0,1},{1,0},{2,3},{3,2},{4,5},{5,4},{6,7},{7,6},{8,9},{9,8},{10,11... | collective-permute-start | bytes 1572872 | tf_op jit(solution)/shard_map/ppermute | solution.py:70
  208.5 13.4 %collective-permute-start.15 = (bf16[256,1024]{1,0:T(8,128)(2,1)S(1)}, bf16[256,1024]{1,0:T(8,128)(2,1)S(1)}, u32[]{:S(2)}, u32[]{:S(2)}) collective-permute-start(bf16[256,1024]{1,0:T(8,128)(2,1)S(1)} %dynamic-slice_convert_fusion.2), channel_id=1, source_target_pairs={{0,1},{1,0},{2,3},{3,2},{4,5},{5,4},{6,7},{7,6},{8,9},{9,8},{10,11... | collective-permute-start | bytes 1572872 | tf_op jit(solution)/shard_map/ppermute | solution.py:70
  222.4 10.9 %collective-permute-start.16 = (bf16[256,1024]{1,0:T(8,128)(2,1)S(1)}, bf16[256,1024]{1,0:T(8,128)(2,1)S(1)}, u32[]{:S(2)}, u32[]{:S(2)}) collective-permute-start(bf16[256,1024]{1,0:T(8,128)(2,1)S(1)} %multiply_convert_fusion.8), channel_id=1, source_target_pairs={{0,1},{1,0},{2,3},{3,2},{4,5},{5,4},{6,7},{7,6},{8,9},{9,8},{10,11... | collective-permute-start | bytes 1572872 | tf_op jit(solution)/shard_map/ppermute | solution.py:70
  240.3 14.9 %collective-permute-start.17 = (bf16[256,1024]{1,0:T(8,128)(2,1)S(1)}, bf16[256,1024]{1,0:T(8,128)(2,1)S(1)}, u32[]{:S(2)}, u32[]{:S(2)}) collective-permute-start(bf16[256,1024]{1,0:T(8,128)(2,1)S(1)} %get-tuple-element.205), channel_id=1, source_target_pairs={{0,1},{1,0},{2,3},{3,2},{4,5},{5,4},{6,7},{7,6},{8,9},{9,8},{10,11... | collective-permute-start | bytes 1572872 | tf_op jit(solution)/shard_map/ppermute | solution.py:70
  255.2 27.7 %collective-permute-start.18 = (bf16[512,1024]{1,0:T(8,128)(2,1)}, bf16[512,1024]{1,0:T(8,128)(2,1)}, u32[]{:S(2)}, u32[]{:S(2)}) collective-permute-start(bf16[512,1024]{1,0:T(8,128)(2,1)} %convolution_convert_fusion.5), channel_id=1, source_target_pairs={{0,1},{1,0},{2,3},{3,2},{4,5},{5,4},{6,7},{7,6},{8,9},{9,8},{10,11... | collective-permute-start | bytes 3145736 | tf_op jit(solution)/shard_map/ppermute | solution.py:70
  292.1 3.7 collective-permute-start.19
  292.7 22.4 %collective-permute-start.20 = (bf16[512,1024]{1,0:T(8,128)(2,1)}, bf16[512,1024]{1,0:T(8,128)(2,1)}, u32[]{:S(2)}, u32[]{:S(2)}) collective-permute-start(bf16[512,1024]{1,0:T(8,128)(2,1)} %convolution_convert_fusion.4), channel_id=1, source_target_pairs={{0,1},{1,0},{2,3},{3,2},{4,5},{5,4},{6,7},{7,6},{8,9},{9,8},{10,11... | collective-permute-start | bytes 3145736 | tf_op jit(solution)/shard_map/ppermute | solution.py:70
  294.2 404.0 %all-gather.7.cloned.1.call-start = ((), (), s32[]{:S(2)}) async-start(), calls=%async_computation.1 | async-start | bytes 7798784 | tf_op jit(solution)/shard_map/all_gather | solution.py:316
  323.3 4.1 collective-permute-start.21
  326.1 14.9 %collective-permute-start.22 = (bf16[512,1024]{1,0:T(8,128)(2,1)S(1)}, bf16[512,1024]{1,0:T(8,128)(2,1)S(1)}, u32[]{:S(2)}, u32[]{:S(2)}) collective-permute-start(bf16[512,1024]{1,0:T(8,128)(2,1)S(1)} %add_convert_fusion.9), channel_id=1, source_target_pairs={{0,1},{1,0},{2,3},{3,2},{4,5},{5,4},{6,7},{7,6},{8,9},{9,8},{10,11... | collective-permute-start | bytes 3145736 | tf_op jit(solution)/shard_map/ppermute | solution.py:70
  337.1 30.0 %collective-permute-start.24 = (bf16[2,2,2,192,512]{4,3,1,0,2:T(8,128)(2,1)S(1)}, bf16[2,2,2,192,512]{4,3,1,0,2:T(8,128)(2,1)S(1)}, u32[]{:S(2)}, u32[]{:S(2)}) collective-permute-start(bf16[2,2,2,192,512]{4,3,1,0,2:T(8,128)(2,1)S(1)} %pad_maximum_fusion.2), channel_id=1, source_target_pairs={{0,2},{2,0},{4,6},{6,4},{8,10},{10,8},{12,14},{14,12},{16,18},{18,... | collective-permute-start | bytes 4718600 | tf_op jit(solution)/shard_map/ppermute | solution.py:247
  341.0 26.7 %collective-permute-start.23 = (bf16[512,1024]{1,0:T(8,128)(2,1)S(1)}, bf16[512,1024]{1,0:T(8,128)(2,1)S(1)}, u32[]{:S(2)}, u32[]{:S(2)}) collective-permute-start(bf16[512,1024]{1,0:T(8,128)(2,1)S(1)} %add_convert_fusion.8), channel_id=1, source_target_pairs={{0,1},{1,0},{2,3},{3,2},{4,5},{5,4},{6,7},{7,6},{8,9},{9,8},{10,11... | collective-permute-start | bytes 3145736 | tf_op jit(solution)/shard_map/ppermute | solution.py:70
  378.9 28.9 %collective-permute-start.25 = (bf16[512,1024]{1,0:T(8,128)(2,1)S(1)}, bf16[512,1024]{1,0:T(8,128)(2,1)S(1)}, u32[]{:S(2)}, u32[]{:S(2)}) collective-permute-start(bf16[512,1024]{1,0:T(8,128)(2,1)S(1)} %add_convert_fusion.7), channel_id=1, source_target_pairs={{0,1},{1,0},{2,3},{3,2},{4,5},{5,4},{6,7},{7,6},{8,9},{9,8},{10,11... | collective-permute-start | bytes 3145736 | tf_op jit(solution)/shard_map/ppermute | solution.py:70
  381.1 26.5 %collective-permute-start.26 = (bf16[2,2,192,512]{3,2,1,0:T(8,128)(2,1)S(1)}, bf16[2,2,192,512]{3,2,1,0:T(8,128)(2,1)S(1)}, u32[]{:S(2)}, u32[]{:S(2)}) collective-permute-start(bf16[2,2,192,512]{3,2,1,0:T(8,128)(2,1)S(1)} %get-tuple-element.241), channel_id=1, source_target_pairs={{0,4},{2,6},{4,0},{6,2},{8,12},{10,14},{12,8},{14,10},{16,20},{18,... | collective-permute-start | bytes 2359304 | tf_op jit(solution)/shard_map/ppermute | solution.py:247
  413.7 37.6 %collective-permute-start.30 = (bf16[2,2,2,256,512]{4,3,1,0,2:T(8,128)(2,1)S(1)}, bf16[2,2,2,256,512]{4,3,1,0,2:T(8,128)(2,1)S(1)}, u32[]{:S(2)}, u32[]{:S(2)}) collective-permute-start(bf16[2,2,2,256,512]{4,3,1,0,2:T(8,128)(2,1)S(1)} %bitcast_dynamic-update-slice_fusion), channel_id=1, source_target_pairs={{0,2},{2,0},{4,6},{6,4},{8,10},{10,8},{12,14},{14,12},{16,18},{18,... | collective-permute-start | bytes 6291464 | tf_op jit(solution)/shard_map/ppermute | solution.py:247
  414.5 20.0 %collective-permute-start.28 = (bf16[2,192,512]{2,1,0:T(8,128)(2,1)S(1)}, bf16[2,192,512]{2,1,0:T(8,128)(2,1)S(1)}, u32[]{:S(2)}, u32[]{:S(2)}) collective-permute-start(bf16[2,192,512]{2,1,0:T(8,128)(2,1)S(1)} %get-tuple-element.246), channel_id=1, source_target_pairs={{0,8},{2,10},{4,12},{6,14},{8,0},{10,2},{12,4},{14,6},{16,24},{18,... | collective-permute-start | bytes 1179656 | tf_op jit(solution)/shard_map/ppermute | solution.py:247
  418.8 33.4 %collective-permute-start.27 = (bf16[512,1024]{1,0:T(8,128)(2,1)S(1)}, bf16[512,1024]{1,0:T(8,128)(2,1)S(1)}, u32[]{:S(2)}, u32[]{:S(2)}) collective-permute-start(bf16[512,1024]{1,0:T(8,128)(2,1)S(1)} %add_convert_fusion.6), channel_id=1, source_target_pairs={{0,1},{1,0},{2,3},{3,2},{4,5},{5,4},{6,7},{7,6},{8,9},{9,8},{10,11... | collective-permute-start | bytes 3145736 | tf_op jit(solution)/shard_map/ppermute | solution.py:70
  434.6 15.9 %collective-permute-start.29 = (bf16[192,512]{1,0:T(8,128)(2,1)S(1)}, bf16[192,512]{1,0:T(8,128)(2,1)S(1)}, u32[]{:S(2)}, u32[]{:S(2)}) collective-permute-start(bf16[192,512]{1,0:T(8,128)(2,1)S(1)} %dynamic-slice_bitcast_fusion.20), channel_id=1, source_target_pairs={{0,16},{2,18},{4,20},{6,22},{8,24},{10,26},{12,28},{14,30},{16,0},... | collective-permute-start | bytes 589832 | tf_op jit(solution)/shard_map/ppermute | solution.py:247
  468.7 34.7 %collective-permute-start.34 = (bf16[2,2,2,128,1024]{4,3,1,0,2:T(8,128)(2,1)S(1)}, bf16[2,2,2,128,1024]{4,3,1,0,2:T(8,128)(2,1)S(1)}, u32[]{:S(2)}, u32[]{:S(2)}) collective-permute-start(bf16[2,2,2,128,1024]{4,3,1,0,2:T(8,128)(2,1)S(1)} %pad_maximum_fusion), channel_id=1, source_target_pairs={{0,2},{2,0},{4,6},{6,4},{8,10},{10,8},{12,14},{14,12},{16,18},{18,... | collective-permute-start | bytes 6291464 | tf_op jit(solution)/shard_map/ppermute | solution.py:247
  476.4 29.2 %collective-permute-start.33 = (bf16[2,2,2,128,1024]{4,3,2,1,0:T(8,128)(2,1)S(1)}, bf16[2,2,2,128,1024]{4,3,2,1,0:T(8,128)(2,1)S(1)}, u32[]{:S(2)}, u32[]{:S(2)}) collective-permute-start(bf16[2,2,2,128,1024]{4,3,2,1,0:T(8,128)(2,1)S(1)} %dynamic-slice_bitcast_fusion), channel_id=1, source_target_pairs={{0,2},{2,0},{4,6},{6,4},{8,10},{10,8},{12,14},{14,12},{16,18},{18,... | collective-permute-start | bytes 6291464 | tf_op jit(solution)/shard_map/ppermute | solution.py:247
  476.5 25.6 %collective-permute-start.32 = (bf16[2,2,256,512]{3,2,1,0:T(8,128)(2,1)S(1)}, bf16[2,2,256,512]{3,2,1,0:T(8,128)(2,1)S(1)}, u32[]{:S(2)}, u32[]{:S(2)}) collective-permute-start(bf16[2,2,256,512]{3,2,1,0:T(8,128)(2,1)S(1)} %get-tuple-element.253), channel_id=1, source_target_pairs={{0,4},{2,6},{4,0},{6,2},{8,12},{10,14},{12,8},{14,10},{16,20},{18,... | collective-permute-start | bytes 3145736 | tf_op jit(solution)/shard_map/ppermute | solution.py:247
  478.2 30.0 %collective-permute-start.31 = (bf16[256,1024]{1,0:T(8,128)(2,1)}, bf16[256,1024]{1,0:T(8,128)(2,1)}, u32[]{:S(2)}, u32[]{:S(2)}) collective-permute-start(bf16[256,1024]{1,0:T(8,128)(2,1)} %dynamic-slice_convert_fusion.1), channel_id=1, source_target_pairs={{0,1},{1,0},{2,3},{3,2},{4,5},{5,4},{6,7},{7,6},{8,9},{9,8},{10,11... | collective-permute-start | bytes 1572872 | tf_op jit(solution)/shard_map/ppermute | solution.py:70
  508.2 13.7 %collective-permute-start.36 = (bf16[2,256,512]{2,1,0:T(8,128)(2,1)}, bf16[2,256,512]{2,1,0:T(8,128)(2,1)S(1)}, u32[]{:S(2)}, u32[]{:S(2)}) collective-permute-start(bf16[2,256,512]{2,1,0:T(8,128)(2,1)} %get-tuple-element.257), channel_id=1, source_target_pairs={{0,8},{2,10},{4,12},{6,14},{8,0},{10,2},{12,4},{14,6},{16,24},{18,... | collective-permute-start | bytes 1572872 | tf_op jit(solution)/shard_map/ppermute | solution.py:247
  508.2 28.6 %collective-permute-start.39 = (bf16[2,2,128,1024]{3,2,1,0:T(8,128)(2,1)}, bf16[2,2,128,1024]{3,2,1,0:T(8,128)(2,1)S(1)}, u32[]{:S(2)}, u32[]{:S(2)}) collective-permute-start(bf16[2,2,128,1024]{3,2,1,0:T(8,128)(2,1)} %get-tuple-element.261), channel_id=1, source_target_pairs={{0,4},{2,6},{4,0},{6,2},{8,12},{10,14},{12,8},{14,10},{16,20},{18,... | collective-permute-start | bytes 3145736 | tf_op jit(solution)/shard_map/ppermute | solution.py:247
  509.8 45.9 %collective-permute-start.38 = (bf16[2,2,128,1024]{3,2,1,0:T(8,128)(2,1)}, bf16[2,2,128,1024]{3,2,1,0:T(8,128)(2,1)S(1)}, u32[]{:S(2)}, u32[]{:S(2)}) collective-permute-start(bf16[2,2,128,1024]{3,2,1,0:T(8,128)(2,1)} %get-tuple-element.259), channel_id=1, source_target_pairs={{0,4},{2,6},{4,0},{6,2},{8,12},{10,14},{12,8},{14,10},{16,20},{18,... | collective-permute-start | bytes 3145736 | tf_op jit(solution)/shard_map/ppermute | solution.py:247
  523.1 13.6 %collective-permute-start.37 = (bf16[256,512]{1,0:T(8,128)(2,1)S(1)}, bf16[256,512]{1,0:T(8,128)(2,1)S(1)}, u32[]{:S(2)}, u32[]{:S(2)}) collective-permute-start(bf16[256,512]{1,0:T(8,128)(2,1)S(1)} %dynamic-slice_bitcast_fusion.19), channel_id=1, source_target_pairs={{0,16},{2,18},{4,20},{6,22},{8,24},{10,26},{12,28},{14,30},{16,0},... | collective-permute-start | bytes 786440 | tf_op jit(solution)/shard_map/ppermute | solution.py:247
  524.5 32.7 %collective-permute-start.35 = (bf16[256,1024]{1,0:T(8,128)(2,1)}, bf16[256,1024]{1,0:T(8,128)(2,1)}, u32[]{:S(2)}, u32[]{:S(2)}) collective-permute-start(bf16[256,1024]{1,0:T(8,128)(2,1)} %dynamic-slice_convert_fusion), channel_id=1, source_target_pairs={{0,1},{1,0},{2,3},{3,2},{4,5},{5,4},{6,7},{7,6},{8,9},{9,8},{10,11... | collective-permute-start | bytes 1572872 | tf_op jit(solution)/shard_map/ppermute | solution.py:70
  558.1 179.1 %all-gather.5.cloned.1.call-start = ((), (), s32[]{:S(2)}) async-start(), calls=%async_computation | async-start | bytes 8912896 | tf_op jit(solution)/shard_map/all_gather | solution.py:316
  565.6 4.2 collective-permute-start.40
  565.7 29.5 %collective-permute-start.43 = (bf16[2,128,1024]{2,1,0:T(8,128)(2,1)}, bf16[2,128,1024]{2,1,0:T(8,128)(2,1)S(1)}, u32[]{:S(2)}, u32[]{:S(2)}) collective-permute-start(bf16[2,128,1024]{2,1,0:T(8,128)(2,1)} %get-tuple-element.274), channel_id=1, source_target_pairs={{0,8},{2,10},{4,12},{6,14},{8,0},{10,2},{12,4},{14,6},{16,24},{18,... | collective-permute-start | bytes 1572872 | tf_op jit(solution)/shard_map/ppermute | solution.py:247
  567.4 53.2 %collective-permute-start.41 = (bf16[2,128,1024]{2,1,0:T(8,128)(2,1)}, bf16[2,128,1024]{2,1,0:T(8,128)(2,1)S(1)}, u32[]{:S(2)}, u32[]{:S(2)}) collective-permute-start(bf16[2,128,1024]{2,1,0:T(8,128)(2,1)} %get-tuple-element.272), channel_id=1, source_target_pairs={{0,8},{2,10},{4,12},{6,14},{8,0},{10,2},{12,4},{14,6},{16,24},{18,... | collective-permute-start | bytes 1572872 | tf_op jit(solution)/shard_map/ppermute | solution.py:247
  595.4 25.8 %collective-permute-start.44 = (bf16[128,1024]{1,0:T(8,128)(2,1)S(1)}, bf16[128,1024]{1,0:T(8,128)(2,1)S(1)}, u32[]{:S(2)}, u32[]{:S(2)}) collective-permute-start(bf16[128,1024]{1,0:T(8,128)(2,1)S(1)} %dynamic-slice_bitcast_fusion.17), channel_id=1, source_target_pairs={{0,16},{2,18},{4,20},{6,22},{8,24},{10,26},{12,28},{14,30},{16,0},... | collective-permute-start | bytes 786440 | tf_op jit(solution)/shard_map/ppermute | solution.py:247
  621.0 26.9 %collective-permute-start.42 = (bf16[128,1024]{1,0:T(8,128)(2,1)S(1)}, bf16[128,1024]{1,0:T(8,128)(2,1)S(1)}, u32[]{:S(2)}, u32[]{:S(2)}) collective-permute-start(bf16[128,1024]{1,0:T(8,128)(2,1)S(1)} %dynamic-slice_bitcast_fusion.18), channel_id=1, source_target_pairs={{0,16},{2,18},{4,20},{6,22},{8,24},{10,26},{12,28},{14,30},{16,0},... | collective-permute-start | bytes 786440 | tf_op jit(solution)/shard_map/ppermute | solution.py:247
  621.3 26.6 %collective-permute-start.45 = (f32[43520]{0:T(1024)S(1)}, f32[43520]{0:T(1024)}, u32[]{:S(2)}, u32[]{:S(2)}) collective-permute-start(f32[43520]{0:T(1024)S(1)} %slice_dynamic-update-slice_fusion.1), channel_id=1, source_target_pairs={{0,2},{2,0},{4,6},{6,4},{8,10},{10,8},{12,14},{14,12},{16,18},{18,... | collective-permute-start | bytes 522248 | tf_op jit(solution)/shard_map/ppermute | solution.py:247
  663.7 9.1 %collective-permute-start.46 = (f32[43520]{0:T(1024)S(1)}, f32[43520]{0:T(1024)S(1)}, u32[]{:S(2)}, u32[]{:S(2)}) collective-permute-start(f32[43520]{0:T(1024)S(1)} %add.902), channel_id=1, source_target_pairs={{0,4},{2,6},{4,0},{6,2},{8,12},{10,14},{12,8},{14,10},{16,20},{18,... | collective-permute-start | bytes 522248 | tf_op jit(solution)/shard_map/ppermute | solution.py:247
  672.7 12.9 %collective-permute-start.47 = (f32[43520]{0:T(1024)S(1)}, f32[43520]{0:T(1024)S(1)}, u32[]{:S(2)}, u32[]{:S(2)}) collective-permute-start(f32[43520]{0:T(1024)S(1)} %add.903), channel_id=1, source_target_pairs={{0,8},{2,10},{4,12},{6,14},{8,0},{10,2},{12,4},{14,6},{16,24},{18,... | collective-permute-start | bytes 522248 | tf_op jit(solution)/shard_map/ppermute | solution.py:247
  685.7 9.2 %collective-permute-start.48 = (f32[43520]{0:T(1024)S(1)}, f32[43520]{0:T(1024)S(1)}, u32[]{:S(2)}, u32[]{:S(2)}) collective-permute-start(f32[43520]{0:T(1024)S(1)} %add.904), channel_id=1, source_target_pairs={{0,16},{2,18},{4,20},{6,22},{8,24},{10,26},{12,28},{14,30},{16,0},... | collective-permute-start | bytes 522248 | tf_op jit(solution)/shard_map/ppermute | solution.py:247
  (192 other events, 1939.0 us)
Sparse Core Ops, SparseCore 0:
  294.4 189.4 all-reduce.4
  558.2 95.6 all-gather.6
  656.9 80.2 all-gather.4

commit v4 on v3

--- a/solution.py
+++ b/solution.py
@@ -1053,6 +1053,7 @@
             "attend",
             [(attend_kept[7], spread)] + [(attend_kept[3], low) for low in lows],
             lows[0].shape[1],
+            eager=True,
         )
         grads.sums("attend_sums", [query_sum, value_sum, output_sum, table_sum])
         grads.gather("middle", ["convolve", "attend"])

time: 765 us -> 763 us (level)
  waiting for transfers between devices: 331 us -> 311 us
  Pallas kernels: 120 us -> 131 us
    ppermute x24, waiting for transfers between devices: 183 us -> 164 us  [dp_swap(): lax.ppermute(values, 'dp', [(place, place ^ bit) for place in range(16)])]
    all_gather x2, waiting for transfers between devices: 27.9 us -> 15.4 us  [gather_job(): whole = lax.all_gather(shards, 'dp', axis=0)]
    pallas_call x2, Pallas kernels: 8.5 us -> 19.6 us  [mix_channels(): pl.pallas_call(mix_kernel, out_shape=(jax.ShapeDtypeStruct((length, width...]
    ppermute x20, waiting for transfers between devices: 112 us -> 123 us  [swap(): return lax.ppermute(values, 'tensor', [(0, 1), (1, 0)])]
  transfers between devices with their start and end apart: 52 -> 52, of which waited for: 34 -> 35; matrix products, arithmetic and copies ran while one was open for 22% -> 21% of each run, Pallas kernels for 16% -> 18%
where the time goes in v4:
time: 763 us; the launch traced here: 749 us
  waiting for transfers between devices  311 us (41%)
  Pallas kernels  131 us (17%)
  other arithmetic  106 us (14%)
  matrix products  84.1 us (11%)
  starting transfers between devices  60 us (8%)
  local copies, waits for them, and re-layouts  39 us (5%)
  between operations  18.3 us (2%)
    ppermute x24, waiting for transfers between devices, dp_swap(): lax.ppermute(values, 'dp', [(place, place ^ bit) for place in range(16)])  164 us
    ppermute x20, waiting for transfers between devices, swap(): return lax.ppermute(values, 'tensor', [(0, 1), (1, 0)])  123 us
    dot_general x22, matrix products, product_right(): lax.dot_general(left, right, (((1,), (1,)), ((), ())), preferred_element_...  47.6 us
    pallas_call x2, Pallas kernels, attend_heads_back(): pl.pallas_call(attend_back_kernel, out_shape=(jax.ShapeDtypeStruct((lengt...  41.5 us
    dot_general x22, matrix products, product(): return jnp.dot(left, right, preferred_element_type=jnp.float32)  36.6 us
    div x13, other arithmetic, per_device(): widen(value) / clips  35.1 us
    pallas_call x11, Pallas kernels, weight_grad(): pl.pallas_call(functools.partial(weight_grad_kernel, len(lefts)), out_sha...  30.4 us
    pallas_call x2, Pallas kernels, attend_heads(): pl.pallas_call(attend_kernel, out_shape=jax.ShapeDtypeStruct((length, wid...  27.6 us
  transfers between devices with their start and end apart: 52, of which 35 were waited for; matrix products, arithmetic and copies ran while one was open for 21% of the time, Pallas kernels for 18%

profile of v4, /device:TPU:0, one launch (start us, length us, event | category | flops | bytes accessed | tf_op | source)
XLA Modules:
  0.0 749.5 jit_solution(14379169985178785352)
XLA Ops:
  16.6 8.5 %collective-permute-done.1 = bf16[256,1024]{1,0:T(8,128)(2,1)S(1)} collective-permute-done((bf16[256,1024]{1,0:T(8,128)(2,1)S(1)}, bf16[256,1024]{1,0:T(8,128)(2,1)S(1)}, u32[]{:S(2)}, u32[]{:S(2)}) %collective-permute-start.1) | collective-permute-done | bytes 524320 | tf_op jit(solution)/shard_map/ppermute | solution.py:70
  29.8 4.8 multiply_convert_fusion.3
  36.9 4.1 collective-permute-done.3
  43.8 4.8 multiply_convert_fusion.2
  53.7 12.2 %collective-permute-done.5 = bf16[512,1024]{1,0:T(8,128)(2,1)S(1)} collective-permute-done((bf16[512,1024]{1,0:T(8,128)(2,1)S(1)}, bf16[512,1024]{1,0:T(8,128)(2,1)S(1)}, u32[]{:S(2)}, u32[]{:S(2)}) %collective-permute-start.5) | collective-permute-done | bytes 1048608 | tf_op jit(solution)/shard_map/ppermute | solution.py:70
  73.0 13.8 %attend_heads.2.refs_0_ = bf16[512,512]{1,0:T(8,128)(2,1)S(1)} custom-call(bf16[512,512]{1,0:T(8,128)(2,1)S(1)} %fusion.25.query_ref, bf16[512,512]{1,0:T(8,128)(2,1)S(1)} %convolution_convert_fusion.11.key_ref, bf16[512,512]{1,0:T(8,128)(2,1)S(1)} %fusion.26.value_ref, bf16[128,128]{1,0:T(8,128)(2,1)S(1)} %copy.76.table_ref), custom_call_target="tpu_custom_call" | custom-call | tf_op jit(solution)/shard_map/attend_heads/pallas_call | solution.py:529
  95.2 13.8 %attend_heads.3.refs_2_ = bf16[512,512]{1,0:T(8,128)(2,1)S(1)} custom-call(bf16[512,512]{1,0:T(8,128)(2,1)S(1)} %fusion.27.query_ref, bf16[512,512]{1,0:T(8,128)(2,1)S(1)} %convolution_convert_fusion.10.key_ref, bf16[512,512]{1,0:T(8,128)(2,1)S(1)} %fusion.28.value_ref, bf16[128,128]{1,0:T(8,128)(2,1)S(1)} %copy.76.table_ref), custom_call_target="tpu_custom_call" | custom-call | tf_op jit(solution)/shard_map/attend_heads/pallas_call | solution.py:529
  109.9 4.0 collective-permute-done.8
  118.3 15.4 %mix_channels.2 = (f32[512,512]{1,0:T(8,128)S(1)}, f32[16,512]{1,0:T(8,128)S(1)}) custom-call(f32[512,512]{1,0:T(8,128)S(1)} %fusion.43.linear_ref, f32[512,512]{1,0:T(8,128)S(1)} %fusion.35.gate_ref, f32[32,512]{1,0:T(8,128)S(1)} %pad_convert_fusion.taps_ref), custom_call_target="tpu_custom_call" | custom-call | tf_op jit(solution)/shard_map/mix_channels/pallas_call | solution.py:623
  145.9 4.2 mix_channels.3
  151.0 10.6 %collective-permute-done.11 = bf16[512,1024]{1,0:T(8,128)(2,1)S(1)} collective-permute-done((bf16[512,1024]{1,0:T(8,128)(2,1)S(1)}, bf16[512,1024]{1,0:T(8,128)(2,1)S(1)}, u32[]{:S(2)}, u32[]{:S(2)}) %collective-permute-start.11) | collective-permute-done | bytes 1048608 | tf_op jit(solution)/shard_map/ppermute | solution.py:70
  173.0 4.8 multiply_convert_fusion.1
  180.2 9.5 %collective-permute-done.13 = bf16[512,1024]{1,0:T(8,128)(2,1)S(1)} collective-permute-done((bf16[512,1024]{1,0:T(8,128)(2,1)S(1)}, bf16[512,1024]{1,0:T(8,128)(2,1)S(1)}, u32[]{:S(2)}, u32[]{:S(2)}) %collective-permute-start.13) | collective-permute-done | bytes 1048608 | tf_op jit(solution)/shard_map/ppermute | solution.py:70
  197.8 10.1 %collective-permute-done.14 = bf16[256,1024]{1,0:T(8,128)(2,1)S(1)} collective-permute-done((bf16[256,1024]{1,0:T(8,128)(2,1)S(1)}, bf16[256,1024]{1,0:T(8,128)(2,1)S(1)}, u32[]{:S(2)}, u32[]{:S(2)}) %collective-permute-start.14) | collective-permute-done | bytes 524320 | tf_op jit(solution)/shard_map/ppermute | solution.py:70
  212.9 8.9 %collective-permute-done.15 = bf16[256,1024]{1,0:T(8,128)(2,1)S(1)} collective-permute-done((bf16[256,1024]{1,0:T(8,128)(2,1)S(1)}, bf16[256,1024]{1,0:T(8,128)(2,1)S(1)}, u32[]{:S(2)}, u32[]{:S(2)}) %collective-permute-start.15) | collective-permute-done | bytes 524320 | tf_op jit(solution)/shard_map/ppermute | solution.py:70
  226.3 7.0 collective-permute-done.16
  233.7 6.6 fusion.88
  245.2 9.9 %collective-permute-done.17 = bf16[256,1024]{1,0:T(8,128)(2,1)S(1)} collective-permute-done((bf16[256,1024]{1,0:T(8,128)(2,1)S(1)}, bf16[256,1024]{1,0:T(8,128)(2,1)S(1)}, u32[]{:S(2)}, u32[]{:S(2)}) %collective-permute-start.17) | collective-permute-done | bytes 524320 | tf_op jit(solution)/shard_map/ppermute | solution.py:70
  256.8 4.9 fusion.87
  261.6 5.4 weight_grad.12
  269.3 5.3 weight_grad.11
  276.6 6.3 convolution_convert_fusion.4
  297.8 6.0 mix_channels_back.2
  305.3 9.9 %collective-permute-done.20 = bf16[512,1024]{1,0:T(8,128)(2,1)} collective-permute-done((bf16[512,1024]{1,0:T(8,128)(2,1)}, bf16[512,1024]{1,0:T(8,128)(2,1)}, u32[]{:S(2)}, u32[]{:S(2)}) %collective-permute-start.20) | collective-permute-done | bytes 1048608 | tf_op jit(solution)/shard_map/ppermute | solution.py:70
  327.9 6.2 mix_channels_back.3
  346.2 20.8 %attend_heads_back.2 = (bf16[512,512]{1,0:T(8,128)(2,1)S(1)}, bf16[512,512]{1,0:T(8,128)(2,1)S(1)}, bf16[512,512]{1,0:T(8,128)(2,1)S(1)}, f32[1,512]{1,0:T(1,128...) custom-call(bf16[512,512]{1,0:T(8,128)(2,1)S(1)} %copy-done.40, bf16[512,512]{1,0:T(8,128)(2,1)S(1)} %copy-done.38, ...), custom_call_target="tpu_custom_call" | custom-call | tf_op jit(solution)/shard_map/attend_heads_back/pallas_call | solution.py:548
  380.1 20.6 %attend_heads_back.3 = (bf16[512,512]{1,0:T(8,128)(2,1)S(1)}, bf16[512,512]{1,0:T(8,128)(2,1)S(1)}, bf16[512,512]{1,0:T(8,128)(2,1)S(1)}, f32[1,512]{1,0:T(1,128...) custom-call(bf16[512,512]{1,0:T(8,128)(2,1)S(1)} %copy-done.36, bf16[512,512]{1,0:T(8,128)(2,1)S(1)} %copy-done.32, ...), custom_call_target="tpu_custom_call" | custom-call | tf_op jit(solution)/shard_map/attend_heads_back/pallas_call | solution.py:548
  404.4 21.5 %collective-permute-done.25 = bf16[512,1024]{1,0:T(8,128)(2,1)S(1)} collective-permute-done((bf16[512,1024]{1,0:T(8,128)(2,1)S(1)}, bf16[512,1024]{1,0:T(8,128)(2,1)S(1)}, u32[]{:S(2)}, u32[]{:S(2)}) %collective-permute-start.25) | collective-permute-done | bytes 1048608 | tf_op jit(solution)/shard_map/ppermute | solution.py:70
  430.4 4.5 collective-permute-done.26
  450.8 9.5 %collective-permute-done.29 = bf16[2,192,512]{2,1,0:T(8,128)(2,1)S(1)} collective-permute-done((bf16[2,192,512]{2,1,0:T(8,128)(2,1)S(1)}, bf16[2,192,512]{2,1,0:T(8,128)(2,1)S(1)}, u32[]{:S(2)}, u32[]{:S(2)}) %collective-permute-start.29) | collective-permute-done | bytes 393248 | tf_op jit(solution)/shard_map/ppermute | solution.py:247
  467.1 6.8 collective-permute-done.30
  484.7 5.3 weight_grad.21
  493.3 5.5 weight_grad.20
  499.1 6.7 collective-permute-done.33
  512.0 8.3 %collective-permute-done.34 = bf16[256,512]{1,0:T(8,128)(2,1)S(1)} collective-permute-done((bf16[256,512]{1,0:T(8,128)(2,1)S(1)}, bf16[256,512]{1,0:T(8,128)(2,1)S(1)}, u32[]{:S(2)}, u32[]{:S(2)}) %collective-permute-start.34) | collective-permute-done | bytes 262176 | tf_op jit(solution)/shard_map/ppermute | solution.py:247
  532.6 27.1 %collective-permute-done.39 = bf16[2,2,128,1024]{3,2,1,0:T(8,128)(2,1)S(1)} collective-permute-done((bf16[2,2,128,1024]{3,2,1,0:T(8,128)(2,1)}, bf16[2,2,128,1024]{3,2,1,0:T(8,128)(2,1)S(1)}, u32[]{:S(2)}, u32[]{:S(2)}) %collective-permute-start.39) | collective-permute-done | bytes 1048608 | tf_op jit(solution)/shard_map/ppermute | solution.py:247
  560.9 38.3 %collective-permute-done.38 = bf16[2,2,128,1024]{3,2,1,0:T(8,128)(2,1)S(1)} collective-permute-done((bf16[2,2,128,1024]{3,2,1,0:T(8,128)(2,1)}, bf16[2,2,128,1024]{3,2,1,0:T(8,128)(2,1)S(1)}, u32[]{:S(2)}, u32[]{:S(2)}) %collective-permute-start.38) | collective-permute-done | bytes 1048608 | tf_op jit(solution)/shard_map/ppermute | solution.py:247
  614.5 9.3 %collective-permute-done.43 = bf16[2,128,1024]{2,1,0:T(8,128)(2,1)S(1)} collective-permute-done((bf16[2,128,1024]{2,1,0:T(8,128)(2,1)}, bf16[2,128,1024]{2,1,0:T(8,128)(2,1)S(1)}, u32[]{:S(2)}, u32[]{:S(2)}) %collective-permute-start.43) | collective-permute-done | bytes 524320 | tf_op jit(solution)/shard_map/ppermute | solution.py:247
  627.6 12.1 %collective-permute-done.41 = bf16[2,128,1024]{2,1,0:T(8,128)(2,1)S(1)} collective-permute-done((bf16[2,128,1024]{2,1,0:T(8,128)(2,1)}, bf16[2,128,1024]{2,1,0:T(8,128)(2,1)S(1)}, u32[]{:S(2)}, u32[]{:S(2)}) %collective-permute-start.41) | collective-permute-done | bytes 524320 | tf_op jit(solution)/shard_map/ppermute | solution.py:247
  640.2 13.3 %collective-permute-done.42 = bf16[128,1024]{1,0:T(8,128)(2,1)S(1)} collective-permute-done((bf16[128,1024]{1,0:T(8,128)(2,1)S(1)}, bf16[128,1024]{1,0:T(8,128)(2,1)S(1)}, u32[]{:S(2)}, u32[]{:S(2)}) %collective-permute-start.42) | collective-permute-done | bytes 262176 | tf_op jit(solution)/shard_map/ppermute | solution.py:247
  655.6 7.0 convert_divide_fusion
  662.7 5.5 convert_divide_fusion.1
  669.7 5.9 collective-permute-done.46
  675.7 8.5 %collective-permute-done.47 = f32[43520]{0:T(1024)S(1)} collective-permute-done((f32[43520]{0:T(1024)S(1)}, f32[43520]{0:T(1024)S(1)}, u32[]{:S(2)}, u32[]{:S(2)}) %collective-permute-start.47) | collective-permute-done | bytes 174112 | tf_op jit(solution)/shard_map/ppermute | solution.py:247
  689.1 12.3 %collective-permute-done.48 = f32[43520]{0:T(1024)S(1)} collective-permute-done((f32[43520]{0:T(1024)S(1)}, f32[43520]{0:T(1024)S(1)}, u32[]{:S(2)}, u32[]{:S(2)}) %collective-permute-start.48) | collective-permute-done | bytes 174112 | tf_op jit(solution)/shard_map/ppermute | solution.py:247
  715.8 15.4 %all-gather.5.cloned.1.call-done = bf16[4096,1024]{1,0:T(8,128)(2,1)} async-done(((bf16[256,1024]{1,0:T(8,128)(2,1)}), bf16[4096,1024]{1,0:T(8,128)(2,1)}) %all-gather.5.cloned.1.call-update) | async-done | bytes 8388624 | tf_op jit(solution)/shard_map/all_gather | solution.py:316
  731.2 7.0 convert_divide_fusion.2
  738.8 4.0 convert_divide_fusion.3
  (775 shorter events, 259.3 us)
Async XLA Ops:
  7.4 518.8 %all-reduce.5.cloned.1.call-start = ((), (), s32[]{:S(2)}) async-start(), calls=%async_computation.2 | async-start | bytes 16777216 | tf_op jit(solution)/shard_map/psum | solution.py:303
  9.9 15.2 %collective-permute-start.1 = (bf16[256,1024]{1,0:T(8,128)(2,1)S(1)}, bf16[256,1024]{1,0:T(8,128)(2,1)S(1)}, u32[]{:S(2)}, u32[]{:S(2)}) collective-permute-start(bf16[256,1024]{1,0:T(8,128)(2,1)S(1)} %get-tuple-element.160), channel_id=1, source_target_pairs={{0,1},{1,0},{2,3},{3,2},{4,5},{5,4},{6,7},{7,6},{8,9},{9,8},{10,11... | collective-permute-start | bytes 1572872 | tf_op jit(solution)/shard_map/ppermute | solution.py:70
  25.9 11.0 %collective-permute-start.4 = (f32[128]{0:T(128)S(1)}, f32[128]{0:T(128)S(1)}, u32[]{:S(2)}, u32[]{:S(2)}) collective-permute-start(f32[128]{0:T(128)S(1)} %fusion.180), channel_id=1, source_target_pairs={{0,8},{2,10},{4,12},{6,14},{8,0},{10,2},{12,4},{14,6},{16,24},{18,... | collective-permute-start | bytes 1544 | tf_op jit(solution)/shard_map/ppermute | solution.py:247
  27.8 13.3 %collective-permute-start.3 = (bf16[256,1024]{1,0:T(8,128)(2,1)S(1)}, bf16[256,1024]{1,0:T(8,128)(2,1)S(1)}, u32[]{:S(2)}, u32[]{:S(2)}) collective-permute-start(bf16[256,1024]{1,0:T(8,128)(2,1)S(1)} %get-tuple-element.164), channel_id=1, source_target_pairs={{0,1},{1,0},{2,3},{3,2},{4,5},{5,4},{6,7},{7,6},{8,9},{9,8},{10,11... | collective-permute-start | bytes 1572872 | tf_op jit(solution)/shard_map/ppermute | solution.py:70
  42.3 23.6 %collective-permute-start.5 = (bf16[512,1024]{1,0:T(8,128)(2,1)S(1)}, bf16[512,1024]{1,0:T(8,128)(2,1)S(1)}, u32[]{:S(2)}, u32[]{:S(2)}) collective-permute-start(bf16[512,1024]{1,0:T(8,128)(2,1)S(1)} %convolution_convert_fusion.7), channel_id=1, source_target_pairs={{0,1},{1,0},{2,3},{3,2},{4,5},{5,4},{6,7},{7,6},{8,9},{9,8},{10,11... | collective-permute-start | bytes 3145736 | tf_op jit(solution)/shard_map/ppermute | solution.py:70
  48.7 5.0 collective-permute-start.6
  67.0 22.7 %collective-permute-start.7 = (bf16[512,1024]{1,0:T(8,128)(2,1)S(1)}, bf16[512,1024]{1,0:T(8,128)(2,1)S(1)}, u32[]{:S(2)}, u32[]{:S(2)}) collective-permute-start(bf16[512,1024]{1,0:T(8,128)(2,1)S(1)} %convolution_convert_fusion.6), channel_id=1, source_target_pairs={{0,1},{1,0},{2,3},{3,2},{4,5},{5,4},{6,7},{7,6},{8,9},{9,8},{10,11... | collective-permute-start | bytes 3145736 | tf_op jit(solution)/shard_map/ppermute | solution.py:70
  91.5 22.4 %collective-permute-start.8 = (bf16[512,1024]{1,0:T(8,128)(2,1)S(1)}, bf16[512,1024]{1,0:T(8,128)(2,1)S(1)}, u32[]{:S(2)}, u32[]{:S(2)}) collective-permute-start(bf16[512,1024]{1,0:T(8,128)(2,1)S(1)} %convolution_convert_fusion.3), channel_id=1, source_target_pairs={{0,1},{1,0},{2,3},{3,2},{4,5},{5,4},{6,7},{7,6},{8,9},{9,8},{10,11... | collective-permute-start | bytes 3145736 | tf_op jit(solution)/shard_map/ppermute | solution.py:70
  114.8 21.0 %collective-permute-start.9 = (bf16[512,1024]{1,0:T(8,128)(2,1)S(1)}, bf16[512,1024]{1,0:T(8,128)(2,1)S(1)}, u32[]{:S(2)}, u32[]{:S(2)}) collective-permute-start(bf16[512,1024]{1,0:T(8,128)(2,1)S(1)} %convolution_convert_fusion.2), channel_id=1, source_target_pairs={{0,1},{1,0},{2,3},{3,2},{4,5},{5,4},{6,7},{7,6},{8,9},{9,8},{10,11... | collective-permute-start | bytes 3145736 | tf_op jit(solution)/shard_map/ppermute | solution.py:70
  142.4 19.2 %collective-permute-start.11 = (bf16[512,1024]{1,0:T(8,128)(2,1)S(1)}, bf16[512,1024]{1,0:T(8,128)(2,1)S(1)}, u32[]{:S(2)}, u32[]{:S(2)}) collective-permute-start(bf16[512,1024]{1,0:T(8,128)(2,1)S(1)} %convolution_convert_fusion.1), channel_id=1, source_target_pairs={{0,1},{1,0},{2,3},{3,2},{4,5},{5,4},{6,7},{7,6},{8,9},{9,8},{10,11... | collective-permute-start | bytes 3145736 | tf_op jit(solution)/shard_map/ppermute | solution.py:70
  170.4 19.3 %collective-permute-start.13 = (bf16[512,1024]{1,0:T(8,128)(2,1)S(1)}, bf16[512,1024]{1,0:T(8,128)(2,1)S(1)}, u32[]{:S(2)}, u32[]{:S(2)}) collective-permute-start(bf16[512,1024]{1,0:T(8,128)(2,1)S(1)} %convolution_convert_fusion), channel_id=1, source_target_pairs={{0,1},{1,0},{2,3},{3,2},{4,5},{5,4},{6,7},{7,6},{8,9},{9,8},{10,11... | collective-permute-start | bytes 3145736 | tf_op jit(solution)/shard_map/ppermute | solution.py:70
  193.7 14.1 %collective-permute-start.14 = (bf16[256,1024]{1,0:T(8,128)(2,1)S(1)}, bf16[256,1024]{1,0:T(8,128)(2,1)S(1)}, u32[]{:S(2)}, u32[]{:S(2)}) collective-permute-start(bf16[256,1024]{1,0:T(8,128)(2,1)S(1)} %dynamic-slice_convert_fusion.3), channel_id=1, source_target_pairs={{0,1},{1,0},{2,3},{3,2},{4,5},{5,4},{6,7},{7,6},{8,9},{9,8},{10,11... | collective-permute-start | bytes 1572872 | tf_op jit(solution)/shard_map/ppermute | solution.py:70
  208.5 13.3 %collective-permute-start.15 = (bf16[256,1024]{1,0:T(8,128)(2,1)S(1)}, bf16[256,1024]{1,0:T(8,128)(2,1)S(1)}, u32[]{:S(2)}, u32[]{:S(2)}) collective-permute-start(bf16[256,1024]{1,0:T(8,128)(2,1)S(1)} %dynamic-slice_convert_fusion.2), channel_id=1, source_target_pairs={{0,1},{1,0},{2,3},{3,2},{4,5},{5,4},{6,7},{7,6},{8,9},{9,8},{10,11... | collective-permute-start | bytes 1572872 | tf_op jit(solution)/shard_map/ppermute | solution.py:70
  222.4 11.0 %collective-permute-start.16 = (bf16[256,1024]{1,0:T(8,128)(2,1)S(1)}, bf16[256,1024]{1,0:T(8,128)(2,1)S(1)}, u32[]{:S(2)}, u32[]{:S(2)}) collective-permute-start(bf16[256,1024]{1,0:T(8,128)(2,1)S(1)} %multiply_convert_fusion.8), channel_id=1, source_target_pairs={{0,1},{1,0},{2,3},{3,2},{4,5},{5,4},{6,7},{7,6},{8,9},{9,8},{10,11... | collective-permute-start | bytes 1572872 | tf_op jit(solution)/shard_map/ppermute | solution.py:70
  240.3 14.9 %collective-permute-start.17 = (bf16[256,1024]{1,0:T(8,128)(2,1)S(1)}, bf16[256,1024]{1,0:T(8,128)(2,1)S(1)}, u32[]{:S(2)}, u32[]{:S(2)}) collective-permute-start(bf16[256,1024]{1,0:T(8,128)(2,1)S(1)} %get-tuple-element.205), channel_id=1, source_target_pairs={{0,1},{1,0},{2,3},{3,2},{4,5},{5,4},{6,7},{7,6},{8,9},{9,8},{10,11... | collective-permute-start | bytes 1572872 | tf_op jit(solution)/shard_map/ppermute | solution.py:70
  255.2 27.7 %collective-permute-start.18 = (bf16[512,1024]{1,0:T(8,128)(2,1)}, bf16[512,1024]{1,0:T(8,128)(2,1)}, u32[]{:S(2)}, u32[]{:S(2)}) collective-permute-start(bf16[512,1024]{1,0:T(8,128)(2,1)} %convolution_convert_fusion.5), channel_id=1, source_target_pairs={{0,1},{1,0},{2,3},{3,2},{4,5},{5,4},{6,7},{7,6},{8,9},{9,8},{10,11... | collective-permute-start | bytes 3145736 | tf_op jit(solution)/shard_map/ppermute | solution.py:70
  292.1 3.7 collective-permute-start.19
  292.7 22.5 %collective-permute-start.20 = (bf16[512,1024]{1,0:T(8,128)(2,1)}, bf16[512,1024]{1,0:T(8,128)(2,1)}, u32[]{:S(2)}, u32[]{:S(2)}) collective-permute-start(bf16[512,1024]{1,0:T(8,128)(2,1)} %convolution_convert_fusion.4), channel_id=1, source_target_pairs={{0,1},{1,0},{2,3},{3,2},{4,5},{5,4},{6,7},{7,6},{8,9},{9,8},{10,11... | collective-permute-start | bytes 3145736 | tf_op jit(solution)/shard_map/ppermute | solution.py:70
  294.3 410.4 %all-gather.7.cloned.1.call-start = ((), (), s32[]{:S(2)}) async-start(), calls=%async_computation.1 | async-start | bytes 7798784 | tf_op jit(solution)/shard_map/all_gather | solution.py:316
  323.4 4.1 collective-permute-start.21
  326.2 14.9 %collective-permute-start.22 = (bf16[512,1024]{1,0:T(8,128)(2,1)S(1)}, bf16[512,1024]{1,0:T(8,128)(2,1)S(1)}, u32[]{:S(2)}, u32[]{:S(2)}) collective-permute-start(bf16[512,1024]{1,0:T(8,128)(2,1)S(1)} %add_convert_fusion.9), channel_id=1, source_target_pairs={{0,1},{1,0},{2,3},{3,2},{4,5},{5,4},{6,7},{7,6},{8,9},{9,8},{10,11... | collective-permute-start | bytes 3145736 | tf_op jit(solution)/shard_map/ppermute | solution.py:70
  337.1 30.0 %collective-permute-start.24 = (bf16[2,2,2,192,512]{4,3,1,0,2:T(8,128)(2,1)S(1)}, bf16[2,2,2,192,512]{4,3,1,0,2:T(8,128)(2,1)S(1)}, u32[]{:S(2)}, u32[]{:S(2)}) collective-permute-start(bf16[2,2,2,192,512]{4,3,1,0,2:T(8,128)(2,1)S(1)} %pad_maximum_fusion.2), channel_id=1, source_target_pairs={{0,2},{2,0},{4,6},{6,4},{8,10},{10,8},{12,14},{14,12},{16,18},{18,... | collective-permute-start | bytes 4718600 | tf_op jit(solution)/shard_map/ppermute | solution.py:247
  341.0 26.7 %collective-permute-start.23 = (bf16[512,1024]{1,0:T(8,128)(2,1)S(1)}, bf16[512,1024]{1,0:T(8,128)(2,1)S(1)}, u32[]{:S(2)}, u32[]{:S(2)}) collective-permute-start(bf16[512,1024]{1,0:T(8,128)(2,1)S(1)} %add_convert_fusion.8), channel_id=1, source_target_pairs={{0,1},{1,0},{2,3},{3,2},{4,5},{5,4},{6,7},{7,6},{8,9},{9,8},{10,11... | collective-permute-start | bytes 3145736 | tf_op jit(solution)/shard_map/ppermute | solution.py:70
  400.8 25.2 %collective-permute-start.25 = (bf16[512,1024]{1,0:T(8,128)(2,1)S(1)}, bf16[512,1024]{1,0:T(8,128)(2,1)S(1)}, u32[]{:S(2)}, u32[]{:S(2)}) collective-permute-start(bf16[512,1024]{1,0:T(8,128)(2,1)S(1)} %add_convert_fusion.7), channel_id=1, source_target_pairs={{0,1},{1,0},{2,3},{3,2},{4,5},{5,4},{6,7},{7,6},{8,9},{9,8},{10,11... | collective-permute-start | bytes 3145736 | tf_op jit(solution)/shard_map/ppermute | solution.py:70
  402.9 31.9 %collective-permute-start.26 = (bf16[2,2,192,512]{3,2,1,0:T(8,128)(2,1)S(1)}, bf16[2,2,192,512]{3,2,1,0:T(8,128)(2,1)S(1)}, u32[]{:S(2)}, u32[]{:S(2)}) collective-permute-start(bf16[2,2,192,512]{3,2,1,0:T(8,128)(2,1)S(1)} %get-tuple-element.241), channel_id=1, source_target_pairs={{0,4},{2,6},{4,0},{6,2},{8,12},{10,14},{12,8},{14,10},{16,20},{18,... | collective-permute-start | bytes 2359304 | tf_op jit(solution)/shard_map/ppermute | solution.py:247
  430.3 7.2 collective-permute-start.27
  438.5 36.1 %collective-permute-start.31 = (bf16[2,2,256,512]{3,2,1,0:T(8,128)(2,1)S(1)}, bf16[2,2,256,512]{3,2,1,0:T(8,128)(2,1)S(1)}, u32[]{:S(2)}, u32[]{:S(2)}) collective-permute-start(bf16[2,2,256,512]{3,2,1,0:T(8,128)(2,1)S(1)} %get-tuple-element.248), channel_id=1, source_target_pairs={{0,4},{2,6},{4,0},{6,2},{8,12},{10,14},{12,8},{14,10},{16,20},{18,... | collective-permute-start | bytes 3145736 | tf_op jit(solution)/shard_map/ppermute | solution.py:247
  441.0 19.4 %collective-permute-start.29 = (bf16[2,192,512]{2,1,0:T(8,128)(2,1)S(1)}, bf16[2,192,512]{2,1,0:T(8,128)(2,1)S(1)}, u32[]{:S(2)}, u32[]{:S(2)}) collective-permute-start(bf16[2,192,512]{2,1,0:T(8,128)(2,1)S(1)} %get-tuple-element.246), channel_id=1, source_target_pairs={{0,8},{2,10},{4,12},{6,14},{8,0},{10,2},{12,4},{14,6},{16,24},{18,... | collective-permute-start | bytes 1179656 | tf_op jit(solution)/shard_map/ppermute | solution.py:247
  444.4 30.6 %collective-permute-start.28 = (bf16[512,1024]{1,0:T(8,128)(2,1)S(1)}, bf16[512,1024]{1,0:T(8,128)(2,1)S(1)}, u32[]{:S(2)}, u32[]{:S(2)}) collective-permute-start(bf16[512,1024]{1,0:T(8,128)(2,1)S(1)} %add_convert_fusion.6), channel_id=1, source_target_pairs={{0,1},{1,0},{2,3},{3,2},{4,5},{5,4},{6,7},{7,6},{8,9},{9,8},{10,11... | collective-permute-start | bytes 3145736 | tf_op jit(solution)/shard_map/ppermute | solution.py:70
  460.4 13.4 %collective-permute-start.30 = (bf16[192,512]{1,0:T(8,128)(2,1)S(1)}, bf16[192,512]{1,0:T(8,128)(2,1)S(1)}, u32[]{:S(2)}, u32[]{:S(2)}) collective-permute-start(bf16[192,512]{1,0:T(8,128)(2,1)S(1)} %dynamic-slice_bitcast_fusion.20), channel_id=1, source_target_pairs={{0,16},{2,18},{4,20},{6,22},{8,24},{10,26},{12,28},{14,30},{16,0},... | collective-permute-start | bytes 589832 | tf_op jit(solution)/shard_map/ppermute | solution.py:247
  491.4 29.7 %collective-permute-start.36 = (bf16[2,2,2,128,1024]{4,3,1,0,2:T(8,128)(2,1)S(1)}, bf16[2,2,2,128,1024]{4,3,1,0,2:T(8,128)(2,1)S(1)}, u32[]{:S(2)}, u32[]{:S(2)}) collective-permute-start(bf16[2,2,2,128,1024]{4,3,1,0,2:T(8,128)(2,1)S(1)} %pad_maximum_fusion), channel_id=1, source_target_pairs={{0,2},{2,0},{4,6},{6,4},{8,10},{10,8},{12,14},{14,12},{16,18},{18,... | collective-permute-start | bytes 6291464 | tf_op jit(solution)/shard_map/ppermute | solution.py:247
  491.4 14.3 %collective-permute-start.33 = (bf16[2,256,512]{2,1,0:T(8,128)(2,1)S(1)}, bf16[2,256,512]{2,1,0:T(8,128)(2,1)S(1)}, u32[]{:S(2)}, u32[]{:S(2)}) collective-permute-start(bf16[2,256,512]{2,1,0:T(8,128)(2,1)S(1)} %get-tuple-element.255), channel_id=1, source_target_pairs={{0,8},{2,10},{4,12},{6,14},{8,0},{10,2},{12,4},{14,6},{16,24},{18,... | collective-permute-start | bytes 1572872 | tf_op jit(solution)/shard_map/ppermute | solution.py:247
  499.0 24.6 %collective-permute-start.35 = (bf16[2,2,2,128,1024]{4,3,2,1,0:T(8,128)(2,1)S(1)}, bf16[2,2,2,128,1024]{4,3,2,1,0:T(8,128)(2,1)S(1)}, u32[]{:S(2)}, u32[]{:S(2)}) collective-permute-start(bf16[2,2,2,128,1024]{4,3,2,1,0:T(8,128)(2,1)S(1)} %dynamic-slice_bitcast_fusion), channel_id=1, source_target_pairs={{0,2},{2,0},{4,6},{6,4},{8,10},{10,8},{12,14},{14,12},{16,18},{18,... | collective-permute-start | bytes 6291464 | tf_op jit(solution)/shard_map/ppermute | solution.py:247
  506.0 14.3 %collective-permute-start.34 = (bf16[256,512]{1,0:T(8,128)(2,1)S(1)}, bf16[256,512]{1,0:T(8,128)(2,1)S(1)}, u32[]{:S(2)}, u32[]{:S(2)}) collective-permute-start(bf16[256,512]{1,0:T(8,128)(2,1)S(1)} %dynamic-slice_bitcast_fusion.19), channel_id=1, source_target_pairs={{0,16},{2,18},{4,20},{6,22},{8,24},{10,26},{12,28},{14,30},{16,0},... | collective-permute-start | bytes 786440 | tf_op jit(solution)/shard_map/ppermute | solution.py:247
  509.9 16.3 %collective-permute-start.32 = (bf16[256,1024]{1,0:T(8,128)(2,1)}, bf16[256,1024]{1,0:T(8,128)(2,1)}, u32[]{:S(2)}, u32[]{:S(2)}) collective-permute-start(bf16[256,1024]{1,0:T(8,128)(2,1)} %dynamic-slice_convert_fusion.1), channel_id=1, source_target_pairs={{0,1},{1,0},{2,3},{3,2},{4,5},{5,4},{6,7},{7,6},{8,9},{9,8},{10,11... | collective-permute-start | bytes 1572872 | tf_op jit(solution)/shard_map/ppermute | solution.py:70
  528.2 203.0 %all-gather.5.cloned.1.call-start = ((), (), s32[]{:S(2)}) async-start(), calls=%async_computation | async-start | bytes 8912896 | tf_op jit(solution)/shard_map/all_gather | solution.py:316
  528.4 31.2 %collective-permute-start.39 = (bf16[2,2,128,1024]{3,2,1,0:T(8,128)(2,1)}, bf16[2,2,128,1024]{3,2,1,0:T(8,128)(2,1)S(1)}, u32[]{:S(2)}, u32[]{:S(2)}) collective-permute-start(bf16[2,2,128,1024]{3,2,1,0:T(8,128)(2,1)} %get-tuple-element.261), channel_id=1, source_target_pairs={{0,4},{2,6},{4,0},{6,2},{8,12},{10,14},{12,8},{14,10},{16,20},{18,... | collective-permute-start | bytes 3145736 | tf_op jit(solution)/shard_map/ppermute | solution.py:247
  529.8 69.4 %collective-permute-start.38 = (bf16[2,2,128,1024]{3,2,1,0:T(8,128)(2,1)}, bf16[2,2,128,1024]{3,2,1,0:T(8,128)(2,1)S(1)}, u32[]{:S(2)}, u32[]{:S(2)}) collective-permute-start(bf16[2,2,128,1024]{3,2,1,0:T(8,128)(2,1)} %get-tuple-element.259), channel_id=1, source_target_pairs={{0,4},{2,6},{4,0},{6,2},{8,12},{10,14},{12,8},{14,10},{16,20},{18,... | collective-permute-start | bytes 3145736 | tf_op jit(solution)/shard_map/ppermute | solution.py:247
  531.7 68.8 %collective-permute-start.37 = (bf16[256,1024]{1,0:T(8,128)(2,1)S(1)}, bf16[256,1024]{1,0:T(8,128)(2,1)S(1)}, u32[]{:S(2)}, u32[]{:S(2)}) collective-permute-start(bf16[256,1024]{1,0:T(8,128)(2,1)S(1)} %copy-done.116), channel_id=1, source_target_pairs={{0,1},{1,0},{2,3},{3,2},{4,5},{5,4},{6,7},{7,6},{8,9},{9,8},{10,11... | collective-permute-start | bytes 1572872 | tf_op jit(solution)/shard_map/ppermute | solution.py:70
  603.2 4.2 collective-permute-start.40
  603.3 20.5 %collective-permute-start.43 = (bf16[2,128,1024]{2,1,0:T(8,128)(2,1)}, bf16[2,128,1024]{2,1,0:T(8,128)(2,1)S(1)}, u32[]{:S(2)}, u32[]{:S(2)}) collective-permute-start(bf16[2,128,1024]{2,1,0:T(8,128)(2,1)} %get-tuple-element.274), channel_id=1, source_target_pairs={{0,8},{2,10},{4,12},{6,14},{8,0},{10,2},{12,4},{14,6},{16,24},{18,... | collective-permute-start | bytes 1572872 | tf_op jit(solution)/shard_map/ppermute | solution.py:247
  603.4 36.3 %collective-permute-start.41 = (bf16[2,128,1024]{2,1,0:T(8,128)(2,1)}, bf16[2,128,1024]{2,1,0:T(8,128)(2,1)S(1)}, u32[]{:S(2)}, u32[]{:S(2)}) collective-permute-start(bf16[2,128,1024]{2,1,0:T(8,128)(2,1)} %get-tuple-element.272), channel_id=1, source_target_pairs={{0,8},{2,10},{4,12},{6,14},{8,0},{10,2},{12,4},{14,6},{16,24},{18,... | collective-permute-start | bytes 1572872 | tf_op jit(solution)/shard_map/ppermute | solution.py:247
  624.1 16.0 %collective-permute-start.44 = (bf16[128,1024]{1,0:T(8,128)(2,1)S(1)}, bf16[128,1024]{1,0:T(8,128)(2,1)S(1)}, u32[]{:S(2)}, u32[]{:S(2)}) collective-permute-start(bf16[128,1024]{1,0:T(8,128)(2,1)S(1)} %dynamic-slice_bitcast_fusion.17), channel_id=1, source_target_pairs={{0,16},{2,18},{4,20},{6,22},{8,24},{10,26},{12,28},{14,30},{16,0},... | collective-permute-start | bytes 786440 | tf_op jit(solution)/shard_map/ppermute | solution.py:247
  640.0 13.6 %collective-permute-start.42 = (bf16[128,1024]{1,0:T(8,128)(2,1)S(1)}, bf16[128,1024]{1,0:T(8,128)(2,1)S(1)}, u32[]{:S(2)}, u32[]{:S(2)}) collective-permute-start(bf16[128,1024]{1,0:T(8,128)(2,1)S(1)} %dynamic-slice_bitcast_fusion.18), channel_id=1, source_target_pairs={{0,16},{2,18},{4,20},{6,22},{8,24},{10,26},{12,28},{14,30},{16,0},... | collective-permute-start | bytes 786440 | tf_op jit(solution)/shard_map/ppermute | solution.py:247
  640.1 13.6 %collective-permute-start.45 = (f32[43520]{0:T(1024)S(1)}, f32[43520]{0:T(1024)}, u32[]{:S(2)}, u32[]{:S(2)}) collective-permute-start(f32[43520]{0:T(1024)S(1)} %slice_dynamic-update-slice_fusion.1), channel_id=1, source_target_pairs={{0,2},{2,0},{4,6},{6,4},{8,10},{10,8},{12,14},{14,12},{16,18},{18,... | collective-permute-start | bytes 522248 | tf_op jit(solution)/shard_map/ppermute | solution.py:247
  669.1 6.4 collective-permute-start.46
  675.6 8.6 %collective-permute-start.47 = (f32[43520]{0:T(1024)S(1)}, f32[43520]{0:T(1024)S(1)}, u32[]{:S(2)}, u32[]{:S(2)}) collective-permute-start(f32[43520]{0:T(1024)S(1)} %add.903), channel_id=1, source_target_pairs={{0,8},{2,10},{4,12},{6,14},{8,0},{10,2},{12,4},{14,6},{16,24},{18,... | collective-permute-start | bytes 522248 | tf_op jit(solution)/shard_map/ppermute | solution.py:247
  684.2 17.1 %collective-permute-start.48 = (f32[43520]{0:T(1024)S(1)}, f32[43520]{0:T(1024)S(1)}, u32[]{:S(2)}, u32[]{:S(2)}) collective-permute-start(f32[43520]{0:T(1024)S(1)} %add.904), channel_id=1, source_target_pairs={{0,16},{2,18},{4,20},{6,22},{8,24},{10,26},{12,28},{14,30},{16,0},... | collective-permute-start | bytes 522248 | tf_op jit(solution)/shard_map/ppermute | solution.py:247
  (192 other events, 2398.4 us)
Sparse Core Ops, SparseCore 0:
  294.4 186.9 all-reduce.4
  528.3 92.3 all-gather.6
  654.6 76.5 all-gather.4
